TPU v7x, 256 devices: a whole 4x4x8 slice. The times are simulated.
256 devices in a mesh: dp: 32 (over x, z), expert: 8 (over y, core).
Axes of the slice: x: 4, y: 4, z: 8, core: 2. Of those that a mesh axis runs over, the one named last changes fastest.
Arguments:
- text_embed: bfloat16 [16384, 2048], P(('dp', 'expert')), may hold values from -6 to 6
- image_feats: bfloat16 [8192, 4608], P(('dp', 'expert')), may hold values from -6 to 6
- tile_pos: int32 [8192], P(('dp', 'expert')), may hold values from 0 to 16383, as said below
- proj_in: bfloat16 [4608, 2048], P(None, 'expert'), may hold values from -0.09375 to 0.09375
- proj_out: bfloat16 [2048, 2048], P('expert'), may hold values from -0.125 to 0.125
- norm_gain: float32 [2048], replicated, may hold values from 0.1 to 1.9
- shared_gate: bfloat16 [2048, 2816], P(None, 'expert'), may hold values from -0.125 to 0.125
- shared_up: bfloat16 [2048, 2816], P(None, 'expert'), may hold values from -0.125 to 0.125
- shared_down: bfloat16 [2816, 2048], P('expert'), may hold values from -0.109375 to 0.109375
- expert_gate: bfloat16 [32, 2048, 1408], P('dp', None, 'expert'), may hold values from -0.125 to 0.125
- expert_up: bfloat16 [32, 2048, 1408], P('dp', None, 'expert'), may hold values from -0.125 to 0.125
- expert_down: bfloat16 [32, 1408, 2048], P('dp', 'expert'), may hold values from -0.15625 to 0.15625
- route_ids: int32 [16384, 2], P(('dp', 'expert')), may hold values from 0 to 31, all different within a row; in each aligned block of 512 rows (0 to 511, 512 to 1023, ...) at most 48 rows name the same one
- route_wts: int32 [16384, 2], P(('dp', 'expert')), may hold values from 1 to 65535
Outputs:
- block_out: bfloat16 [16384, 2048], P(('dp', 'expert'))
Inputs may be any that keep to these rules, and one draw needn't show every extreme that they name: `tile_pos`: positions are distinct. The 32 image tokens of one device go 1 to each index of dp, always to rows held by the devices with the sender's own index of expert. `route_ids`: in each aligned block of 512 rows no expert is named by more than 48 rows, a bound that some block reaches.
All inputs are finite; a program needn't handle non-finite values.
Results may differ from a plain program's by a relative error of at most 0.018.
Values may be sent and summed in bfloat16 or wider, within the bound.
A program may use at most 128 MiB of HBM per device.

v0:
```python
import jax
import jax.numpy as jnp
from jax import lax
from jax.sharding import PartitionSpec as P


def normalize(rows, norm_gain):
    rows_f = rows.astype(jnp.float32)
    meansq = jnp.mean(rows_f * rows_f, axis=-1, keepdims=True) + 1e-06
    return (rows_f * lax.rsqrt(meansq) * norm_gain).astype(jnp.bfloat16)


def project_part(feats, proj_in, proj_out):
    vis_hidden = jax.nn.gelu(
        jnp.dot(feats, proj_in, preferred_element_type=jnp.float32), approximate=True
    ).astype(jnp.bfloat16)
    return jnp.dot(vis_hidden, proj_out, preferred_element_type=jnp.float32)


def shards(
    text_embed,
    image_feats,
    tile_pos,
    proj_in,
    proj_out,
    norm_gain,
    shared_gate,
    shared_up,
    shared_down,
    expert_gate,
    expert_up,
    expert_down,
    route_ids,
    route_wts,
):
    tok_dev = text_embed.shape[0]
    img_dev = image_feats.shape[0]
    width_model = text_embed.shape[1]
    n_data = lax.axis_size("dp")
    n_group = lax.axis_size("expert")
    peer = img_dev // n_data
    my_place = lax.axis_index("expert")
    owner = tile_pos // tok_dev
    dest_index = owner // n_group
    order = jnp.argsort(dest_index, stable=True)
    sorted_feats = image_feats[order].reshape(n_data, peer, image_feats.shape[1])
    sorted_offs = (tile_pos[order] % tok_dev).reshape(n_data, peer)
    moved_feats, moved_offs = (
        lax.all_to_all(sorted_feats, "dp", split_axis=0, concat_axis=0, tiled=True),
        lax.all_to_all(sorted_offs, "dp", split_axis=0, concat_axis=0, tiled=True),
    )
    moved_feats = moved_feats.reshape(img_dev, image_feats.shape[1])
    moved_offs = moved_offs.reshape(img_dev)
    texts, feats, offsets, ids, weights = (
        lax.all_gather(text_embed, "expert", axis=0, tiled=True),
        lax.all_gather(moved_feats, "expert", axis=0, tiled=True),
        lax.all_gather(moved_offs, "expert", axis=0, tiled=True),
        lax.all_gather(route_ids, "expert", axis=0, tiled=True),
        lax.all_gather(route_wts, "expert", axis=0, tiled=True),
    )
    partial_value = project_part(feats, proj_in, proj_out)
    projected = lax.psum(partial_value.astype(jnp.bfloat16), "expert")
    block_start = jnp.arange(offsets.shape[0], dtype=jnp.int32) // img_dev * tok_dev
    embed_group = texts.at[offsets + block_start].set(projected)
    normed = normalize(embed_group, norm_gain)
    own_rows = lax.dynamic_slice_in_dim(embed_group, my_place * tok_dev, tok_dev, 0)
    gate_s = jnp.dot(normed, shared_gate, preferred_element_type=jnp.float32)
    up_s = jnp.dot(normed, shared_up, preferred_element_type=jnp.float32)
    shared_hidden = (jax.nn.silu(gate_s) * up_s).astype(jnp.bfloat16)
    group_rows = normed.shape[0]
    top_count = ids.shape[1]
    capacity = 3 * group_rows * top_count // (2 * n_data)
    share = capacity // n_group
    flat_ids = ids.reshape(-1)
    onehot = (flat_ids[:, None] == jnp.arange(n_data, dtype=jnp.int32)[None, :]).astype(jnp.int32)
    rank = jnp.sum(jnp.cumsum(onehot, axis=0) * onehot, axis=1) - 1
    pair_token = jnp.arange(group_rows * top_count, dtype=jnp.int32) // top_count
    send = (
        jnp.zeros((n_data, capacity, width_model), jnp.bfloat16)
        .at[flat_ids, rank]
        .set(normed[pair_token])
    )
    slots = lax.all_to_all(send, "dp", split_axis=0, concat_axis=0, tiled=True)
    gate_e = jnp.einsum("ncd,df->ncf", slots, expert_gate[0], preferred_element_type=jnp.float32)
    up_e = jnp.einsum("ncd,df->ncf", slots, expert_up[0], preferred_element_type=jnp.float32)
    hidden_e = (jax.nn.silu(gate_e) * up_e).astype(jnp.bfloat16)
    partial_out = jnp.einsum(
        "ncf,fd->ncd", hidden_e, expert_down[0], preferred_element_type=jnp.float32
    )
    summed = lax.psum_scatter(
        partial_out.astype(jnp.bfloat16), "expert", scatter_dimension=1, tiled=True
    )
    returned = lax.all_to_all(summed, "dp", split_axis=0, concat_axis=0, tiled=True)
    inside = rank // share == my_place
    local_slot = jnp.where(inside, rank - my_place * share, 0)
    picked = returned.reshape(n_data * share, width_model)[flat_ids * share + local_slot]
    weights_f = weights.astype(jnp.float32)
    weights_n = weights_f / jnp.sum(weights_f, axis=1, keepdims=True)
    coef = jnp.where(inside, weights_n.reshape(-1), 0.0)
    combined = jnp.sum(
        (picked.astype(jnp.float32) * coef[:, None]).reshape(group_rows, top_count, width_model),
        axis=1,
    )
    total = lax.psum_scatter(
        (jnp.dot(shared_hidden, shared_down, preferred_element_type=jnp.float32) + combined).astype(
            jnp.bfloat16
        ),
        "expert",
        scatter_dimension=0,
        tiled=True,
    ).astype(jnp.float32)
    return (own_rows.astype(jnp.float32) + total).astype(jnp.bfloat16)


def solution(mesh):
    return jax.shard_map(
        shards,
        mesh=mesh,
        in_specs=(
            P(("dp", "expert"), None),
            P(("dp", "expert"), None),
            P(("dp", "expert")),
            P(None, "expert"),
            P("expert", None),
            P(),
            P(None, "expert"),
            P(None, "expert"),
            P("expert", None),
            P("dp", None, "expert"),
            P("dp", None, "expert"),
            P("dp", "expert", None),
            P(("dp", "expert"), None),
            P(("dp", "expert"), None),
        ),
        out_specs=P(("dp", "expert"), None),
        check_vma=False,
    )
```

profile of v0, /device:TPU:1, one launch (start us, length us, event | category | flops | bytes accessed | tf_op | source)
XLA Modules:
  0.0 532.2 jit_solution(12676066431425173796)
XLA Ops:
  12.4 21.6 %all_to_all.21 = bf16[32,2,2304]{2,1,0:T(2,128)(2,1)S(1)} all-to-all(bf16[32,2,2304]{2,1,0:T(2,128)(2,1)S(1)} %reshape.350), channel_id=1, replica_groups=mesh['dp'=32,'expert'=8] {'dp'}, dimensions={0} | all-to-all | bytes 589824 | tf_op jit(solution)/shard_map/all_to_all | solution.py:49
  37.3 6.7 %all-to-all-start = ((s32[32,1,1]{2,1,0:T(1,128)}), s32[32,1,1]{2,1,0:T(1,128)S(1)}, u32[]{:S(2)}, u32[]{:S(2)}) async-start(s32[32,1,1]{2,1,0:T(1,128)} %copy.48), calls=%async_computation | async-start | bytes 32768 | tf_op jit(solution)/shard_map/all_to_all | solution.py:50
  44.1 12.5 %all-gather.2 = s32[8,64,2]{1,2,0:T(2,128)S(1)} all-gather(s32[1,64,2]{1,2,0:T(2,128)S(1)} %bitcast.70), channel_id=1, replica_groups=mesh['dp'=32,'expert'=8] {'expert'}, dimensions={0}, use_global_device_ids=true | all-gather | bytes 4608 | tf_op jit(solution)/shard_map/all_gather | solution.py:58
  57.2 9.0 %reduce-window.6 = s32[32,8,128]{2,1,0:T(8,128)S(1)} reduce-window(s32[32,8,128]{2,1,0:T(8,128)S(1)} %fusion.38, s32[]{:T(128)} %constant.99.clone.1), window={size=1x1x128 pad=0_0x0_0x127_0}, to_apply=%region_4.5 | reduce-window | flops 4161536 | bytes 262148 | tf_op jit(solution)/shard_map/reduce-window
  67.1 4.6 convolution_convert_fusion.1
  74.0 4.7 all-reduce
  78.8 14.8 %all-gather.7.cloned.1.call-done = bf16[512,2048]{1,0:T(8,128)(2,1)} async-done(((bf16[64,2048]{1,0:T(8,128)(2,1)}), bf16[512,2048]{1,0:T(8,128)(2,1)}) %all-gather.7.cloned.1.call-update) | async-done | bytes 2097168 | tf_op jit(solution)/shard_map/all_gather | solution.py:55
  93.6 67.9 %all-reduce.3.cloned.1.call-done = bf16[256,2048]{1,0:T(8,128)(2,1)} async-done(((bf16[256,2048]{1,0:T(8,128)(2,1)}), bf16[256,2048]{1,0:T(8,128)(2,1)}) %all-reduce.3.cloned.1.call-update) | async-done | bytes 1048592 | tf_op jit(solution)/shard_map/psum | solution.py:62
  161.5 6.4 %scatter_fusion = bf16[512,2048]{1,0:T(8,128)(2,1)} fusion(bf16[512,2048]{1,0:T(8,128)(2,1)} %all-gather.7.cloned.1.call-done, s32[256]{0:T(256)S(1)} %compare_select_fusion.5, bf16[256,2048]{1,0:T(8,128)(2,1)} %all-reduce.3.cloned.1.call-done), kind=kCustom, calls=%fused_computation.4 | custom fusion | bytes 3146752 | tf_op jit(solution)/shard_map/scatter | solution.py:64
  172.1 22.1 %scatter_custom_fusion.1 = bf16[1536,2048]{1,0:T(8,128)(2,1)} fusion(s32[1024]{0:T(1024)S(1)} %get-tuple-element.14, bf16[512,2048]{1,0:T(8,128)(2,1)} %fusion.2, s32[1024]{0:T(1024)S(1)} %get-tuple-element.13, bf16[]{:T(256)} %constant.118.clone.1), kind=kCustom, calls=%fused_computation.13 | custom fusion | bytes 6291968
  194.1 145.5 %all_to_all.22 = bf16[32,48,2048]{2,1,0:T(8,128)(2,1)S(1)} all-to-all(bf16[32,48,2048]{2,1,0:T(8,128)(2,1)} %bitcast.61), channel_id=1, replica_groups=mesh['dp'=32,'expert'=8] {'dp'}, dimensions={0} | all-to-all | bytes 12582912 | tf_op jit(solution)/shard_map/all_to_all | solution.py:83
  342.3 3.0 fusion.13
  345.3 12.3 %convolution_convert_fusion = bf16[32,48,2048]{2,1,0:T(8,128)(2,1)} fusion(f32[32,48,176]{2,1,0:T(8,128)} %fusion.13, bf16[32,48,2048]{2,1,0:T(8,128)(2,1)} %copy-done.4, bf16[1,176,2048]{2,1,0:T(8,128)(2,1)S(1)} %copy-done.11, bf16[1,2048,176]{1,2,0:T(8,128)(2,1)S(1)} %copy-done.12), kind=kOutput, calls=%fused_computation.9 | convolution fusion | flops 2219360256 | bytes 15106048 | tf_op jit(solution)/shard_map/ncf,fd->ncd/dot_general | solution.py:87
  357.6 8.9 %copy.57 = bf16[32,48,2048]{2,0,1:T(8,128)(2,1)} copy(bf16[32,48,2048]{2,1,0:T(8,128)(2,1)} %convolution_convert_fusion) | data formatting | bytes 12582912 | tf_op jit(solution)/shard_map/convert_element_type | solution.py:91
  366.5 47.4 %reduce-scatter.3.cloned.1.call-done = bf16[32,6,2048]{2,0,1:T(8,128)(2,1)} async-done(((bf16[32,48,2048]{2,0,1:T(8,128)(2,1)}), bf16[32,6,2048]{2,0,1:T(8,128)(2,1)}) %reduce-scatter.3.cloned.1.call-update) | async-done | bytes 786448 | tf_op jit(solution)/shard_map/reduce_scatter | solution.py:90
  416.5 9.5 %all-to-all-start.3 = ((bf16[32,6,2048]{2,1,0:T(8,128)(2,1)}), bf16[32,6,2048]{2,1,0:T(8,128)(2,1)S(1)}, u32[]{:S(2)}, u32[]{:S(2)}) async-start(bf16[32,6,2048]{2,1,0:T(8,128)(2,1)} %copy.58), calls=%async_computation.4 | async-start | bytes 2097152 | tf_op jit(solution)/shard_map/all_to_all | solution.py:93
  426.8 10.0 %all-gather.3 = s32[8,64,2]{1,2,0:T(2,128)S(1)} all-gather(s32[1,64,2]{1,2,0:T(2,128)S(1)} %bitcast.71), channel_id=1, replica_groups=mesh['dp'=32,'expert'=8] {'expert'}, dimensions={0}, use_global_device_ids=true | all-gather | bytes 4608 | tf_op jit(solution)/shard_map/all_gather | solution.py:59
  437.2 2.9 fusion.50
  440.1 10.5 %all-to-all-done.3 = bf16[32,6,2048]{2,1,0:T(8,128)(2,1)S(1)} async-done(((bf16[32,6,2048]{2,1,0:T(8,128)(2,1)}), bf16[32,6,2048]{2,1,0:T(8,128)(2,1)S(1)}, u32[]{:S(2)}, u32[]{:S(2)}) %all-to-all-start.3) | async-done | bytes 786464 | tf_op jit(solution)/shard_map/all_to_all | solution.py:93
  450.9 6.1 %gather_fusion.2 = bf16[1024,2048]{1,0:T(8,128)(2,1)} fusion(bf16[192,2048]{1,0:T(8,128)(2,1)S(1)} %reshape.268, s32[1024]{0:T(1024)S(1)} %broadcast_clamp_fusion), kind=kCustom, calls=%fused_computation.3 | custom fusion | bytes 8392704 | tf_op jit(solution)/shard_map/gather | solution.py:96
  457.0 9.6 %reshape.273 = f32[512,2,2048]{2,1,0:T(2,128)} reshape(bf16[1024,2048]{1,0:T(8,128)(2,1)} %gather_fusion.2) | data formatting | bytes 12582912 | tf_op jit(solution)/shard_map/convert_element_type | solution.py:101
  466.7 15.5 %multiply_reduce_fusion = f32[512,2048]{1,0:T(8,128)} fusion(f32[512,2,2048]{2,1,0:T(2,128)} %reshape.273, f32[512,2]{1,0:T(8,128)S(1)} %fusion.31), kind=kLoop, calls=%fused_computation.6 | loop fusion | flops 3145728 | bytes 12587008 | tf_op jit(solution)/shard_map/reduce_sum | solution.py:100
  482.1 7.4 %add_convert_fusion = bf16[512,2048]{1,0:T(8,128)(2,1)} fusion(f32[512,2048]{1,0:T(8,128)} %multiply_reduce_fusion, bf16[352,2048]{1,0:T(8,128)(2,1)} %param.22, bf16[512,2048]{1,0:T(8,128)(2,1)} %fusion.2, bf16[2048,352]{0,1:T(8,128)(2,1)} %param.21, f32[512,352]{0,1:T(8,128)S(1)} %fusion.50), kind=kOutput, calls=%fused_computation.15 | convolution fusion | flops 1479573504 | bytes 11993088 | tf_op jit(solution)/shard_map/dot_general | solution.py:105
  489.6 34.0 %reduce-scatter.5.cloned.1.call-done = bf16[64,2048]{1,0:T(8,128)(2,1)} async-done(((bf16[512,2048]{1,0:T(8,128)(2,1)}), bf16[64,2048]{1,0:T(8,128)(2,1)}) %reduce-scatter.5.cloned.1.call-update) | async-done | bytes 262160 | tf_op jit(solution)/shard_map/reduce_scatter | solution.py:104
  (93 shorter events, 24.7 us)
Async XLA Ops:
  6.5 60.5 %copy-start = (bf16[4608,256]{1,0:T(8,128)(2,1)S(1)}, bf16[4608,256]{1,0:T(8,128)(2,1)}, u32[]{:S(2)}) copy-start(bf16[4608,256]{1,0:T(8,128)(2,1)} %param.17) | copy-start | bytes 7077892
  6.5 60.5 %all-gather.9.cloned.1.call-start = ((), (), s32[]{:S(2)}) async-start(), calls=%async_computation.10 | async-start | bytes 2654208 | tf_op jit(solution)/shard_map/all_gather | solution.py:56
  11.0 24.8 %copy-start.2 = (s32[32]{0:T(128)S(1)}, s32[32]{0:T(128)}, u32[]{:S(2)}) copy-start(s32[32]{0:T(128)} %param.16) | copy-start | bytes 388
  11.0 33.0 %copy-start.6 = (s32[64,2]{0,1:T(2,128)S(1)}, s32[64,2]{0,1:T(2,128)}, u32[]{:S(2)}) copy-start(s32[64,2]{0,1:T(2,128)} %param.26) | copy-start | bytes 1540
  34.3 32.5 %copy-start.9 = (s32[2]{0:T(128)S(1)}, s32[2]{0:T(128)}, u32[]{:S(2)}) copy-start(s32[2]{0:T(128)} %constant.129) | copy-start | bytes 28
  34.3 32.6 %copy-start.8 = (s32[2]{0:T(128)S(1)}, s32[2]{0:T(128)}, u32[]{:S(2)}) copy-start(s32[2]{0:T(128)} %constant.132) | copy-start | bytes 28
  35.1 58.5 %all-gather.7.cloned.1.call-start = ((), (), s32[]{:S(2)}) async-start(), calls=%async_computation.6 | async-start | bytes 2359296 | tf_op jit(solution)/shard_map/all_gather | solution.py:55
  37.3 35.9 %all-to-all-start = ((s32[32,1,1]{2,1,0:T(1,128)}), s32[32,1,1]{2,1,0:T(1,128)S(1)}, u32[]{:S(2)}, u32[]{:S(2)}) async-start(s32[32,1,1]{2,1,0:T(1,128)} %copy.48), calls=%async_computation | async-start | bytes 32768 | tf_op jit(solution)/shard_map/all_to_all | solution.py:50
  44.0 117.5 %all-reduce.3.cloned.1.call-start = ((), (), s32[]{:S(2)}) async-start(), calls=%async_computation.7 | async-start | bytes 2097152 | tf_op jit(solution)/shard_map/psum | solution.py:62
  67.0 4.7 copy-start.13
  71.7 342.3 %reduce-scatter.3.cloned.1.call-start = ((), (), s32[]{:S(2)}) async-start(), calls=%async_computation.8 | async-start | bytes 7077888 | tf_op jit(solution)/shard_map/reduce_scatter | solution.py:90
  78.7 91.4 %copy-start.5 = (f32[2048]{0:T(1024)S(1)}, f32[2048]{0:T(1024)}, u32[]{:S(2)}) copy-start(f32[2048]{0:T(1024)} %param.19) | copy-start | bytes 24580
  167.9 2.3 copy-start.3
  194.1 148.1 %copy-start.10 = (bf16[1,2048,176]{1,2,0:T(8,128)(2,1)S(1)}, bf16[1,2048,176]{1,2,0:T(8,128)(2,1)}, u32[]{:S(2)}) copy-start(bf16[1,2048,176]{1,2,0:T(8,128)(2,1)} %param.23) | copy-start | bytes 2162692
  339.6 2.7 copy-start.4
  342.3 3.0 copy-start.11
  342.3 3.0 copy-start.12
  366.5 60.3 %copy-start.7 = (s32[64,2]{0,1:T(2,128)S(1)}, s32[64,2]{0,1:T(2,128)}, u32[]{:S(2)}) copy-start(s32[64,2]{0,1:T(2,128)} %param.27) | copy-start | bytes 1540
  416.5 34.2 %all-to-all-start.3 = ((bf16[32,6,2048]{2,1,0:T(8,128)(2,1)}), bf16[32,6,2048]{2,1,0:T(8,128)(2,1)S(1)}, u32[]{:S(2)}, u32[]{:S(2)}) async-start(bf16[32,6,2048]{2,1,0:T(8,128)(2,1)} %copy.58), calls=%async_computation.4 | async-start | bytes 2097152 | tf_op jit(solution)/shard_map/all_to_all | solution.py:93
  426.0 97.6 %reduce-scatter.5.cloned.1.call-start = ((), (), s32[]{:S(2)}) async-start(), calls=%async_computation.9 | async-start | bytes 2359296 | tf_op jit(solution)/shard_map/reduce_scatter | solution.py:104
  482.1 43.3 %copy-start.1 = (bf16[4608,256]{1,0:T(8,128)(2,1)S(1)}, bf16[4608,256]{1,0:T(8,128)(2,1)}, u32[]{:S(2)}) copy-start(bf16[4608,256]{1,0:T(8,128)(2,1)} %param.17) | copy-start | bytes 7077892
Sparse Core Ops, SparseCore 0:
  35.2 28.1 all-gather.8
  65.3 28.2 all-gather.6
  96.0 65.4 all-reduce.2
  366.6 47.2 reduce-scatter.2
  489.7 33.8 reduce-scatter.4
where the time goes:
time: 541 us; the launch traced here: 532 us
  blocking collectives  194 us (36%)
  waiting for transfers between devices  176 us (33%)
  local copies, waits for them, and re-layouts  66.2 us (12%)
  other arithmetic  35 us (6%)
  matrix products  30.3 us (6%)
  starting transfers between devices  16.6 us (3%)
  between operations  14.4 us (3%)
    all_to_all x1, blocking collectives, shards(): slots = lax.all_to_all(send, 'dp', split_axis=0, concat_axis=0, tiled=True)  145 us
    psum x1, waiting for transfers between devices, shards(): projected = lax.psum(partial_value.astype(jnp.bfloat16), 'expert')  67.9 us
    reduce_scatter x1, waiting for transfers between devices, shards(): lax.psum_scatter(partial_out.astype(jnp.bfloat16), 'expert', scatter_dime...  47.4 us
    reduce_scatter x1, waiting for transfers between devices, shards(): lax.psum_scatter((jnp.dot(shared_hidden, shared_down, preferred_element_t...  34 us
    unnamed x34, local copies, waits for them, and re-layouts  26 us
    all_to_all x1, blocking collectives, shards(): lax.all_to_all(sorted_feats, 'dp', split_axis=0, concat_axis=0, tiled=True)  21.6 us
    reduce_sum x1, other arithmetic, shards(): jnp.sum((picked.astype(jnp.float32) * coef[:, None]).reshape(group_rows,...  15.5 us
    all_gather x1, waiting for transfers between devices, shards(): lax.all_gather(text_embed, 'expert', axis=0, tiled=True)  14.8 us
  transfers between devices with their start and end apart: 7, of which 5 were waited for; matrix products, arithmetic and copies ran while one was open for 4% of the time, Pallas kernels for 0%

commit v1 on v0

v1 whole, which is shorter than its diff:
```python
import jax
import jax.numpy as jnp
from jax import lax
from jax.sharding import PartitionSpec as P


def normalize(rows, norm_gain):
    rows_f = rows.astype(jnp.float32)
    meansq = jnp.mean(rows_f * rows_f, axis=-1, keepdims=True) + 1e-06
    return (rows_f * lax.rsqrt(meansq) * norm_gain).astype(jnp.bfloat16)


def select_dot(sel, rows):
    return jnp.dot(sel, rows, preferred_element_type=jnp.float32)


def shards(
    text_embed,
    image_feats,
    tile_pos,
    proj_in,
    proj_out,
    norm_gain,
    shared_gate,
    shared_up,
    shared_down,
    expert_gate,
    expert_up,
    expert_down,
    route_ids,
    route_wts,
):
    bf16, f32 = jnp.bfloat16, jnp.float32
    tok_dev, width_model = text_embed.shape
    img_dev, width_vis = image_feats.shape
    n_data = lax.axis_size("dp")
    n_group = lax.axis_size("expert")
    peer = img_dev // n_data
    my_place = lax.axis_index("expert")

    dest_index = tile_pos // tok_dev // n_group
    order = jnp.argsort(dest_index, stable=True)
    offs_sorted = (tile_pos[order] % tok_dev).astype(bf16)
    pad = 128
    packed = jnp.concatenate(
        [image_feats[order], jnp.broadcast_to(offs_sorted[:, None], (img_dev, pad))], axis=1
    ).reshape(n_data, peer, width_vis + pad)
    moved = lax.all_to_all(packed, "dp", split_axis=0, concat_axis=0, tiled=True)
    moved = moved.reshape(img_dev, width_vis + pad)
    moved_feats = moved[:, :width_vis]
    moved_offs = moved[:, width_vis].astype(jnp.int32)

    feats = lax.all_gather(moved_feats, "expert", axis=0, tiled=True)
    vis_hidden = jax.nn.gelu(
        jnp.dot(feats, proj_in, preferred_element_type=f32), approximate=True
    ).astype(bf16)
    partial_proj = jnp.dot(vis_hidden, proj_out, preferred_element_type=f32).astype(bf16)
    projected = lax.psum_scatter(partial_proj, "expert", scatter_dimension=0, tiled=True)

    place = (
        moved_offs[None, :] == jnp.arange(tok_dev, dtype=jnp.int32)[:, None]
    ).astype(bf16)
    placed = select_dot(place, projected)
    has_image = jnp.sum(place.astype(f32), axis=1, keepdims=True) > 0
    embed_own = jnp.where(has_image, placed, text_embed.astype(f32))
    normed_own = normalize(embed_own, norm_gain)

    normed = lax.all_gather(normed_own, "expert", axis=0, tiled=True)
    routes = lax.all_gather(
        jnp.concatenate([route_ids, route_wts], axis=1), "expert", axis=0, tiled=True
    )
    top_count = route_ids.shape[1]
    ids = routes[:, :top_count]
    weights = routes[:, top_count:]

    gate_s = jnp.dot(normed, shared_gate, preferred_element_type=f32)
    up_s = jnp.dot(normed, shared_up, preferred_element_type=f32)
    shared_hidden = (jax.nn.silu(gate_s) * up_s).astype(bf16)

    group_rows = normed.shape[0]
    n_pairs = group_rows * top_count
    capacity = 3 * group_rows * top_count // (2 * n_data)
    share = capacity // n_group
    flat_ids = ids.reshape(-1)
    onehot = (flat_ids[:, None] == jnp.arange(n_data, dtype=jnp.int32)[None, :]).astype(bf16)
    pair_iota = jnp.arange(n_pairs, dtype=jnp.int32)
    earlier = (pair_iota[None, :] < pair_iota[:, None]).astype(bf16)
    counts = select_dot(earlier, onehot)
    rank = jnp.sum(counts * onehot.astype(f32), axis=1).astype(jnp.int32)

    inside = rank // share == my_place
    row_of = jnp.where(inside, flat_ids * share + rank - my_place * share, -1)
    n_rows = n_data * share
    hit = (
        row_of.reshape(group_rows, top_count)[:, :, None]
        == jnp.arange(n_rows, dtype=jnp.int32)[None, None, :]
    )
    pick = jnp.sum(hit.astype(f32), axis=1).astype(bf16)
    send = select_dot(pick.T, normed).astype(bf16).reshape(n_data, share, width_model)
    arrived = lax.all_to_all(send, "dp", split_axis=0, concat_axis=0, tiled=True)
    slots = lax.all_gather(
        arrived.reshape(n_rows, width_model), "expert", axis=0, tiled=True
    )

    gate_e = jnp.dot(slots, expert_gate[0], preferred_element_type=f32)
    up_e = jnp.dot(slots, expert_up[0], preferred_element_type=f32)
    hidden_e = (jax.nn.silu(gate_e) * up_e).astype(bf16)
    partial_out = jnp.dot(hidden_e, expert_down[0], preferred_element_type=f32).astype(bf16)
    summed = lax.psum_scatter(partial_out, "expert", scatter_dimension=0, tiled=True)
    returned = lax.all_to_all(
        summed.reshape(n_data, share, width_model), "dp", split_axis=0, concat_axis=0, tiled=True
    ).reshape(n_rows, width_model)

    weights_f = weights.astype(f32)
    weights_n = weights_f / jnp.sum(weights_f, axis=1, keepdims=True)
    coef = jnp.sum(jnp.where(hit, weights_n[:, :, None], 0.0), axis=1)
    coef_hi = coef.astype(bf16)
    coef_lo = (coef - coef_hi.astype(f32)).astype(bf16)
    combined = select_dot(coef_hi, returned) + select_dot(coef_lo, returned)
    total = lax.psum_scatter(
        (jnp.dot(shared_hidden, shared_down, preferred_element_type=f32) + combined).astype(bf16),
        "expert",
        scatter_dimension=0,
        tiled=True,
    ).astype(f32)
    return (embed_own + total).astype(bf16)


def solution(mesh):
    return jax.shard_map(
        shards,
        mesh=mesh,
        in_specs=(
            P(("dp", "expert"), None),
            P(("dp", "expert"), None),
            P(("dp", "expert")),
            P(None, "expert"),
            P("expert", None),
            P(),
            P(None, "expert"),
            P(None, "expert"),
            P("expert", None),
            P("dp", None, "expert"),
            P("dp", None, "expert"),
            P("dp", "expert", None),
            P(("dp", "expert"), None),
            P(("dp", "expert"), None),
        ),
        out_specs=P(("dp", "expert"), None),
        check_vma=False,
    )
```

time: 541 us -> 375 us (0.69); the launches traced: 532 us -> 373 us
  blocking collectives: 194 us -> 70.7 us
  local copies, waits for them, and re-layouts: 66.2 us -> 12.8 us
  waiting for transfers between devices: 176 us -> 216 us
  other arithmetic: 35 us -> 6.97 us
  matrix products: 30.3 us -> 42.7 us
  starting transfers between devices: 16.6 us -> 10.1 us
    all_to_all x2, blocking collectives: 167 us -> 56.5 us  [the longest x1 34.9 us: shards(): lax.all_to_all(send, 'dp', split_axis=0, concat_axis=0, tiled=True)]
    all_gather x2 -> x3, waiting for transfers between devices: 14.9 us -> 84.8 us  [the longest x1 42.9 us: shards(): lax.all_gather(arrived.reshape(n_rows, width_model), 'expert', axis=0, ti...]
    psum x1 -> x0, waiting for transfers between devices: 67.9 us -> none  [shards(): projected = lax.psum(partial_value.astype(jnp.bfloat16), 'expert')]
    reduce_scatter x1 -> x2, waiting for transfers between devices: 47.4 us -> 76.3 us  [the longest x1 44.3 us: shards(): lax.psum_scatter(partial_out, 'expert', scatter_dimension=0, tiled=True)]
    unnamed x34 -> x22, local copies, waits for them, and re-layouts: 26 us -> 1.73 us
    convert_element_type x3 -> x2, local copies, waits for them, and re-layouts: 18.7 us -> 0.31 us  [shards(): rank = jnp.sum(counts * onehot.astype(f32), axis=1).astype(jnp.int32)]
    reduce_sum x3 -> x2, other arithmetic: 17.7 us -> 1 us  [the longest x1 0.91 us: shards(): coef = jnp.sum(jnp.where(hit, weights_n[:, :, None], 0.0), axis=1)]
    all_gather x3 -> x1, blocking collectives: 27.1 us -> 14.2 us  [shards(): lax.all_gather(jnp.concatenate([route_ids, route_wts], axis=1), 'expert',...]
  transfers between devices with their start and end apart: 7 -> 7, of which waited for: 5 -> 7; matrix products, arithmetic and copies ran while one was open for 4% -> 2% of each run, Pallas kernels for 0% -> 0%
where the time goes in v1:
time: 375 us; the launch traced here: 373 us
  waiting for transfers between devices  216 us (58%)
  blocking collectives  70.7 us (19%)
  matrix products  42.7 us (11%)
  between operations  13.7 us (4%)
  local copies, waits for them, and re-layouts  12.8 us (3%)
  starting transfers between devices  10.1 us (3%)
  other arithmetic  6.97 us (2%)
    reduce_scatter x1, waiting for transfers between devices, shards(): lax.psum_scatter(partial_out, 'expert', scatter_dimension=0, tiled=True)  44.3 us
    all_gather x1, waiting for transfers between devices, shards(): lax.all_gather(arrived.reshape(n_rows, width_model), 'expert', axis=0, ti...  42.9 us
    all_to_all x1, blocking collectives, shards(): lax.all_to_all(send, 'dp', split_axis=0, concat_axis=0, tiled=True)  34.9 us
    reduce_scatter x1, waiting for transfers between devices, shards(): lax.psum_scatter((jnp.dot(shared_hidden, shared_down, preferred_element_t...  34 us
    reduce_scatter x1, waiting for transfers between devices, shards(): lax.psum_scatter(partial_proj, 'expert', scatter_dimension=0, tiled=True)  32 us
    all_gather x1, waiting for transfers between devices, shards(): feats = lax.all_gather(moved_feats, 'expert', axis=0, tiled=True)  28.6 us
    all_to_all x1, blocking collectives, shards(): lax.all_to_all(packed, 'dp', split_axis=0, concat_axis=0, tiled=True)  21.6 us
    all_to_all x1, waiting for transfers between devices, shards(): lax.all_to_all(summed.reshape(n_data, share, width_model), 'dp', split_ax...  20.8 us
  transfers between devices with their start and end apart: 7, of which 7 were waited for; matrix products, arithmetic and copies ran while one was open for 2% of the time, Pallas kernels for 0%

profile of v1, /device:TPU:1, one launch (start us, length us, event | category | flops | bytes accessed | tf_op | source)
XLA Modules:
  0.0 372.9 jit_solution(14832235509471755536)
XLA Ops:
  7.4 1.6 sort.17
  12.8 21.6 %all_to_all.15 = bf16[32,2,2368]{2,1,0:T(2,128)(2,1)S(1)} all-to-all(bf16[32,2,2368]{2,1,0:T(2,128)(2,1)S(1)} %reshape.103), channel_id=1, replica_groups=mesh['dp'=32,'expert'=8] {'dp'}, dimensions={0} | all-to-all | bytes 606208 | tf_op jit(solution)/shard_map/all_to_all | solution.py:48
  35.8 28.6 %all-gather.5.cloned.1.call-done = bf16[256,4608]{1,0:T(8,128)(2,1)} async-done(((bf16[32,4608]{1,0:T(8,128)(2,1)}), bf16[256,4608]{1,0:T(8,128)(2,1)}) %all-gather.5.cloned.1.call-update) | async-done | bytes 2359312 | tf_op jit(solution)/shard_map/all_gather | solution.py:53
  64.4 4.6 %convolution_convert_fusion.1 = bf16[256,2048]{1,0:T(8,128)(2,1)} fusion(bf16[256,2048]{1,0:T(8,128)(2,1)} %param.18, bf16[256,4608]{1,0:T(8,128)(2,1)} %all-gather.5.cloned.1.call-done, bf16[4608,256]{1,0:T(8,128)(2,1)S(1)} %copy-done), kind=kOutput, calls=%fused_computation.7 | convolution fusion | flops 873529344 | bytes 6815744 | tf_op jit(solution)/shard_map/dot_general | solution.py:57
  69.2 32.0 %reduce-scatter.4.cloned.1.call-done = bf16[32,2048]{1,0:T(8,128)(2,1)} async-done(((bf16[256,2048]{1,0:T(8,128)(2,1)}), bf16[32,2048]{1,0:T(8,128)(2,1)}) %reduce-scatter.4.cloned.1.call-update) | async-done | bytes 131088 | tf_op jit(solution)/shard_map/reduce_scatter | solution.py:58
  104.4 14.2 %all-gather = s32[8,64,4]{1,2,0:T(4,128)S(1)} all-gather(s32[1,64,4]{1,2,0:T(4,128)S(1)} %add_bitcast_fusion), channel_id=1, replica_groups=mesh['dp'=32,'expert'=8] {'expert'}, dimensions={0}, use_global_device_ids=true | all-gather | bytes 9216 | tf_op jit(solution)/shard_map/all_gather | solution.py:69
  120.8 13.4 %all-gather.7.cloned.1.call-done = bf16[512,2048]{1,0:T(8,128)(2,1)} async-done(((bf16[64,2048]{1,0:T(8,128)(2,1)}), bf16[512,2048]{1,0:T(8,128)(2,1)}) %all-gather.7.cloned.1.call-update) | async-done | bytes 2097168 | tf_op jit(solution)/shard_map/all_gather | solution.py:68
  134.2 2.3 convolution_convert_fusion.2
  137.8 34.9 %all_to_all.16 = bf16[32,6,2048]{2,1,0:T(8,128)(2,1)} all-to-all(bf16[32,6,2048]{2,1,0:T(8,128)(2,1)} %reshape.77), channel_id=1, replica_groups=mesh['dp'=32,'expert'=8] {'dp'}, dimensions={0} | all-to-all | bytes 1572864 | tf_op jit(solution)/shard_map/all_to_all | solution.py:100
  172.7 2.1 reshape.78
  175.1 42.9 %all-gather.9.cloned.1.call-done = bf16[1536,2048]{1,0:T(8,128)(2,1)} async-done(((bf16[192,2048]{1,0:T(8,128)(2,1)}), bf16[1536,2048]{1,0:T(8,128)(2,1)}) %all-gather.9.cloned.1.call-update) | async-done | bytes 6291472 | tf_op jit(solution)/shard_map/all_gather | solution.py:101
  218.0 6.0 %fusion.13 = f32[1536,176]{0,1:T(8,128)} fusion(bf16[1536,2048]{1,0:T(8,128)(2,1)} %all-gather.9.cloned.1.call-done, bf16[1,2048,176]{1,2,0:T(8,128)(2,1)S(1)} %copy-done.8), kind=kOutput, calls=%fused_computation.25 | convolution fusion | flops 1107296256 | bytes 8093696 | tf_op jit(solution)/shard_map/dot_general | solution.py:105
  224.0 10.0 %convolution_convert_fusion = bf16[1536,2048]{1,0:T(8,128)(2,1)} fusion(bf16[1536,2048]{1,0:T(8,128)(2,1)} %all-gather.9.cloned.1.call-done, f32[1536,176]{0,1:T(8,128)} %fusion.13, bf16[1,176,2048]{2,1,0:T(8,128)(2,1)} %param.25, bf16[1,2048,176]{1,2,0:T(8,128)(2,1)} %param.24), kind=kOutput, calls=%fused_computation.2 | convolution fusion | flops 2219360256 | bytes 15106048 | tf_op jit(solution)/shard_map/dot_general | solution.py:108
  234.0 44.3 %reduce-scatter.6.cloned.1.call-done = bf16[192,2048]{1,0:T(8,128)(2,1)} async-done(((bf16[1536,2048]{1,0:T(8,128)(2,1)}), bf16[192,2048]{1,0:T(8,128)(2,1)}) %reduce-scatter.6.cloned.1.call-update) | async-done | bytes 786448 | tf_op jit(solution)/shard_map/reduce_scatter | solution.py:109
  278.3 2.2 reshape.79
  280.5 9.7 %all-to-all-start.2 = ((bf16[32,6,2048]{2,1,0:T(8,128)(2,1)}), bf16[32,6,2048]{2,1,0:T(8,128)(2,1)}, u32[]{:S(2)}, u32[]{:S(2)}) async-start(bf16[32,6,2048]{2,1,0:T(8,128)(2,1)} %reshape.79), calls=%async_computation.4 | async-start | bytes 2097152 | tf_op jit(solution)/shard_map/all_to_all | solution.py:110
  290.2 3.8 %fusion.51 = f32[512,352]{0,1:T(8,128)} fusion(bf16[512,2048]{1,0:T(8,128)(2,1)} %all-gather.7.cloned.1.call-done, bf16[2048,352]{0,1:T(8,128)(2,1)} %param.20), kind=kOutput, calls=%fused_computation.91 | convolution fusion | flops 738197504 | bytes 4259840 | tf_op jit(solution)/shard_map/dot_general | solution.py:76
  294.0 20.8 %all-to-all-done.2 = bf16[32,6,2048]{2,1,0:T(8,128)(2,1)} async-done(((bf16[32,6,2048]{2,1,0:T(8,128)(2,1)}), bf16[32,6,2048]{2,1,0:T(8,128)(2,1)}, u32[]{:S(2)}, u32[]{:S(2)}) %all-to-all-start.2) | async-done | bytes 786464 | tf_op jit(solution)/shard_map/all_to_all | solution.py:110
  314.8 1.4 reshape.80
  316.2 2.7 fusion.25
  318.9 2.7 fusion.34
  321.6 8.7 %add_convert_fusion = bf16[512,2048]{1,0:T(8,128)(2,1)} fusion(f32[512,2048]{1,0:T(8,128)} %fusion.34, f32[512,2048]{1,0:T(8,128)} %fusion.25, bf16[352,2048]{1,0:T(8,128)(2,1)} %param.22, bf16[512,2048]{1,0:T(8,128)(2,1)} %all-gather.7.cloned.1.call-done, bf16[2048,352]{0,1:T(8,128)(2,1)} %param.21, f32[512,352]{0,1:T(8,128)} %fusion.51), kind=kOutput, calls=%fused_computation.3 | convolution fusion | flops 1480622080 | bytes 16187392 | tf_op jit(solution)/shard_map/dot_general | solution.py:121
  330.3 34.0 %reduce-scatter.8.cloned.1.call-done = bf16[64,2048]{1,0:T(8,128)(2,1)} async-done(((bf16[512,2048]{1,0:T(8,128)(2,1)}), bf16[64,2048]{1,0:T(8,128)(2,1)}) %reduce-scatter.8.cloned.1.call-update) | async-done | bytes 262160 | tf_op jit(solution)/shard_map/reduce_scatter | solution.py:120
  364.3 1.7 add_convert_fusion.1
  (66 shorter events, 13.1 us)
Async XLA Ops:
  6.5 57.8 %copy-start = (bf16[4608,256]{1,0:T(8,128)(2,1)S(1)}, bf16[4608,256]{1,0:T(8,128)(2,1)}, u32[]{:S(2)}) copy-start(bf16[4608,256]{1,0:T(8,128)(2,1)} %param.17) | copy-start | bytes 7077892
  6.5 3.8 %copy-start.1 = (bf16[32,4608]{1,0:T(8,128)(2,1)S(1)}, bf16[32,4608]{1,0:T(8,128)(2,1)}, u32[]{:S(2)}) copy-start(bf16[32,4608]{1,0:T(8,128)(2,1)} %param.15) | copy-start | bytes 884740
  6.5 57.8 %all-gather.5.cloned.1.call-start = ((), (), s32[]{:S(2)}) async-start(), calls=%async_computation.6 | async-start | bytes 2654208 | tf_op jit(solution)/shard_map/all_gather | solution.py:53
  35.7 65.6 %copy-start.4 = (bf16[64,2048]{1,0:T(8,128)(2,1)S(1)}, bf16[64,2048]{1,0:T(8,128)(2,1)}, u32[]{:S(2)}) copy-start(bf16[64,2048]{1,0:T(8,128)(2,1)} %param.14) | copy-start | bytes 786436
  35.7 67.7 %copy-start.5 = (f32[2048]{0:T(1024)S(1)}, f32[2048]{0:T(1024)}, u32[]{:S(2)}) copy-start(f32[2048]{0:T(1024)} %param.19) | copy-start | bytes 24580
  35.7 65.6 %reduce-scatter.4.cloned.1.call-start = ((), (), s32[]{:S(2)}) async-start(), calls=%async_computation.7 | async-start | bytes 1179648 | tf_op jit(solution)/shard_map/reduce_scatter | solution.py:58
  69.0 35.4 %copy-start.6 = (s32[64,2]{0,1:T(2,128)S(1)}, s32[64,2]{0,1:T(2,128)}, u32[]{:S(2)}) copy-start(s32[64,2]{0,1:T(2,128)} %param.27) | copy-start | bytes 1540
  69.0 35.4 %copy-start.7 = (s32[64,2]{0,1:T(2,128)S(1)}, s32[64,2]{0,1:T(2,128)}, u32[]{:S(2)}) copy-start(s32[64,2]{0,1:T(2,128)} %param.26) | copy-start | bytes 1540
  69.0 65.2 %all-gather.7.cloned.1.call-start = ((), (), s32[]{:S(2)}) async-start(), calls=%async_computation.8 | async-start | bytes 2359296 | tf_op jit(solution)/shard_map/all_gather | solution.py:68
  102.6 0.8 copy-start.2
  104.3 113.7 %all-gather.9.cloned.1.call-start = ((), (), s32[]{:S(2)}) async-start(), calls=%async_computation.9 | async-start | bytes 7077888 | tf_op jit(solution)/shard_map/all_gather | solution.py:101
  137.8 80.2 %copy-start.8 = (bf16[1,2048,176]{1,2,0:T(8,128)(2,1)S(1)}, bf16[1,2048,176]{1,2,0:T(8,128)(2,1)}, u32[]{:S(2)}) copy-start(bf16[1,2048,176]{1,2,0:T(8,128)(2,1)} %param.23) | copy-start | bytes 2162692
  174.9 103.4 %reduce-scatter.6.cloned.1.call-start = ((), (), s32[]{:S(2)}) async-start(), calls=%async_computation.10 | async-start | bytes 7077888 | tf_op jit(solution)/shard_map/reduce_scatter | solution.py:109
  280.5 34.3 %all-to-all-start.2 = ((bf16[32,6,2048]{2,1,0:T(8,128)(2,1)}), bf16[32,6,2048]{2,1,0:T(8,128)(2,1)}, u32[]{:S(2)}, u32[]{:S(2)}) async-start(bf16[32,6,2048]{2,1,0:T(8,128)(2,1)} %reshape.79), calls=%async_computation.4 | async-start | bytes 2097152 | tf_op jit(solution)/shard_map/all_to_all | solution.py:110
  290.2 74.2 %reduce-scatter.8.cloned.1.call-start = ((), (), s32[]{:S(2)}) async-start(), calls=%async_computation.11 | async-start | bytes 2359296 | tf_op jit(solution)/shard_map/reduce_scatter | solution.py:120
  330.3 34.0 %copy-start.3 = (f32[64,2048]{1,0:T(8,128)S(1)}, f32[64,2048]{1,0:T(8,128)}, u32[]{:S(2)}) copy-start(f32[64,2048]{1,0:T(8,128)} %copy-done.2) | copy-start | bytes 1572868
Sparse Core Ops, SparseCore 0:
  35.8 28.5 all-gather.4
  69.1 32.1 reduce-scatter.3
  104.4 29.7 all-gather.6
  175.0 42.9 all-gather.8
  234.2 44.1 reduce-scatter.5
  330.5 33.8 reduce-scatter.7

commit v2 on v1

--- a/solution.py
+++ b/solution.py
@@ -1,7 +1,55 @@
 import jax
 import jax.numpy as jnp
 from jax import lax
+from jax.experimental import pallas as pl
+from jax.experimental.pallas import tpu as pltpu
 from jax.sharding import PartitionSpec as P
+
+
+def dp_all_to_all(x, collective_id):
+    n = x.shape[0]
+    mesh_ids = pl.DeviceIdType.MESH
+
+    def kernel(x_ref, y_ref, send_sem, recv_sem, local_sem):
+        me = lax.axis_index("dp")
+        j = lax.axis_index("expert")
+        barrier = pltpu.get_barrier_semaphore()
+        for k in range(1, n):
+            pl.semaphore_signal(
+                barrier, inc=1, device_id=(lax.rem(me + k, n), j), device_id_type=mesh_ids
+            )
+        pl.semaphore_wait(barrier, n - 1)
+        local = pltpu.make_async_copy(x_ref.at[me], y_ref.at[me], local_sem)
+        local.start()
+        copies = []
+        for k in range(1, n):
+            peer = lax.rem(me + k, n)
+            copy = pltpu.make_async_remote_copy(
+                src_ref=x_ref.at[peer],
+                dst_ref=y_ref.at[me],
+                send_sem=send_sem.at[k],
+                recv_sem=recv_sem.at[k],
+                device_id=(peer, j),
+                device_id_type=mesh_ids,
+            )
+            copy.start()
+            copies.append(copy)
+        local.wait()
+        for copy in copies:
+            copy.wait()
+
+    return pl.pallas_call(
+        kernel,
+        out_shape=jax.ShapeDtypeStruct(x.shape, x.dtype),
+        in_specs=[pl.BlockSpec(memory_space=pl.ANY)],
+        out_specs=pl.BlockSpec(memory_space=pl.ANY),
+        scratch_shapes=[
+            pltpu.SemaphoreType.DMA((n,)),
+            pltpu.SemaphoreType.DMA((n,)),
+            pltpu.SemaphoreType.DMA,
+        ],
+        compiler_params=pltpu.CompilerParams(collective_id=collective_id, has_side_effects=True),
+    )(x)
 
 
 def normalize(rows, norm_gain):
@@ -45,7 +93,7 @@
     packed = jnp.concatenate(
         [image_feats[order], jnp.broadcast_to(offs_sorted[:, None], (img_dev, pad))], axis=1
     ).reshape(n_data, peer, width_vis + pad)
-    moved = lax.all_to_all(packed, "dp", split_axis=0, concat_axis=0, tiled=True)
+    moved = dp_all_to_all(packed, 0)
     moved = moved.reshape(img_dev, width_vis + pad)
     moved_feats = moved[:, :width_vis]
     moved_offs = moved[:, width_vis].astype(jnp.int32)
@@ -97,7 +145,7 @@
     )
     pick = jnp.sum(hit.astype(f32), axis=1).astype(bf16)
     send = select_dot(pick.T, normed).astype(bf16).reshape(n_data, share, width_model)
-    arrived = lax.all_to_all(send, "dp", split_axis=0, concat_axis=0, tiled=True)
+    arrived = dp_all_to_all(send, 1)
     slots = lax.all_gather(
         arrived.reshape(n_rows, width_model), "expert", axis=0, tiled=True
     )
@@ -107,9 +155,9 @@
     hidden_e = (jax.nn.silu(gate_e) * up_e).astype(bf16)
     partial_out = jnp.dot(hidden_e, expert_down[0], preferred_element_type=f32).astype(bf16)
     summed = lax.psum_scatter(partial_out, "expert", scatter_dimension=0, tiled=True)
-    returned = lax.all_to_all(
-        summed.reshape(n_data, share, width_model), "dp", split_axis=0, concat_axis=0, tiled=True
-    ).reshape(n_rows, width_model)
+    returned = dp_all_to_all(summed.reshape(n_data, share, width_model), 2).reshape(
+        n_rows, width_model
+    )
 
     weights_f = weights.astype(f32)
     weights_n = weights_f / jnp.sum(weights_f, axis=1, keepdims=True)

time: 375 us -> 373 us (level)
  Pallas kernels: 0 us -> 88.4 us
  blocking collectives: 70.7 us -> 14.2 us
  waiting for transfers between devices: 216 us -> 192 us
  starting transfers between devices: 10.1 us -> 0.39 us
    pallas_call x0 -> x3, Pallas kernels: none -> 88.4 us  [dp_all_to_all(): pl.pallas_call(kernel, out_shape=jax.ShapeDtypeStruct(x.shape, x.dtype),...]
    all_to_all x2 -> x0, blocking collectives: 56.5 us -> none  [the longest x1 34.9 us: shards(): lax.all_to_all(send, 'dp', split_axis=0, concat_axis=0, tiled=True)]
    all_to_all x1 -> x0, waiting for transfers between devices: 20.8 us -> none  [shards(): lax.all_to_all(summed.reshape(n_data, share, width_model), 'dp', split_ax...]
    all_to_all x1 -> x0, starting transfers between devices: 9.67 us -> none  [shards(): lax.all_to_all(summed.reshape(n_data, share, width_model), 'dp', split_ax...]
    reduce_scatter x1, waiting for transfers between devices: 44.3 us -> 40.4 us  [shards(): lax.psum_scatter(partial_out, 'expert', scatter_dimension=0, tiled=True)]
  transfers between devices with their start and end apart: 7 -> 6, of which waited for: 7 -> 6; matrix products, arithmetic and copies ran while one was open for 2% -> 2% of each run, Pallas kernels for 0% -> 0%
where the time goes in v2:
time: 373 us; the launch traced here: 371 us
  waiting for transfers between devices  192 us (51%)
  Pallas kernels  88.4 us (24%)
  matrix products  42.7 us (11%)
  blocking collectives  14.2 us (4%)
  local copies, waits for them, and re-layouts  13.9 us (4%)
  between operations  13.7 us (4%)
  other arithmetic  6.19 us (2%)
    pallas_call x3, Pallas kernels, dp_all_to_all(): pl.pallas_call(kernel, out_shape=jax.ShapeDtypeStruct(x.shape, x.dtype),...  88.4 us
    all_gather x1, waiting for transfers between devices, shards(): lax.all_gather(arrived.reshape(n_rows, width_model), 'expert', axis=0, ti...  42.2 us
    reduce_scatter x1, waiting for transfers between devices, shards(): lax.psum_scatter(partial_out, 'expert', scatter_dimension=0, tiled=True)  40.4 us
    reduce_scatter x1, waiting for transfers between devices, shards(): lax.psum_scatter((jnp.dot(shared_hidden, shared_down, preferred_element_t...  34.1 us
    reduce_scatter x1, waiting for transfers between devices, shards(): lax.psum_scatter(partial_proj, 'expert', scatter_dimension=0, tiled=True)  32 us
    all_gather x1, waiting for transfers between devices, shards(): feats = lax.all_gather(moved_feats, 'expert', axis=0, tiled=True)  29.7 us
    all_gather x1, blocking collectives, shards(): lax.all_gather(jnp.concatenate([route_ids, route_wts], axis=1), 'expert',...  14.2 us
    all_gather x1, waiting for transfers between devices, shards(): normed = lax.all_gather(normed_own, 'expert', axis=0, tiled=True)  13.4 us
  transfers between devices with their start and end apart: 6, of which 6 were waited for; matrix products, arithmetic and copies ran while one was open for 2% of the time, Pallas kernels for 0%

profile of v2, /device:TPU:1, one launch (start us, length us, event | category | flops | bytes accessed | tf_op | source)
XLA Modules:
  0.0 371.3 jit_solution(1259739728335765657)
XLA Ops:
  7.4 1.6 sort.17
  9.0 1.4 gather_fusion.1
  12.5 24.7 %shard_map.136 = bf16[32,1,4736]{2,1,0:T(2,128)(2,1)} custom-call(bf16[32,1,4736]{2,1,0:T(2,128)(2,1)} %copy.33.x_ref), custom_call_target="tpu_custom_call" | custom-call | tf_op jit(solution)/shard_map/pallas_call | solution.py:41
  39.2 29.7 %all-gather.5.cloned.1.call-done = bf16[256,4608]{1,0:T(8,128)(2,1)} async-done(((bf16[32,4608]{1,0:T(8,128)(2,1)}), bf16[256,4608]{1,0:T(8,128)(2,1)}) %all-gather.5.cloned.1.call-update) | async-done | bytes 2359312 | tf_op jit(solution)/shard_map/all_gather | solution.py:101
  68.9 4.6 %convolution_convert_fusion.1 = bf16[256,2048]{1,0:T(8,128)(2,1)} fusion(bf16[256,2048]{1,0:T(8,128)(2,1)} %param.18, bf16[256,4608]{1,0:T(8,128)(2,1)} %all-gather.5.cloned.1.call-done, bf16[4608,256]{1,0:T(8,128)(2,1)S(1)} %copy-done), kind=kOutput, calls=%fused_computation.7 | convolution fusion | flops 873529344 | bytes 6815744 | tf_op jit(solution)/shard_map/dot_general | solution.py:105
  73.7 32.0 %reduce-scatter.4.cloned.1.call-done = bf16[32,2048]{1,0:T(8,128)(2,1)} async-done(((bf16[256,2048]{1,0:T(8,128)(2,1)}), bf16[32,2048]{1,0:T(8,128)(2,1)}) %reduce-scatter.4.cloned.1.call-update) | async-done | bytes 131088 | tf_op jit(solution)/shard_map/reduce_scatter | solution.py:106
  108.8 14.2 %all-gather = s32[8,64,4]{1,2,0:T(4,128)S(1)} all-gather(s32[1,64,4]{1,2,0:T(4,128)S(1)} %add_bitcast_fusion), channel_id=1, replica_groups=mesh['dp'=32,'expert'=8] {'expert'}, dimensions={0}, use_global_device_ids=true | all-gather | bytes 9216 | tf_op jit(solution)/shard_map/all_gather | solution.py:117
  125.3 13.4 %all-gather.7.cloned.1.call-done = bf16[512,2048]{1,0:T(8,128)(2,1)} async-done(((bf16[64,2048]{1,0:T(8,128)(2,1)}), bf16[512,2048]{1,0:T(8,128)(2,1)}) %all-gather.7.cloned.1.call-update) | async-done | bytes 2097168 | tf_op jit(solution)/shard_map/all_gather | solution.py:116
  138.7 2.3 convolution_convert_fusion.2
  142.3 32.5 %shard_map.137 = bf16[32,6,2048]{2,1,0:T(8,128)(2,1)} custom-call(bf16[32,6,2048]{2,1,0:T(8,128)(2,1)} %reshape.77.x_ref), custom_call_target="tpu_custom_call" | custom-call | tf_op jit(solution)/shard_map/pallas_call | solution.py:41
  174.8 2.2 reshape.78
  177.2 42.2 %all-gather.9.cloned.1.call-done = bf16[1536,2048]{1,0:T(8,128)(2,1)} async-done(((bf16[192,2048]{1,0:T(8,128)(2,1)}), bf16[1536,2048]{1,0:T(8,128)(2,1)}) %all-gather.9.cloned.1.call-update) | async-done | bytes 6291472 | tf_op jit(solution)/shard_map/all_gather | solution.py:149
  219.4 6.0 %fusion.13 = f32[1536,176]{0,1:T(8,128)} fusion(bf16[1536,2048]{1,0:T(8,128)(2,1)} %all-gather.9.cloned.1.call-done, bf16[1,2048,176]{1,2,0:T(8,128)(2,1)S(1)} %copy-done.8), kind=kOutput, calls=%fused_computation.25 | convolution fusion | flops 1107296256 | bytes 8093696 | tf_op jit(solution)/shard_map/dot_general | solution.py:153
  225.4 10.0 %convolution_convert_fusion = bf16[1536,2048]{1,0:T(8,128)(2,1)} fusion(bf16[1536,2048]{1,0:T(8,128)(2,1)} %all-gather.9.cloned.1.call-done, f32[1536,176]{0,1:T(8,128)} %fusion.13, bf16[1,176,2048]{2,1,0:T(8,128)(2,1)} %param.25, bf16[1,2048,176]{1,2,0:T(8,128)(2,1)} %param.24), kind=kOutput, calls=%fused_computation.2 | convolution fusion | flops 2219360256 | bytes 15106048 | tf_op jit(solution)/shard_map/dot_general | solution.py:156
  235.5 3.8 %fusion.51 = f32[512,352]{0,1:T(8,128)} fusion(bf16[512,2048]{1,0:T(8,128)(2,1)} %all-gather.7.cloned.1.call-done, bf16[2048,352]{0,1:T(8,128)(2,1)} %param.20), kind=kOutput, calls=%fused_computation.91 | convolution fusion | flops 738197504 | bytes 4259840 | tf_op jit(solution)/shard_map/dot_general | solution.py:124
  239.3 40.4 %reduce-scatter.6.cloned.1.call-done = bf16[192,2048]{1,0:T(8,128)(2,1)} async-done(((bf16[1536,2048]{1,0:T(8,128)(2,1)}), bf16[192,2048]{1,0:T(8,128)(2,1)}) %reduce-scatter.6.cloned.1.call-update) | async-done | bytes 786448 | tf_op jit(solution)/shard_map/reduce_scatter | solution.py:157
  279.7 2.2 reshape.79.x_ref
  281.9 31.2 %shard_map.138 = bf16[32,6,2048]{2,1,0:T(8,128)(2,1)} custom-call(bf16[32,6,2048]{2,1,0:T(8,128)(2,1)} %reshape.79.x_ref), custom_call_target="tpu_custom_call" | custom-call | tf_op jit(solution)/shard_map/pallas_call | solution.py:41
  313.1 1.4 reshape.80
  314.5 2.7 fusion.25
  317.2 2.7 fusion.34
  319.9 8.7 %add_convert_fusion = bf16[512,2048]{1,0:T(8,128)(2,1)} fusion(f32[512,2048]{1,0:T(8,128)} %fusion.34, f32[512,2048]{1,0:T(8,128)} %fusion.25, bf16[352,2048]{1,0:T(8,128)(2,1)} %param.22, bf16[512,2048]{1,0:T(8,128)(2,1)} %all-gather.7.cloned.1.call-done, bf16[2048,352]{0,1:T(8,128)(2,1)} %param.21, f32[512,352]{0,1:T(8,128)} %fusion.51), kind=kOutput, calls=%fused_computation.3 | convolution fusion | flops 1480622080 | bytes 16187392 | tf_op jit(solution)/shard_map/dot_general | solution.py:169
  328.6 34.1 %reduce-scatter.8.cloned.1.call-done = bf16[64,2048]{1,0:T(8,128)(2,1)} async-done(((bf16[512,2048]{1,0:T(8,128)(2,1)}), bf16[64,2048]{1,0:T(8,128)(2,1)}) %reduce-scatter.8.cloned.1.call-update) | async-done | bytes 262160 | tf_op jit(solution)/shard_map/reduce_scatter | solution.py:168
  362.7 1.7 add_convert_fusion.1
  (62 shorter events, 12.0 us)
Async XLA Ops:
  6.5 62.3 %copy-start = (bf16[4608,256]{1,0:T(8,128)(2,1)S(1)}, bf16[4608,256]{1,0:T(8,128)(2,1)}, u32[]{:S(2)}) copy-start(bf16[4608,256]{1,0:T(8,128)(2,1)} %param.17) | copy-start | bytes 7077892
  6.5 3.8 %copy-start.1 = (bf16[32,4608]{1,0:T(8,128)(2,1)S(1)}, bf16[32,4608]{1,0:T(8,128)(2,1)}, u32[]{:S(2)}) copy-start(bf16[32,4608]{1,0:T(8,128)(2,1)} %param.15) | copy-start | bytes 884740
  6.5 62.3 %all-gather.5.cloned.1.call-start = ((), (), s32[]{:S(2)}) async-start(), calls=%async_computation.3 | async-start | bytes 2654208 | tf_op jit(solution)/shard_map/all_gather | solution.py:101
  39.1 66.7 %copy-start.4 = (bf16[64,2048]{1,0:T(8,128)(2,1)S(1)}, bf16[64,2048]{1,0:T(8,128)(2,1)}, u32[]{:S(2)}) copy-start(bf16[64,2048]{1,0:T(8,128)(2,1)} %param.14) | copy-start | bytes 786436
  39.1 68.8 %copy-start.5 = (f32[2048]{0:T(1024)S(1)}, f32[2048]{0:T(1024)}, u32[]{:S(2)}) copy-start(f32[2048]{0:T(1024)} %param.19) | copy-start | bytes 24580
  39.1 66.7 %reduce-scatter.4.cloned.1.call-start = ((), (), s32[]{:S(2)}) async-start(), calls=%async_computation.4 | async-start | bytes 1179648 | tf_op jit(solution)/shard_map/reduce_scatter | solution.py:106
  73.4 35.4 %copy-start.6 = (s32[64,2]{0,1:T(2,128)S(1)}, s32[64,2]{0,1:T(2,128)}, u32[]{:S(2)}) copy-start(s32[64,2]{0,1:T(2,128)} %param.27) | copy-start | bytes 1540
  73.4 35.4 %copy-start.7 = (s32[64,2]{0,1:T(2,128)S(1)}, s32[64,2]{0,1:T(2,128)}, u32[]{:S(2)}) copy-start(s32[64,2]{0,1:T(2,128)} %param.26) | copy-start | bytes 1540
  73.5 65.2 %all-gather.7.cloned.1.call-start = ((), (), s32[]{:S(2)}) async-start(), calls=%async_computation.5 | async-start | bytes 2359296 | tf_op jit(solution)/shard_map/all_gather | solution.py:116
  107.1 0.8 copy-start.2
  108.8 110.6 %all-gather.9.cloned.1.call-start = ((), (), s32[]{:S(2)}) async-start(), calls=%async_computation.6 | async-start | bytes 7077888 | tf_op jit(solution)/shard_map/all_gather | solution.py:149
  142.3 77.1 %copy-start.8 = (bf16[1,2048,176]{1,2,0:T(8,128)(2,1)S(1)}, bf16[1,2048,176]{1,2,0:T(8,128)(2,1)}, u32[]{:S(2)}) copy-start(bf16[1,2048,176]{1,2,0:T(8,128)(2,1)} %param.23) | copy-start | bytes 2162692
  177.0 102.7 %reduce-scatter.6.cloned.1.call-start = ((), (), s32[]{:S(2)}) async-start(), calls=%async_computation.7 | async-start | bytes 7077888 | tf_op jit(solution)/shard_map/reduce_scatter | solution.py:157
  235.4 127.3 %reduce-scatter.8.cloned.1.call-start = ((), (), s32[]{:S(2)}) async-start(), calls=%async_computation.8 | async-start | bytes 2359296 | tf_op jit(solution)/shard_map/reduce_scatter | solution.py:168
  328.6 34.1 %copy-start.3 = (f32[64,2048]{1,0:T(8,128)S(1)}, f32[64,2048]{1,0:T(8,128)}, u32[]{:S(2)}) copy-start(f32[64,2048]{1,0:T(8,128)} %copy-done.2) | copy-start | bytes 1572868
Sparse Core Ops, SparseCore 0:
  39.2 29.6 all-gather.4
  73.6 32.1 reduce-scatter.3
  108.9 29.7 all-gather.6
  177.1 42.2 all-gather.8
  235.6 44.1 reduce-scatter.5
  328.8 33.9 reduce-scatter.7

commit v3 on v2

--- a/solution.py
+++ b/solution.py
@@ -86,6 +86,9 @@
     peer = img_dev // n_data
     my_place = lax.axis_index("expert")
 
+    route_cols = jnp.concatenate([route_ids, route_wts // 256, route_wts % 256], axis=1)
+    route_cols = jnp.pad(route_cols, ((0, 0), (0, 128 - route_cols.shape[1])))
+
     dest_index = tile_pos // tok_dev // n_group
     order = jnp.argsort(dest_index, stable=True)
     offs_sorted = (tile_pos[order] % tok_dev).astype(bf16)
@@ -113,13 +116,14 @@
     embed_own = jnp.where(has_image, placed, text_embed.astype(f32))
     normed_own = normalize(embed_own, norm_gain)
 
-    normed = lax.all_gather(normed_own, "expert", axis=0, tiled=True)
-    routes = lax.all_gather(
-        jnp.concatenate([route_ids, route_wts], axis=1), "expert", axis=0, tiled=True
-    )
+    gathered = lax.all_gather(
+        jnp.concatenate([normed_own, route_cols.astype(bf16)], axis=1), "expert", axis=0, tiled=True
+    )
+    normed = gathered[:, :width_model]
+    routes = gathered[:, width_model:].astype(f32)
     top_count = route_ids.shape[1]
-    ids = routes[:, :top_count]
-    weights = routes[:, top_count:]
+    ids = routes[:, :top_count].astype(jnp.int32)
+    weights_f = routes[:, top_count : 2 * top_count] * 256.0 + routes[:, 2 * top_count : 3 * top_count]
 
     gate_s = jnp.dot(normed, shared_gate, preferred_element_type=f32)
     up_s = jnp.dot(normed, shared_up, preferred_element_type=f32)
@@ -159,7 +163,6 @@
         n_rows, width_model
     )
 
-    weights_f = weights.astype(f32)
     weights_n = weights_f / jnp.sum(weights_f, axis=1, keepdims=True)
     coef = jnp.sum(jnp.where(hit, weights_n[:, :, None], 0.0), axis=1)
     coef_hi = coef.astype(bf16)

time: 373 us -> 378 us (1.013)
  waiting for transfers between devices: 192 us -> 209 us
  blocking collectives: 14.2 us -> 0 us
    all_gather x1, waiting for transfers between devices: 13.4 us -> 29.8 us  [shards(): lax.all_gather(jnp.concatenate([normed_own, route_cols.astype(bf16)], axi...]
    all_gather x1 -> x0, blocking collectives: 14.2 us -> none  [shards(): lax.all_gather(jnp.concatenate([route_ids, route_wts], axis=1), 'expert',...]
  transfers between devices with their start and end apart: 6 -> 6, of which waited for: 6 -> 6; matrix products, arithmetic and copies ran while one was open for 2% -> 1% of each run, Pallas kernels for 0% -> 0%
where the time goes in v3:
time: 378 us; the launch traced here: 376 us
  waiting for transfers between devices  209 us (55%)
  Pallas kernels  88.4 us (23%)
  matrix products  42.6 us (11%)
  local copies, waits for them, and re-layouts  16.2 us (4%)
  between operations  13.7 us (4%)
  other arithmetic  5.59 us (1%)
    pallas_call x3, Pallas kernels, dp_all_to_all(): pl.pallas_call(kernel, out_shape=jax.ShapeDtypeStruct(x.shape, x.dtype),...  88.4 us
    all_gather x1, waiting for transfers between devices, shards(): lax.all_gather(arrived.reshape(n_rows, width_model), 'expert', axis=0, ti...  42.7 us
    reduce_scatter x1, waiting for transfers between devices, shards(): lax.psum_scatter(partial_out, 'expert', scatter_dimension=0, tiled=True)  40.4 us
    reduce_scatter x1, waiting for transfers between devices, shards(): lax.psum_scatter((jnp.dot(shared_hidden, shared_down, preferred_element_t...  34.1 us
    reduce_scatter x1, waiting for transfers between devices, shards(): lax.psum_scatter(partial_proj, 'expert', scatter_dimension=0, tiled=True)  31.8 us
    all_gather x1, waiting for transfers between devices, shards(): lax.all_gather(jnp.concatenate([normed_own, route_cols.astype(bf16)], axi...  29.8 us
    all_gather x1, waiting for transfers between devices, shards(): feats = lax.all_gather(moved_feats, 'expert', axis=0, tiled=True)  29.7 us
    dot_general x1, matrix products, shards(): jnp.dot(hidden_e, expert_down[0], preferred_element_type=f32).astype(bf16)  10 us
  transfers between devices with their start and end apart: 6, of which 6 were waited for; matrix products, arithmetic and copies ran while one was open for 1% of the time, Pallas kernels for 0%

profile of v3, /device:TPU:1, one launch (start us, length us, event | category | flops | bytes accessed | tf_op | source)
XLA Modules:
  0.0 375.6 jit_solution(15831402378345856949)
XLA Ops:
  7.4 1.6 sort.17
  9.0 1.4 gather_fusion.1
  10.3 2.0 gather_fusion
  13.8 24.7 %shard_map.136 = bf16[32,1,4736]{2,1,0:T(2,128)(2,1)} custom-call(bf16[32,1,4736]{2,1,0:T(2,128)(2,1)} %copy.50.x_ref), custom_call_target="tpu_custom_call" | custom-call | tf_op jit(solution)/shard_map/pallas_call | solution.py:41
  40.5 29.7 %all-gather.4.cloned.1.call-done = bf16[256,4608]{1,0:T(8,128)(2,1)} async-done(((bf16[32,4608]{1,0:T(8,128)(2,1)}), bf16[256,4608]{1,0:T(8,128)(2,1)}) %all-gather.4.cloned.1.call-update) | async-done | bytes 2359312 | tf_op jit(solution)/shard_map/all_gather | solution.py:104
  70.1 4.6 %convolution_convert_fusion.1 = bf16[256,2048]{1,0:T(8,128)(2,1)} fusion(bf16[256,2048]{1,0:T(8,128)(2,1)} %param.18, bf16[256,4608]{1,0:T(8,128)(2,1)} %all-gather.4.cloned.1.call-done, bf16[4608,256]{1,0:T(8,128)(2,1)S(1)} %copy-done), kind=kOutput, calls=%fused_computation.7 | convolution fusion | flops 873529344 | bytes 6815744 | tf_op jit(solution)/shard_map/dot_general | solution.py:108
  75.2 31.8 %reduce-scatter.6.cloned.1.call-done = bf16[32,2048]{1,0:T(8,128)(2,1)} async-done(((bf16[256,2048]{1,0:T(8,128)(2,1)}), bf16[32,2048]{1,0:T(8,128)(2,1)}) %reduce-scatter.6.cloned.1.call-update) | async-done | bytes 131088 | tf_op jit(solution)/shard_map/reduce_scatter | solution.py:109
  110.2 29.8 %all-gather.6.cloned.1.call-done = bf16[512,2176]{1,0:T(8,128)(2,1)} async-done(((bf16[64,2176]{1,0:T(8,128)(2,1)}), bf16[512,2176]{1,0:T(8,128)(2,1)}) %all-gather.6.cloned.1.call-update) | async-done | bytes 2228240 | tf_op jit(solution)/shard_map/all_gather | solution.py:119
  142.5 2.2 convolution_convert_fusion.2
  146.0 32.5 %shard_map.137 = bf16[32,6,2048]{2,1,0:T(8,128)(2,1)} custom-call(bf16[32,6,2048]{2,1,0:T(8,128)(2,1)} %reshape.77.x_ref), custom_call_target="tpu_custom_call" | custom-call | tf_op jit(solution)/shard_map/pallas_call | solution.py:41
  178.5 2.2 reshape.78
  181.0 42.7 %all-gather.8.cloned.1.call-done = bf16[1536,2048]{1,0:T(8,128)(2,1)} async-done(((bf16[192,2048]{1,0:T(8,128)(2,1)}), bf16[1536,2048]{1,0:T(8,128)(2,1)}) %all-gather.8.cloned.1.call-update) | async-done | bytes 6291472 | tf_op jit(solution)/shard_map/all_gather | solution.py:153
  223.7 6.0 %fusion.23 = f32[1536,176]{0,1:T(8,128)} fusion(bf16[1536,2048]{1,0:T(8,128)(2,1)} %all-gather.8.cloned.1.call-done, bf16[1,2048,176]{1,2,0:T(8,128)(2,1)S(1)} %copy-done.6), kind=kOutput, calls=%fused_computation.30 | convolution fusion | flops 1107296256 | bytes 8093696 | tf_op jit(solution)/shard_map/dot_general | solution.py:157
  229.7 10.0 %convolution_convert_fusion = bf16[1536,2048]{1,0:T(8,128)(2,1)} fusion(bf16[1536,2048]{1,0:T(8,128)(2,1)} %all-gather.8.cloned.1.call-done, f32[1536,176]{0,1:T(8,128)} %fusion.23, bf16[1,176,2048]{2,1,0:T(8,128)(2,1)} %param.25, bf16[1,2048,176]{1,2,0:T(8,128)(2,1)} %param.24), kind=kOutput, calls=%fused_computation.2 | convolution fusion | flops 2219360256 | bytes 15106048 | tf_op jit(solution)/shard_map/dot_general | solution.py:160
  239.8 3.8 %fusion.5 = f32[512,352]{0,1:T(8,128)} fusion(bf16[2048,352]{0,1:T(8,128)(2,1)} %param.20, bf16[512,2176]{1,0:T(8,128)(2,1)} %all-gather.6.cloned.1.call-done), kind=kOutput, calls=%fused_computation.14 | convolution fusion | flops 738197504 | bytes 4259840 | tf_op jit(solution)/shard_map/dot_general | solution.py:128
  243.6 40.4 %reduce-scatter.8.cloned.1.call-done = bf16[192,2048]{1,0:T(8,128)(2,1)} async-done(((bf16[1536,2048]{1,0:T(8,128)(2,1)}), bf16[192,2048]{1,0:T(8,128)(2,1)}) %reduce-scatter.8.cloned.1.call-update) | async-done | bytes 786448 | tf_op jit(solution)/shard_map/reduce_scatter | solution.py:161
  284.0 2.2 reshape.79.x_ref
  286.2 31.2 %shard_map.138 = bf16[32,6,2048]{2,1,0:T(8,128)(2,1)} custom-call(bf16[32,6,2048]{2,1,0:T(8,128)(2,1)} %reshape.79.x_ref), custom_call_target="tpu_custom_call" | custom-call | tf_op jit(solution)/shard_map/pallas_call | solution.py:41
  317.4 1.4 reshape.80
  318.8 2.7 fusion.42
  321.6 2.7 fusion.51
  324.2 8.7 %add_convert_fusion = bf16[512,2048]{1,0:T(8,128)(2,1)} fusion(f32[512,2048]{1,0:T(8,128)} %fusion.51, f32[512,2048]{1,0:T(8,128)} %fusion.42, bf16[352,2048]{1,0:T(8,128)(2,1)} %param.22, bf16[2048,352]{0,1:T(8,128)(2,1)} %param.21, bf16[512,2176]{1,0:T(8,128)(2,1)} %all-gather.6.cloned.1.call-done, f32[512,352]{0,1:T(8,128)} %fusion.5), kind=kOutput, calls=%fused_computation.3 | convolution fusion | flops 1480622080 | bytes 16187392 | tf_op jit(solution)/shard_map/dot_general | solution.py:172
  333.0 34.1 %reduce-scatter.10.cloned.1.call-done = bf16[64,2048]{1,0:T(8,128)(2,1)} async-done(((bf16[512,2048]{1,0:T(8,128)(2,1)}), bf16[64,2048]{1,0:T(8,128)(2,1)}) %reduce-scatter.10.cloned.1.call-update) | async-done | bytes 262160 | tf_op jit(solution)/shard_map/reduce_scatter | solution.py:171
  367.0 1.7 add_convert_fusion.1
  (63 shorter events, 11.8 us)
Async XLA Ops:
  6.5 63.6 %copy-start = (bf16[4608,256]{1,0:T(8,128)(2,1)S(1)}, bf16[4608,256]{1,0:T(8,128)(2,1)}, u32[]{:S(2)}) copy-start(bf16[4608,256]{1,0:T(8,128)(2,1)} %param.17) | copy-start | bytes 7077892
  6.5 63.6 %all-gather.4.cloned.1.call-start = ((), (), s32[]{:S(2)}) async-start(), calls=%async_computation.3 | async-start | bytes 2654208 | tf_op jit(solution)/shard_map/all_gather | solution.py:104
  40.4 34.4 %copy-start.7 = (s32[64,2]{0,1:T(2,128)S(1)}, s32[64,2]{0,1:T(2,128)}, u32[]{:S(2)}) copy-start(s32[64,2]{0,1:T(2,128)} %param.26) | copy-start | bytes 1540
  40.4 34.4 %copy-start.5 = (s32[64,2]{0,1:T(2,128)S(1)}, s32[64,2]{0,1:T(2,128)}, u32[]{:S(2)}) copy-start(s32[64,2]{0,1:T(2,128)} %param.27) | copy-start | bytes 1540
  40.4 66.7 %copy-start.3 = (bf16[64,2048]{1,0:T(8,128)(2,1)S(1)}, bf16[64,2048]{1,0:T(8,128)(2,1)}, u32[]{:S(2)}) copy-start(bf16[64,2048]{1,0:T(8,128)(2,1)} %param.14) | copy-start | bytes 786436
  40.4 68.8 %copy-start.4 = (f32[2048]{0:T(1024)S(1)}, f32[2048]{0:T(1024)}, u32[]{:S(2)}) copy-start(f32[2048]{0:T(1024)} %param.19) | copy-start | bytes 24580
  40.4 66.6 %reduce-scatter.6.cloned.1.call-start = ((), (), s32[]{:S(2)}) async-start(), calls=%async_computation.4 | async-start | bytes 1179648 | tf_op jit(solution)/shard_map/reduce_scatter | solution.py:109
  74.7 65.2 %all-gather.6.cloned.1.call-start = ((), (), s32[]{:S(2)}) async-start(), calls=%async_computation.5 | async-start | bytes 2506752 | tf_op jit(solution)/shard_map/all_gather | solution.py:119
  108.4 0.8 copy-start.1
  110.1 113.6 %all-gather.8.cloned.1.call-start = ((), (), s32[]{:S(2)}) async-start(), calls=%async_computation.6 | async-start | bytes 7077888 | tf_op jit(solution)/shard_map/all_gather | solution.py:153
  146.0 77.7 %copy-start.6 = (bf16[1,2048,176]{1,2,0:T(8,128)(2,1)S(1)}, bf16[1,2048,176]{1,2,0:T(8,128)(2,1)}, u32[]{:S(2)}) copy-start(bf16[1,2048,176]{1,2,0:T(8,128)(2,1)} %param.23) | copy-start | bytes 2162692
  180.7 103.3 %reduce-scatter.8.cloned.1.call-start = ((), (), s32[]{:S(2)}) async-start(), calls=%async_computation.7 | async-start | bytes 7077888 | tf_op jit(solution)/shard_map/reduce_scatter | solution.py:161
  239.8 127.3 %reduce-scatter.10.cloned.1.call-start = ((), (), s32[]{:S(2)}) async-start(), calls=%async_computation.8 | async-start | bytes 2359296 | tf_op jit(solution)/shard_map/reduce_scatter | solution.py:171
  332.9 34.1 %copy-start.2 = (f32[64,2048]{1,0:T(8,128)S(1)}, f32[64,2048]{1,0:T(8,128)}, u32[]{:S(2)}) copy-start(f32[64,2048]{1,0:T(8,128)} %copy-done.1) | copy-start | bytes 1572868
Sparse Core Ops, SparseCore 0:
  40.5 29.6 all-gather.3
  74.9 32.1 reduce-scatter.5
  110.2 29.6 all-gather.5
  180.9 42.8 all-gather.7
  239.9 44.1 reduce-scatter.7
  333.1 33.9 reduce-scatter.9

commit v4 on v3

--- a/solution.py
+++ b/solution.py
@@ -47,6 +47,51 @@
             pltpu.SemaphoreType.DMA((n,)),
             pltpu.SemaphoreType.DMA((n,)),
             pltpu.SemaphoreType.DMA,
+        ],
+        compiler_params=pltpu.CompilerParams(collective_id=collective_id, has_side_effects=True),
+    )(x)
+
+
+def expert_reduce_scatter(x, collective_id, out_dtype):
+    n, rows, cols = x.shape
+    mesh_ids = pl.DeviceIdType.MESH
+
+    def kernel(x_ref, o_ref, buf, send_sem, recv_sem):
+        me = lax.axis_index("expert")
+        row = lax.axis_index("dp")
+        barrier = pltpu.get_barrier_semaphore()
+        for k in range(1, n):
+            pl.semaphore_signal(
+                barrier, inc=1, device_id=(row, lax.rem(me + k, n)), device_id_type=mesh_ids
+            )
+        pl.semaphore_wait(barrier, n - 1)
+        copies = []
+        for k in range(1, n):
+            copy = pltpu.make_async_remote_copy(
+                src_ref=x_ref.at[lax.rem(me + k, n)],
+                dst_ref=buf.at[k],
+                send_sem=send_sem.at[k],
+                recv_sem=recv_sem.at[k],
+                device_id=(row, lax.rem(me + k, n)),
+                device_id_type=mesh_ids,
+            )
+            copy.start()
+            copies.append(copy)
+        acc = x_ref[me].astype(jnp.float32)
+        for k, copy in enumerate(copies, 1):
+            copy.wait()
+            acc = acc + buf[k].astype(jnp.float32)
+        o_ref[...] = acc.astype(o_ref.dtype)
+
+    return pl.pallas_call(
+        kernel,
+        out_shape=jax.ShapeDtypeStruct((rows, cols), out_dtype),
+        in_specs=[pl.BlockSpec(memory_space=pltpu.VMEM)],
+        out_specs=pl.BlockSpec(memory_space=pltpu.VMEM),
+        scratch_shapes=[
+            pltpu.VMEM((n, rows, cols), x.dtype),
+            pltpu.SemaphoreType.DMA((n,)),
+            pltpu.SemaphoreType.DMA((n,)),
         ],
         compiler_params=pltpu.CompilerParams(collective_id=collective_id, has_side_effects=True),
     )(x)
@@ -106,7 +151,9 @@
         jnp.dot(feats, proj_in, preferred_element_type=f32), approximate=True
     ).astype(bf16)
     partial_proj = jnp.dot(vis_hidden, proj_out, preferred_element_type=f32).astype(bf16)
-    projected = lax.psum_scatter(partial_proj, "expert", scatter_dimension=0, tiled=True)
+    projected = expert_reduce_scatter(
+        partial_proj.reshape(n_group, img_dev, width_model), 3, bf16
+    )
 
     place = (
         moved_offs[None, :] == jnp.arange(tok_dev, dtype=jnp.int32)[:, None]
@@ -168,12 +215,13 @@
     coef_hi = coef.astype(bf16)
     coef_lo = (coef - coef_hi.astype(f32)).astype(bf16)
     combined = select_dot(coef_hi, returned) + select_dot(coef_lo, returned)
-    total = lax.psum_scatter(
-        (jnp.dot(shared_hidden, shared_down, preferred_element_type=f32) + combined).astype(bf16),
-        "expert",
-        scatter_dimension=0,
-        tiled=True,
-    ).astype(f32)
+    total = expert_reduce_scatter(
+        (jnp.dot(shared_hidden, shared_down, preferred_element_type=f32) + combined)
+        .astype(bf16)
+        .reshape(n_group, tok_dev, width_model),
+        4,
+        f32,
+    )
     return (embed_own + total).astype(bf16)
 
 

time: 378 us -> 358 us (0.947)
  waiting for transfers between devices: 209 us -> 141 us
  Pallas kernels: 88.4 us -> 138 us
    reduce_scatter x2 -> x0, waiting for transfers between devices: 65.9 us -> none  [the longest x1 34.1 us: shards(): lax.psum_scatter((jnp.dot(shared_hidden, shared_down, preferred_element_t...]
    pallas_call x0 -> x2, Pallas kernels: none -> 49.3 us  [expert_reduce_scatter(): pl.pallas_call(kernel, out_shape=jax.ShapeDtypeStruct((rows, cols), out_d...]
  transfers between devices with their start and end apart: 6 -> 4, of which waited for: 6 -> 4; matrix products, arithmetic and copies ran while one was open for 1% -> 1% of each run, Pallas kernels for 0% -> 0%
where the time goes in v4:
time: 358 us
  waiting for transfers between devices  141 us (39%)
  Pallas kernels  138 us (39%)
  matrix products  42.6 us (12%)
  local copies, waits for them, and re-layouts  15.2 us (4%)
  between operations  13.4 us (4%)
  other arithmetic  7.34 us (2%)
    pallas_call x3, Pallas kernels, dp_all_to_all(): pl.pallas_call(kernel, out_shape=jax.ShapeDtypeStruct(x.shape, x.dtype),...  88.4 us
    pallas_call x2, Pallas kernels, expert_reduce_scatter(): pl.pallas_call(kernel, out_shape=jax.ShapeDtypeStruct((rows, cols), out_d...  49.3 us
    all_gather x1, waiting for transfers between devices, shards(): lax.all_gather(arrived.reshape(n_rows, width_model), 'expert', axis=0, ti...  42.7 us
    reduce_scatter x1, waiting for transfers between devices, shards(): lax.psum_scatter(partial_out, 'expert', scatter_dimension=0, tiled=True)  40.5 us
    all_gather x1, waiting for transfers between devices, shards(): feats = lax.all_gather(moved_feats, 'expert', axis=0, tiled=True)  29.3 us
    all_gather x1, waiting for transfers between devices, shards(): lax.all_gather(jnp.concatenate([normed_own, route_cols.astype(bf16)], axi...  28.5 us
    dot_general x1, matrix products, shards(): jnp.dot(hidden_e, expert_down[0], preferred_element_type=f32).astype(bf16)  10 us
    dot_general x5, matrix products, select_dot(): return jnp.dot(sel, rows, preferred_element_type=jnp.float32)  9.47 us
  transfers between devices with their start and end apart: 4, of which 4 were waited for; matrix products, arithmetic and copies ran while one was open for 1% of the time, Pallas kernels for 0%

profile of v4, /device:TPU:1, one launch (start us, length us, event | category | flops | bytes accessed | tf_op | source)
XLA Modules:
  0.0 357.6 jit_solution(1153120413213887946)
XLA Ops:
  7.4 1.6 sort.17
  10.3 2.0 gather_fusion
  13.8 24.7 %shard_map.136 = bf16[32,1,4736]{2,1,0:T(2,128)(2,1)} custom-call(bf16[32,1,4736]{2,1,0:T(2,128)(2,1)} %copy.38.x_ref), custom_call_target="tpu_custom_call" | custom-call | tf_op jit(solution)/shard_map/pallas_call | solution.py:41
  40.8 29.3 %all-gather.4.cloned.1.call-done = bf16[256,4608]{1,0:T(8,128)(2,1)} async-done(((bf16[32,4608]{1,0:T(8,128)(2,1)}), bf16[256,4608]{1,0:T(8,128)(2,1)}) %all-gather.4.cloned.1.call-update) | async-done | bytes 2359312 | tf_op jit(solution)/shard_map/all_gather | solution.py:149
  70.1 4.6 %convolution_convert_fusion.1 = bf16[256,2048]{1,0:T(8,128)(2,1)} fusion(bf16[256,2048]{1,0:T(8,128)(2,1)} %param.18, bf16[256,4608]{1,0:T(8,128)(2,1)} %all-gather.4.cloned.1.call-done, bf16[4608,256]{1,0:T(8,128)(2,1)S(1)} %copy-done), kind=kOutput, calls=%fused_computation.7 | convolution fusion | flops 873529344 | bytes 6815744 | tf_op jit(solution)/shard_map/dot_general | solution.py:153
  74.7 17.4 %shard_map.137 = bf16[32,2048]{1,0:T(8,128)(2,1)} custom-call(bf16[8,32,2048]{2,1,0:T(8,128)(2,1)} %bitcast.30), custom_call_target="tpu_custom_call" | custom-call | tf_op jit(solution)/shard_map/pallas_call | solution.py:86
  92.1 1.4 multiply_reduce_fusion
  95.3 28.5 %all-gather.6.cloned.1.call-done = bf16[512,2176]{1,0:T(8,128)(2,1)} async-done(((bf16[64,2176]{1,0:T(8,128)(2,1)}), bf16[512,2176]{1,0:T(8,128)(2,1)}) %all-gather.6.cloned.1.call-update) | async-done | bytes 2228240 | tf_op jit(solution)/shard_map/all_gather | solution.py:166
  126.9 2.2 convolution_convert_fusion.2
  130.4 32.5 %shard_map.138 = bf16[32,6,2048]{2,1,0:T(8,128)(2,1)} custom-call(bf16[32,6,2048]{2,1,0:T(8,128)(2,1)} %reshape.84.x_ref), custom_call_target="tpu_custom_call" | custom-call | tf_op jit(solution)/shard_map/pallas_call | solution.py:41
  162.9 2.2 reshape.85
  165.4 42.7 %all-gather.8.cloned.1.call-done = bf16[1536,2048]{1,0:T(8,128)(2,1)} async-done(((bf16[192,2048]{1,0:T(8,128)(2,1)}), bf16[1536,2048]{1,0:T(8,128)(2,1)}) %all-gather.8.cloned.1.call-update) | async-done | bytes 6291472 | tf_op jit(solution)/shard_map/all_gather | solution.py:200
  208.1 6.0 %fusion.23 = f32[1536,176]{0,1:T(8,128)} fusion(bf16[1536,2048]{1,0:T(8,128)(2,1)} %all-gather.8.cloned.1.call-done, bf16[1,2048,176]{1,2,0:T(8,128)(2,1)S(1)} %copy-done.6), kind=kOutput, calls=%fused_computation.30 | convolution fusion | flops 1107296256 | bytes 8093696 | tf_op jit(solution)/shard_map/dot_general | solution.py:204
  214.1 10.0 %convolution_convert_fusion = bf16[1536,2048]{1,0:T(8,128)(2,1)} fusion(bf16[1536,2048]{1,0:T(8,128)(2,1)} %all-gather.8.cloned.1.call-done, f32[1536,176]{0,1:T(8,128)} %fusion.23, bf16[1,176,2048]{2,1,0:T(8,128)(2,1)} %param.25, bf16[1,2048,176]{1,2,0:T(8,128)(2,1)} %param.24), kind=kOutput, calls=%fused_computation.2 | convolution fusion | flops 2219360256 | bytes 15106048 | tf_op jit(solution)/shard_map/dot_general | solution.py:207
  224.2 3.8 %fusion.5 = f32[512,352]{0,1:T(8,128)} fusion(bf16[2048,352]{0,1:T(8,128)(2,1)} %param.20, bf16[512,2176]{1,0:T(8,128)(2,1)} %all-gather.6.cloned.1.call-done), kind=kOutput, calls=%fused_computation.14 | convolution fusion | flops 738197504 | bytes 4259840 | tf_op jit(solution)/shard_map/dot_general | solution.py:175
  228.0 40.5 %reduce-scatter.2.cloned.1.call-done = bf16[192,2048]{1,0:T(8,128)(2,1)} async-done(((bf16[1536,2048]{1,0:T(8,128)(2,1)}), bf16[192,2048]{1,0:T(8,128)(2,1)}) %reduce-scatter.2.cloned.1.call-update) | async-done | bytes 786448 | tf_op jit(solution)/shard_map/reduce_scatter | solution.py:208
  268.4 2.2 reshape.86.x_ref
  270.6 31.2 %shard_map.139 = bf16[32,6,2048]{2,1,0:T(8,128)(2,1)} custom-call(bf16[32,6,2048]{2,1,0:T(8,128)(2,1)} %reshape.86.x_ref), custom_call_target="tpu_custom_call" | custom-call | tf_op jit(solution)/shard_map/pallas_call | solution.py:41
  301.8 1.4 reshape.87
  303.2 2.7 fusion.44
  306.0 2.7 fusion.53
  308.6 8.7 %add_convert_fusion = bf16[512,2048]{1,0:T(8,128)(2,1)} fusion(f32[512,2048]{1,0:T(8,128)} %fusion.53, f32[512,2048]{1,0:T(8,128)} %fusion.44, bf16[352,2048]{1,0:T(8,128)(2,1)} %param.22, bf16[2048,352]{0,1:T(8,128)(2,1)} %param.21, bf16[512,2176]{1,0:T(8,128)(2,1)} %all-gather.6.cloned.1.call-done, f32[512,352]{0,1:T(8,128)} %fusion.5), kind=kOutput, calls=%fused_computation.3 | convolution fusion | flops 1480622080 | bytes 16187392 | tf_op jit(solution)/shard_map/dot_general | solution.py:219
  317.3 31.9 %shard_map.140 = f32[64,2048]{1,0:T(8,128)} custom-call(bf16[8,64,2048]{2,1,0:T(8,128)(2,1)} %bitcast.29), custom_call_target="tpu_custom_call" | custom-call | tf_op jit(solution)/shard_map/pallas_call | solution.py:86
  349.2 1.8 add_convert_fusion.1
  (57 shorter events, 12.2 us)
Async XLA Ops:
  6.5 63.6 %copy-start = (bf16[4608,256]{1,0:T(8,128)(2,1)S(1)}, bf16[4608,256]{1,0:T(8,128)(2,1)}, u32[]{:S(2)}) copy-start(bf16[4608,256]{1,0:T(8,128)(2,1)} %param.17) | copy-start | bytes 7077892
  6.5 63.6 %all-gather.4.cloned.1.call-start = ((), (), s32[]{:S(2)}) async-start(), calls=%async_computation.1 | async-start | bytes 2654208 | tf_op jit(solution)/shard_map/all_gather | solution.py:149
  12.5 28.0 %copy-start.7 = (s32[64,2]{0,1:T(2,128)S(1)}, s32[64,2]{0,1:T(2,128)}, u32[]{:S(2)}) copy-start(s32[64,2]{0,1:T(2,128)} %param.26) | copy-start | bytes 1540
  12.5 28.0 %copy-start.5 = (s32[64,2]{0,1:T(2,128)S(1)}, s32[64,2]{0,1:T(2,128)}, u32[]{:S(2)}) copy-start(s32[64,2]{0,1:T(2,128)} %param.27) | copy-start | bytes 1540
  40.4 83.4 %all-gather.6.cloned.1.call-start = ((), (), s32[]{:S(2)}) async-start(), calls=%async_computation.2 | async-start | bytes 2506752 | tf_op jit(solution)/shard_map/all_gather | solution.py:166
  40.8 51.3 %copy-start.3 = (bf16[64,2048]{1,0:T(8,128)(2,1)S(1)}, bf16[64,2048]{1,0:T(8,128)(2,1)}, u32[]{:S(2)}) copy-start(bf16[64,2048]{1,0:T(8,128)(2,1)} %param.14) | copy-start | bytes 786436
  40.8 53.5 %copy-start.4 = (f32[2048]{0:T(1024)S(1)}, f32[2048]{0:T(1024)}, u32[]{:S(2)}) copy-start(f32[2048]{0:T(1024)} %param.19) | copy-start | bytes 24580
  93.5 0.8 copy-start.1
  95.2 112.9 %all-gather.8.cloned.1.call-start = ((), (), s32[]{:S(2)}) async-start(), calls=%async_computation.3 | async-start | bytes 7077888 | tf_op jit(solution)/shard_map/all_gather | solution.py:200
  130.4 77.7 %copy-start.6 = (bf16[1,2048,176]{1,2,0:T(8,128)(2,1)S(1)}, bf16[1,2048,176]{1,2,0:T(8,128)(2,1)}, u32[]{:S(2)}) copy-start(bf16[1,2048,176]{1,2,0:T(8,128)(2,1)} %param.23) | copy-start | bytes 2162692
  165.2 103.3 %reduce-scatter.2.cloned.1.call-start = ((), (), s32[]{:S(2)}) async-start(), calls=%async_computation.4 | async-start | bytes 7077888 | tf_op jit(solution)/shard_map/reduce_scatter | solution.py:208
  317.3 31.9 %copy-start.2 = (f32[64,2048]{1,0:T(8,128)S(1)}, f32[64,2048]{1,0:T(8,128)}, u32[]{:S(2)}) copy-start(f32[64,2048]{1,0:T(8,128)} %copy-done.1) | copy-start | bytes 1572868
Sparse Core Ops, SparseCore 0:
  40.5 29.6 all-gather.3
  95.3 28.3 all-gather.5
  165.3 42.7 all-gather.7
  224.3 44.1 reduce-scatter.1

commit v5 on v4

--- a/solution.py
+++ b/solution.py
@@ -54,33 +54,54 @@
 
 def expert_reduce_scatter(x, collective_id, out_dtype):
     n, rows, cols = x.shape
+    chips = n // 2
     mesh_ids = pl.DeviceIdType.MESH
 
-    def kernel(x_ref, o_ref, buf, send_sem, recv_sem):
+    def kernel(x_ref, o_ref, pair_buf, part, far_buf, send1, recv1, send2, recv2):
         me = lax.axis_index("expert")
         row = lax.axis_index("dp")
+        chip, core = me // 2, me % 2
+        sibling = chip * 2 + 1 - core
         barrier = pltpu.get_barrier_semaphore()
-        for k in range(1, n):
+        pl.semaphore_signal(barrier, inc=1, device_id=(row, sibling), device_id_type=mesh_ids)
+        for k in range(1, chips):
             pl.semaphore_signal(
-                barrier, inc=1, device_id=(row, lax.rem(me + k, n)), device_id_type=mesh_ids
-            )
-        pl.semaphore_wait(barrier, n - 1)
+                barrier,
+                inc=1,
+                device_id=(row, lax.rem(chip + k, chips) * 2 + core),
+                device_id_type=mesh_ids,
+            )
+        pl.semaphore_wait(barrier, chips)
+        first = pltpu.make_async_remote_copy(
+            src_ref=x_ref.at[:, 1 - core],
+            dst_ref=pair_buf,
+            send_sem=send1,
+            recv_sem=recv1,
+            device_id=(row, sibling),
+            device_id_type=mesh_ids,
+        )
+        first.start()
+        first.wait()
         copies = []
-        for k in range(1, n):
+        for k in range(1, chips):
+            dest = lax.rem(chip + k, chips)
+            part[k] = (
+                x_ref[dest, core].astype(jnp.float32) + pair_buf[dest].astype(jnp.float32)
+            ).astype(part.dtype)
             copy = pltpu.make_async_remote_copy(
-                src_ref=x_ref.at[lax.rem(me + k, n)],
-                dst_ref=buf.at[k],
-                send_sem=send_sem.at[k],
-                recv_sem=recv_sem.at[k],
-                device_id=(row, lax.rem(me + k, n)),
+                src_ref=part.at[k],
+                dst_ref=far_buf.at[k],
+                send_sem=send2.at[k],
+                recv_sem=recv2.at[k],
+                device_id=(row, dest * 2 + core),
                 device_id_type=mesh_ids,
             )
             copy.start()
             copies.append(copy)
-        acc = x_ref[me].astype(jnp.float32)
+        acc = x_ref[chip, core].astype(jnp.float32) + pair_buf[chip].astype(jnp.float32)
         for k, copy in enumerate(copies, 1):
             copy.wait()
-            acc = acc + buf[k].astype(jnp.float32)
+            acc = acc + far_buf[k].astype(jnp.float32)
         o_ref[...] = acc.astype(o_ref.dtype)
 
     return pl.pallas_call(
@@ -89,9 +110,93 @@
         in_specs=[pl.BlockSpec(memory_space=pltpu.VMEM)],
         out_specs=pl.BlockSpec(memory_space=pltpu.VMEM),
         scratch_shapes=[
-            pltpu.VMEM((n, rows, cols), x.dtype),
-            pltpu.SemaphoreType.DMA((n,)),
-            pltpu.SemaphoreType.DMA((n,)),
+            pltpu.VMEM((chips, rows, cols), x.dtype),
+            pltpu.VMEM((chips, rows, cols), x.dtype),
+            pltpu.VMEM((chips, rows, cols), x.dtype),
+            pltpu.SemaphoreType.DMA,
+            pltpu.SemaphoreType.DMA,
+            pltpu.SemaphoreType.DMA((chips,)),
+            pltpu.SemaphoreType.DMA((chips,)),
+        ],
+        compiler_params=pltpu.CompilerParams(collective_id=collective_id, has_side_effects=True),
+    )(x.reshape(chips, 2, rows, cols))
+
+
+def expert_all_gather(x, collective_id):
+    rows, cols = x.shape
+    n = lax.axis_size("expert")
+    chips = n // 2
+    mesh_ids = pl.DeviceIdType.MESH
+
+    def kernel(x_ref, o_ref, send0, recv0, send1, recv1, send2, recv2):
+        me = lax.axis_index("expert")
+        row = lax.axis_index("dp")
+        chip, core = me // 2, me % 2
+        sibling = chip * 2 + 1 - core
+        barrier = pltpu.get_barrier_semaphore()
+        pl.semaphore_signal(barrier, inc=1, device_id=(row, sibling), device_id_type=mesh_ids)
+        for k in range(1, chips):
+            pl.semaphore_signal(
+                barrier,
+                inc=1,
+                device_id=(row, lax.rem(chip + k, chips) * 2 + core),
+                device_id_type=mesh_ids,
+            )
+        pl.semaphore_wait(barrier, chips)
+        near = pltpu.make_async_remote_copy(
+            src_ref=x_ref,
+            dst_ref=o_ref.at[me],
+            send_sem=send0,
+            recv_sem=recv0,
+            device_id=(row, sibling),
+            device_id_type=mesh_ids,
+        )
+        near.start()
+        far = []
+        for k in range(1, chips):
+            copy = pltpu.make_async_remote_copy(
+                src_ref=x_ref,
+                dst_ref=o_ref.at[me],
+                send_sem=send1.at[k],
+                recv_sem=recv1.at[k],
+                device_id=(row, lax.rem(chip + k, chips) * 2 + core),
+                device_id_type=mesh_ids,
+            )
+            copy.start()
+            far.append(copy)
+        o_ref[me] = x_ref[...]
+        passed = []
+        for k, copy in enumerate(far, 1):
+            copy.wait_recv()
+            source = lax.rem(chip - k + chips, chips) * 2 + core
+            relay = pltpu.make_async_remote_copy(
+                src_ref=o_ref.at[source],
+                dst_ref=o_ref.at[source],
+                send_sem=send2.at[k],
+                recv_sem=recv2.at[k],
+                device_id=(row, sibling),
+                device_id_type=mesh_ids,
+            )
+            relay.start()
+            passed.append(relay)
+        near.wait()
+        for copy in far:
+            copy.wait_send()
+        for relay in passed:
+            relay.wait()
+
+    return pl.pallas_call(
+        kernel,
+        out_shape=jax.ShapeDtypeStruct((n, rows, cols), x.dtype),
+        in_specs=[pl.BlockSpec(memory_space=pltpu.VMEM)],
+        out_specs=pl.BlockSpec(memory_space=pltpu.VMEM),
+        scratch_shapes=[
+            pltpu.SemaphoreType.DMA,
+            pltpu.SemaphoreType.DMA,
+            pltpu.SemaphoreType.DMA((chips,)),
+            pltpu.SemaphoreType.DMA((chips,)),
+            pltpu.SemaphoreType.DMA((chips,)),
+            pltpu.SemaphoreType.DMA((chips,)),
         ],
         compiler_params=pltpu.CompilerParams(collective_id=collective_id, has_side_effects=True),
     )(x)
@@ -146,7 +251,7 @@
     moved_feats = moved[:, :width_vis]
     moved_offs = moved[:, width_vis].astype(jnp.int32)
 
-    feats = lax.all_gather(moved_feats, "expert", axis=0, tiled=True)
+    feats = expert_all_gather(moved_feats, 5).reshape(n_group * img_dev, width_vis)
     vis_hidden = jax.nn.gelu(
         jnp.dot(feats, proj_in, preferred_element_type=f32), approximate=True
     ).astype(bf16)
@@ -163,9 +268,9 @@
     embed_own = jnp.where(has_image, placed, text_embed.astype(f32))
     normed_own = normalize(embed_own, norm_gain)
 
-    gathered = lax.all_gather(
-        jnp.concatenate([normed_own, route_cols.astype(bf16)], axis=1), "expert", axis=0, tiled=True
-    )
+    gathered = expert_all_gather(
+        jnp.concatenate([normed_own, route_cols.astype(bf16)], axis=1), 6
+    ).reshape(n_group * tok_dev, width_model + route_cols.shape[1])
     normed = gathered[:, :width_model]
     routes = gathered[:, width_model:].astype(f32)
     top_count = route_ids.shape[1]
@@ -197,15 +302,15 @@
     pick = jnp.sum(hit.astype(f32), axis=1).astype(bf16)
     send = select_dot(pick.T, normed).astype(bf16).reshape(n_data, share, width_model)
     arrived = dp_all_to_all(send, 1)
-    slots = lax.all_gather(
-        arrived.reshape(n_rows, width_model), "expert", axis=0, tiled=True
+    slots = expert_all_gather(arrived.reshape(n_rows, width_model), 7).reshape(
+        n_group * n_rows, width_model
     )
 
     gate_e = jnp.dot(slots, expert_gate[0], preferred_element_type=f32)
     up_e = jnp.dot(slots, expert_up[0], preferred_element_type=f32)
     hidden_e = (jax.nn.silu(gate_e) * up_e).astype(bf16)
     partial_out = jnp.dot(hidden_e, expert_down[0], preferred_element_type=f32).astype(bf16)
-    summed = lax.psum_scatter(partial_out, "expert", scatter_dimension=0, tiled=True)
+    summed = expert_reduce_scatter(partial_out.reshape(n_group, n_rows, width_model), 8, bf16)
     returned = dp_all_to_all(summed.reshape(n_data, share, width_model), 2).reshape(
         n_rows, width_model
     )

time: 358 us -> 319 us (0.89)
  waiting for transfers between devices: 141 us -> 0 us
  Pallas kernels: 138 us -> 257 us
  between operations: 13.4 us -> 0.32 us
    all_gather x3 -> x0, waiting for transfers between devices: 101 us -> none  [the longest x1 42.7 us: shards(): lax.all_gather(arrived.reshape(n_rows, width_model), 'expert', axis=0, ti...]
    pallas_call x0 -> x3, Pallas kernels: none -> 89.1 us  [expert_all_gather(): pl.pallas_call(kernel, out_shape=jax.ShapeDtypeStruct((n, rows, cols), x....]
    reduce_scatter x1 -> x0, waiting for transfers between devices: 40.5 us -> none  [shards(): lax.psum_scatter(partial_out, 'expert', scatter_dimension=0, tiled=True)]
    pallas_call x2 -> x3, Pallas kernels: 49.3 us -> 83.4 us  [expert_reduce_scatter(): pl.pallas_call(kernel, out_shape=jax.ShapeDtypeStruct((rows, cols), out_d...]
    pallas_call x3, Pallas kernels: 88.4 us -> 84.6 us  [dp_all_to_all(): pl.pallas_call(kernel, out_shape=jax.ShapeDtypeStruct(x.shape, x.dtype),...]
  transfers between devices with their start and end apart: 4 -> 0, of which waited for: 4 -> 0; matrix products, arithmetic and copies ran while one was open for 1% -> 0% of each run, Pallas kernels for 0% -> 0%
where the time goes in v5:
time: 319 us
  Pallas kernels  257 us (81%)
  matrix products  39.3 us (12%)
  local copies, waits for them, and re-layouts  16.3 us (5%)
  other arithmetic  5.72 us (2%)
    pallas_call x3, Pallas kernels, expert_all_gather(): pl.pallas_call(kernel, out_shape=jax.ShapeDtypeStruct((n, rows, cols), x....  89.1 us
    pallas_call x3, Pallas kernels, dp_all_to_all(): pl.pallas_call(kernel, out_shape=jax.ShapeDtypeStruct(x.shape, x.dtype),...  84.6 us
    pallas_call x3, Pallas kernels, expert_reduce_scatter(): pl.pallas_call(kernel, out_shape=jax.ShapeDtypeStruct((rows, cols), out_d...  83.4 us
    dot_general x1, matrix products, shards(): jnp.dot(hidden_e, expert_down[0], preferred_element_type=f32).astype(bf16)  10 us
    dot_general x5, matrix products, select_dot(): return jnp.dot(sel, rows, preferred_element_type=jnp.float32)  9.59 us
    dot_general x1, matrix products, shards(): jnp.dot(shared_hidden, shared_down, preferred_element_type=f32) + combined  8.49 us

profile of v5, /device:TPU:1, one launch (start us, length us, event | category | flops | bytes accessed | tf_op | source)
XLA Modules:
  0.0 318.8 jit_solution(11712285468377421820)
XLA Ops:
  0.8 1.6 sort.17
  2.5 2.0 gather_fusion
  6.6 24.7 %shard_map.136 = bf16[32,1,4736]{2,1,0:T(2,128)(2,1)} custom-call(bf16[32,1,4736]{2,1,0:T(2,128)(2,1)} %copy.38.x_ref), custom_call_target="tpu_custom_call" | custom-call | tf_op jit(solution)/shard_map/pallas_call | solution.py:41
  33.5 23.4 %shard_map.137 = bf16[8,32,4608]{2,1,0:T(8,128)(2,1)} custom-call(bf16[32,4608]{1,0:T(8,128)(2,1)} %slice.33.x_ref), custom_call_target="tpu_custom_call" | custom-call | tf_op jit(solution)/shard_map/pallas_call | solution.py:188
  56.9 4.3 %convolution_convert_fusion.1 = bf16[256,2048]{1,0:T(8,128)(2,1)} fusion(bf16[256,2048]{1,0:T(8,128)(2,1)S(1)} %copy-done.5, bf16[256,4608]{1,0:T(8,128)(2,1)} %bitcast.33, bf16[4608,256]{1,0:T(8,128)(2,1)S(1)} %copy-done), kind=kOutput, calls=%fused_computation.7 | convolution fusion | flops 873529344 | bytes 6815744 | tf_op jit(solution)/shard_map/dot_general | solution.py:258
  61.2 13.4 %shard_map.138 = bf16[32,2048]{1,0:T(8,128)(2,1)} custom-call(bf16[4,2,32,2048]{3,2,1,0:T(8,128)(2,1)} %bitcast.42), custom_call_target="tpu_custom_call" | custom-call | tf_op jit(solution)/shard_map/pallas_call | solution.py:107
  74.6 1.5 multiply_reduce_fusion
  77.9 20.5 %shard_map.139 = bf16[8,64,2176]{2,1,0:T(8,128)(2,1)} custom-call(bf16[64,2176]{1,0:T(8,128)(2,1)} %fusion.33.x_ref), custom_call_target="tpu_custom_call" | custom-call | tf_op jit(solution)/shard_map/pallas_call | solution.py:188
  101.0 2.2 convolution_convert_fusion.2
  103.2 1.3 reshape.88.x_ref
  104.5 30.6 %shard_map.140 = bf16[32,6,2048]{2,1,0:T(8,128)(2,1)} custom-call(bf16[32,6,2048]{2,1,0:T(8,128)(2,1)} %reshape.88.x_ref), custom_call_target="tpu_custom_call" | custom-call | tf_op jit(solution)/shard_map/pallas_call | solution.py:41
  135.1 2.3 reshape.89.x_ref
  137.5 45.2 %shard_map.141 = bf16[8,192,2048]{2,1,0:T(8,128)(2,1)} custom-call(bf16[192,2048]{1,0:T(8,128)(2,1)} %reshape.89.x_ref), custom_call_target="tpu_custom_call" | custom-call | tf_op jit(solution)/shard_map/pallas_call | solution.py:188
  182.7 6.0 %fusion.23 = f32[1536,176]{0,1:T(8,128)} fusion(bf16[1536,2048]{1,0:T(8,128)(2,1)} %bitcast.39, bf16[1,2048,176]{1,2,0:T(8,128)(2,1)S(1)} %copy-done.9), kind=kOutput, calls=%fused_computation.30 | convolution fusion | flops 1107296256 | bytes 8093696 | tf_op jit(solution)/shard_map/dot_general | solution.py:309
  188.7 10.0 %convolution_convert_fusion = bf16[1536,2048]{1,0:T(8,128)(2,1)} fusion(bf16[1536,2048]{1,0:T(8,128)(2,1)} %bitcast.40, f32[1536,176]{0,1:T(8,128)} %fusion.23, bf16[1,176,2048]{2,1,0:T(8,128)(2,1)} %param.25, bf16[1,2048,176]{1,2,0:T(8,128)(2,1)} %param.24), kind=kOutput, calls=%fused_computation.2 | convolution fusion | flops 2219360256 | bytes 15106048 | tf_op jit(solution)/shard_map/dot_general | solution.py:312
  198.7 47.5 %shard_map.142 = bf16[192,2048]{1,0:T(8,128)(2,1)} custom-call(bf16[4,2,192,2048]{3,2,1,0:T(8,128)(2,1)} %bitcast.41), custom_call_target="tpu_custom_call" | custom-call | tf_op jit(solution)/shard_map/pallas_call | solution.py:107
  246.3 2.2 reshape.91.x_ref
  248.5 29.3 %shard_map.143 = bf16[32,6,2048]{2,1,0:T(8,128)(2,1)} custom-call(bf16[32,6,2048]{2,1,0:T(8,128)(2,1)} %reshape.91.x_ref), custom_call_target="tpu_custom_call" | custom-call | tf_op jit(solution)/shard_map/pallas_call | solution.py:41
  277.8 1.6 reshape.92
  279.4 2.7 fusion.42
  282.1 2.7 fusion.51
  286.0 8.5 %add_convert_fusion = bf16[512,2048]{1,0:T(8,128)(2,1)} fusion(f32[512,2048]{1,0:T(8,128)} %fusion.51, f32[512,2048]{1,0:T(8,128)} %fusion.42, bf16[352,2048]{1,0:T(8,128)(2,1)} %param.22, bf16[2048,352]{0,1:T(8,128)(2,1)} %param.21, bf16[512,2176]{1,0:T(8,128)(2,1)} %bitcast.36, f32[512,352]{0,1:T(8,128)S(1)} %fusion.5), kind=kOutput, calls=%fused_computation.3 | convolution fusion | flops 1480622080 | bytes 16187392 | tf_op jit(solution)/shard_map/dot_general | solution.py:324
  294.5 22.5 %shard_map.144 = f32[64,2048]{1,0:T(8,128)} custom-call(bf16[4,2,64,2048]{3,2,1,0:T(8,128)(2,1)} %bitcast.38), custom_call_target="tpu_custom_call" | custom-call | tf_op jit(solution)/shard_map/pallas_call | solution.py:107
  317.0 1.8 add_convert_fusion.1
  (57 shorter events, 10.6 us)
Async XLA Ops:
  0.0 56.9 %copy-start = (bf16[4608,256]{1,0:T(8,128)(2,1)S(1)}, bf16[4608,256]{1,0:T(8,128)(2,1)}, u32[]{:S(2)}) copy-start(bf16[4608,256]{1,0:T(8,128)(2,1)} %param.17) | copy-start | bytes 7077892
  0.0 4.5 %copy-start.1 = (s32[32]{0:T(128)S(1)}, s32[32]{0:T(128)}, u32[]{:S(2)}) copy-start(s32[32]{0:T(128)} %param.16) | copy-start | bytes 388
  31.3 25.5 %copy-start.5 = (bf16[256,2048]{1,0:T(8,128)(2,1)S(1)}, bf16[256,2048]{1,0:T(8,128)(2,1)}, u32[]{:S(2)}) copy-start(bf16[256,2048]{1,0:T(8,128)(2,1)} %param.18) | copy-start | bytes 3145732
  56.9 20.0 %copy-start.6 = (f32[2048]{0:T(1024)S(1)}, f32[2048]{0:T(1024)}, u32[]{:S(2)}) copy-start(f32[2048]{0:T(1024)} %param.19) | copy-start | bytes 24580
  61.2 15.8 %copy-start.7 = (s32[64,2]{0,1:T(2,128)S(1)}, s32[64,2]{0,1:T(2,128)}, u32[]{:S(2)}) copy-start(s32[64,2]{0,1:T(2,128)} %param.27) | copy-start | bytes 1540
  61.2 15.8 %copy-start.10 = (s32[64,2]{0,1:T(2,128)S(1)}, s32[64,2]{0,1:T(2,128)}, u32[]{:S(2)}) copy-start(s32[64,2]{0,1:T(2,128)} %param.26) | copy-start | bytes 1540
  76.1 0.8 copy-start.3
  137.5 45.2 %copy-start.9 = (bf16[1,2048,176]{1,2,0:T(8,128)(2,1)S(1)}, bf16[1,2048,176]{1,2,0:T(8,128)(2,1)}, u32[]{:S(2)}) copy-start(bf16[1,2048,176]{1,2,0:T(8,128)(2,1)} %param.23) | copy-start | bytes 2162692
  282.1 2.7 copy-start.2
  282.1 2.9 copy-start.8
  294.4 22.5 %copy-start.4 = (f32[64,2048]{1,0:T(8,128)S(1)}, f32[64,2048]{1,0:T(8,128)}, u32[]{:S(2)}) copy-start(f32[64,2048]{1,0:T(8,128)} %copy-done.3) | copy-start | bytes 1572868

commit v6 on v5

--- a/solution.py
+++ b/solution.py
@@ -302,15 +302,16 @@
     pick = jnp.sum(hit.astype(f32), axis=1).astype(bf16)
     send = select_dot(pick.T, normed).astype(bf16).reshape(n_data, share, width_model)
     arrived = dp_all_to_all(send, 1)
-    slots = expert_all_gather(arrived.reshape(n_rows, width_model), 7).reshape(
-        n_group * n_rows, width_model
-    )
-
-    gate_e = jnp.dot(slots, expert_gate[0], preferred_element_type=f32)
-    up_e = jnp.dot(slots, expert_up[0], preferred_element_type=f32)
+    slots = lax.all_gather(arrived.reshape(n_rows, width_model), "expert", axis=0, tiled=True)
+
+    width_e = expert_gate.shape[2]
+    gate_up = jnp.dot(
+        slots, jnp.concatenate([expert_gate[0], expert_up[0]], axis=1), preferred_element_type=f32
+    )
+    gate_e, up_e = gate_up[:, :width_e], gate_up[:, width_e:]
     hidden_e = (jax.nn.silu(gate_e) * up_e).astype(bf16)
     partial_out = jnp.dot(hidden_e, expert_down[0], preferred_element_type=f32).astype(bf16)
-    summed = expert_reduce_scatter(partial_out.reshape(n_group, n_rows, width_model), 8, bf16)
+    summed = lax.psum_scatter(partial_out, "expert", scatter_dimension=0, tiled=True)
     returned = dp_all_to_all(summed.reshape(n_data, share, width_model), 2).reshape(
         n_rows, width_model
     )
@@ -319,10 +320,13 @@
     coef = jnp.sum(jnp.where(hit, weights_n[:, :, None], 0.0), axis=1)
     coef_hi = coef.astype(bf16)
     coef_lo = (coef - coef_hi.astype(f32)).astype(bf16)
-    combined = select_dot(coef_hi, returned) + select_dot(coef_lo, returned)
+    terms = jnp.dot(
+        jnp.concatenate([shared_hidden, coef_hi, coef_lo], axis=1),
+        jnp.concatenate([shared_down, returned, returned], axis=0),
+        preferred_element_type=f32,
+    )
     total = expert_reduce_scatter(
-        (jnp.dot(shared_hidden, shared_down, preferred_element_type=f32) + combined)
-        .astype(bf16)
+        terms.astype(bf16)
         .reshape(n_group, tok_dev, width_model),
         4,
         f32,

time: 319 us -> 314 us (0.984)
  Pallas kernels: 257 us -> 167 us
  waiting for transfers between devices: 0 us -> 80.5 us
  between operations: 0.32 us -> 13.7 us
  matrix products: 39.3 us -> 29.7 us
    pallas_call x3 -> x2, Pallas kernels: 83.4 us -> 36.3 us  [expert_reduce_scatter(): pl.pallas_call(kernel, out_shape=jax.ShapeDtypeStruct((rows, cols), out_d...]
    pallas_call x3 -> x2, Pallas kernels: 89.1 us -> 44 us  [expert_all_gather(): pl.pallas_call(kernel, out_shape=jax.ShapeDtypeStruct((n, rows, cols), x....]
    all_gather x0 -> x1, waiting for transfers between devices: none -> 41.8 us  [shards(): lax.all_gather(arrived.reshape(n_rows, width_model), 'expert', axis=0, ti...]
    reduce_scatter x0 -> x1, waiting for transfers between devices: none -> 38.7 us  [shards(): lax.psum_scatter(partial_out, 'expert', scatter_dimension=0, tiled=True)]
    dot_general x1, matrix products: 10 us -> 4.53 us  [shards(): jnp.dot(hidden_e, expert_down[0], preferred_element_type=f32).astype(bf16)]
    dot_general x5 -> x3, matrix products: 9.59 us -> 5.02 us  [select_dot(): return jnp.dot(sel, rows, preferred_element_type=jnp.float32)]
    dot_general x2 -> x3, matrix products: 14.5 us -> 12.5 us  [the longest x1 5.62 us: shards(): jnp.dot(slots, jnp.concatenate([expert_gate[0], expert_up[0]], axis=1), p...]
  transfers between devices with their start and end apart: 0 -> 2, of which waited for: 0 -> 2; matrix products, arithmetic and copies ran while one was open for 0% -> 2% of each run, Pallas kernels for 0% -> 0%
where the time goes in v6:
time: 314 us; the launch traced here: 313 us
  Pallas kernels  167 us (53%)
  waiting for transfers between devices  80.5 us (26%)
  matrix products  29.7 us (9%)
  local copies, waits for them, and re-layouts  15.9 us (5%)
  between operations  13.7 us (4%)
  other arithmetic  6.39 us (2%)
    pallas_call x3, Pallas kernels, dp_all_to_all(): pl.pallas_call(kernel, out_shape=jax.ShapeDtypeStruct(x.shape, x.dtype),...  86.6 us
    pallas_call x2, Pallas kernels, expert_all_gather(): pl.pallas_call(kernel, out_shape=jax.ShapeDtypeStruct((n, rows, cols), x....  44 us
    all_gather x1, waiting for transfers between devices, shards(): lax.all_gather(arrived.reshape(n_rows, width_model), 'expert', axis=0, ti...  41.8 us
    reduce_scatter x1, waiting for transfers between devices, shards(): lax.psum_scatter(partial_out, 'expert', scatter_dimension=0, tiled=True)  38.7 us
    pallas_call x2, Pallas kernels, expert_reduce_scatter(): pl.pallas_call(kernel, out_shape=jax.ShapeDtypeStruct((rows, cols), out_d...  36.3 us
  transfers between devices with their start and end apart: 2, of which 2 were waited for; matrix products, arithmetic and copies ran while one was open for 2% of the time, Pallas kernels for 0%

profile of v6, /device:TPU:1, one launch (start us, length us, event | category | flops | bytes accessed | tf_op | source)
XLA Modules:
  0.0 313.3 jit_solution(1855182589650627508)
XLA Ops:
  7.4 1.6 sort.17
  9.0 1.4 gather_fusion.1
  12.5 24.7 %shard_map.136 = bf16[32,1,4736]{2,1,0:T(2,128)(2,1)} custom-call(bf16[32,1,4736]{2,1,0:T(2,128)(2,1)} %copy.38.x_ref), custom_call_target="tpu_custom_call" | custom-call | tf_op jit(solution)/shard_map/pallas_call | solution.py:41
  39.5 23.5 %shard_map.137 = bf16[8,32,4608]{2,1,0:T(8,128)(2,1)} custom-call(bf16[32,4608]{1,0:T(8,128)(2,1)} %slice.41.x_ref), custom_call_target="tpu_custom_call" | custom-call | tf_op jit(solution)/shard_map/pallas_call | solution.py:188
  63.0 4.6 %convolution_convert_fusion.1 = bf16[256,2048]{1,0:T(8,128)(2,1)} fusion(bf16[256,2048]{1,0:T(8,128)(2,1)} %param.18, bf16[256,4608]{1,0:T(8,128)(2,1)} %bitcast.22, bf16[4608,256]{1,0:T(8,128)(2,1)S(1)} %copy-done), kind=kOutput, calls=%fused_computation.12 | convolution fusion | flops 873529344 | bytes 6815744 | tf_op jit(solution)/shard_map/dot_general | solution.py:258
  67.6 13.4 %shard_map.138 = bf16[32,2048]{1,0:T(8,128)(2,1)} custom-call(bf16[4,2,32,2048]{3,2,1,0:T(8,128)(2,1)} %bitcast.23), custom_call_target="tpu_custom_call" | custom-call | tf_op jit(solution)/shard_map/pallas_call | solution.py:107
  81.0 1.4 multiply_reduce_fusion
  83.2 20.5 %shard_map.139 = bf16[8,64,2176]{2,1,0:T(8,128)(2,1)} custom-call(bf16[64,2176]{1,0:T(8,128)(2,1)} %fusion.37.x_ref), custom_call_target="tpu_custom_call" | custom-call | tf_op jit(solution)/shard_map/pallas_call | solution.py:188
  106.3 3.1 convolution_convert_fusion.2
  109.4 2.2 reshape.85.x_ref
  111.6 30.6 %shard_map.140 = bf16[32,6,2048]{2,1,0:T(8,128)(2,1)} custom-call(bf16[32,6,2048]{2,1,0:T(8,128)(2,1)} %reshape.85.x_ref), custom_call_target="tpu_custom_call" | custom-call | tf_op jit(solution)/shard_map/pallas_call | solution.py:41
  142.3 2.2 reshape.86
  144.7 41.8 %all-gather.2.cloned.1.call-done = bf16[1536,2048]{1,0:T(8,128)(2,1)} async-done(((bf16[192,2048]{1,0:T(8,128)(2,1)}), bf16[1536,2048]{1,0:T(8,128)(2,1)}) %all-gather.2.cloned.1.call-update) | async-done | bytes 6291472 | tf_op jit(solution)/shard_map/all_gather | solution.py:305
  186.5 5.6 %fusion.15 = f32[1536,352]{0,1:T(8,128)S(1)} fusion(bf16[1536,2048]{1,0:T(8,128)(2,1)} %all-gather.2.cloned.1.call-done, bf16[2048,176]{0,1:T(8,128)(2,1)} %bitcast.31, bf16[2048,176]{0,1:T(8,128)(2,1)} %bitcast.32), kind=kOutput, calls=%fused_computation.20 | convolution fusion | flops 2217476096 | bytes 9895936 | tf_op jit(solution)/shard_map/dot_general | solution.py:308
  192.1 4.5 %convolution_convert_fusion = bf16[1536,2048]{1,0:T(8,128)(2,1)} fusion(bf16[1,176,2048]{2,1,0:T(8,128)(2,1)S(1)} %copy-done.8, f32[1536,352]{0,1:T(8,128)S(1)} %fusion.15), kind=kOutput, calls=%fused_computation.2 | convolution fusion | flops 1112064000 | bytes 9175040 | tf_op jit(solution)/shard_map/dot_general | solution.py:313
  197.4 3.1 fusion.13
  200.5 1.7 fusion.22
  202.3 38.7 %reduce-scatter.2.cloned.1.call-done = bf16[192,2048]{1,0:T(8,128)(2,1)} async-done(((bf16[1536,2048]{1,0:T(8,128)(2,1)}), bf16[192,2048]{1,0:T(8,128)(2,1)}) %reduce-scatter.2.cloned.1.call-update) | async-done | bytes 786448 | tf_op jit(solution)/shard_map/reduce_scatter | solution.py:314
  241.0 2.2 reshape.87.x_ref
  243.2 31.2 %shard_map.141 = bf16[32,6,2048]{2,1,0:T(8,128)(2,1)} custom-call(bf16[32,6,2048]{2,1,0:T(8,128)(2,1)} %reshape.87.x_ref), custom_call_target="tpu_custom_call" | custom-call | tf_op jit(solution)/shard_map/pallas_call | solution.py:41
  274.4 2.2 reshape.88
  276.6 5.1 %fusion.7 = bf16[512,2048]{1,0:T(8,128)(2,1)} fusion(bf16[192,2048]{1,0:T(8,128)(2,1)} %reshape.88, bf16[352,2048]{1,0:T(8,128)(2,1)} %param.22, bf16[512,192]{0,1:T(8,128)(2,1)S(1)} %get-tuple-element.9, bf16[512,192]{0,1:T(8,128)(2,1)S(1)} %copy-done.4, bf16[512,352]{0,1:T(8,128)(2,1)} %fusion.22), kind=kOutput, calls=%fused_computation.11 | convolution fusion | flops 1555857408 | bytes 5079040 | tf_op jit(solution)/shard_map/dot_general | solution.py:323
  281.7 22.9 %shard_map.142 = f32[64,2048]{1,0:T(8,128)} custom-call(bf16[4,2,64,2048]{3,2,1,0:T(8,128)(2,1)} %bitcast.28), custom_call_target="tpu_custom_call" | custom-call | tf_op jit(solution)/shard_map/pallas_call | solution.py:107
  304.7 1.8 add_convert_fusion
  (59 shorter events, 9.5 us)
Async XLA Ops:
  6.5 56.4 %copy-start = (bf16[4608,256]{1,0:T(8,128)(2,1)S(1)}, bf16[4608,256]{1,0:T(8,128)(2,1)}, u32[]{:S(2)}) copy-start(bf16[4608,256]{1,0:T(8,128)(2,1)} %param.17) | copy-start | bytes 7077892
  6.5 3.8 %copy-start.1 = (bf16[32,4608]{1,0:T(8,128)(2,1)S(1)}, bf16[32,4608]{1,0:T(8,128)(2,1)}, u32[]{:S(2)}) copy-start(bf16[32,4608]{1,0:T(8,128)(2,1)} %param.15) | copy-start | bytes 884740
  6.5 180.0 %all-gather.2.cloned.1.call-start = ((), (), s32[]{:S(2)}) async-start(), calls=%async_computation.1 | async-start | bytes 7077888 | tf_op jit(solution)/shard_map/all_gather | solution.py:305
  11.1 28.1 %copy-start.9 = (s32[64,2]{0,1:T(2,128)S(1)}, s32[64,2]{0,1:T(2,128)}, u32[]{:S(2)}) copy-start(s32[64,2]{0,1:T(2,128)} %param.26) | copy-start | bytes 1540
  11.1 28.1 %copy-start.6 = (s32[64,2]{0,1:T(2,128)S(1)}, s32[64,2]{0,1:T(2,128)}, u32[]{:S(2)}) copy-start(s32[64,2]{0,1:T(2,128)} %param.27) | copy-start | bytes 1540
  63.0 18.0 %copy-start.3 = (bf16[64,2048]{1,0:T(8,128)(2,1)S(1)}, bf16[64,2048]{1,0:T(8,128)(2,1)}, u32[]{:S(2)}) copy-start(bf16[64,2048]{1,0:T(8,128)(2,1)} %param.14) | copy-start | bytes 786436
  63.0 19.4 %copy-start.5 = (f32[2048]{0:T(1024)S(1)}, f32[2048]{0:T(1024)}, u32[]{:S(2)}) copy-start(f32[2048]{0:T(1024)} %param.19) | copy-start | bytes 24580
  144.5 96.5 %reduce-scatter.2.cloned.1.call-start = ((), (), s32[]{:S(2)}) async-start(), calls=%async_computation.2 | async-start | bytes 7077888 | tf_op jit(solution)/shard_map/reduce_scatter | solution.py:314
  186.5 5.6 %copy-start.8 = (bf16[1,176,2048]{2,1,0:T(8,128)(2,1)S(1)}, bf16[1,176,2048]{2,1,0:T(8,128)(2,1)}, u32[]{:S(2)}) copy-start(bf16[1,176,2048]{2,1,0:T(8,128)(2,1)} %param.25) | copy-start | bytes 2162692
  197.4 3.1 copy-start.2
  197.4 3.1 copy-start.7
  243.2 33.4 %copy-start.4 = (bf16[512,192]{0,1:T(8,128)(2,1)S(1)}, bf16[512,192]{0,1:T(8,128)(2,1)}, u32[]{:S(2)}) copy-start(bf16[512,192]{0,1:T(8,128)(2,1)} %get-tuple-element.10) | copy-start | bytes 589828
Sparse Core Ops, SparseCore 0:
  144.6 41.8 all-gather.1
  196.8 44.1 reduce-scatter.1

commit v7 on v6

--- a/solution.py
+++ b/solution.py
@@ -300,8 +300,10 @@
         == jnp.arange(n_rows, dtype=jnp.int32)[None, None, :]
     )
     pick = jnp.sum(hit.astype(f32), axis=1).astype(bf16)
-    send = select_dot(pick.T, normed).astype(bf16).reshape(n_data, share, width_model)
-    arrived = dp_all_to_all(send, 1)
+    lanes = 128
+    block = (n_data, share * width_model // lanes, lanes)
+    send = select_dot(pick.T, normed).astype(bf16).reshape(block)
+    arrived = lax.all_to_all(send, "dp", split_axis=0, concat_axis=0, tiled=True)
     slots = lax.all_gather(arrived.reshape(n_rows, width_model), "expert", axis=0, tiled=True)
 
     width_e = expert_gate.shape[2]
@@ -312,9 +314,9 @@
     hidden_e = (jax.nn.silu(gate_e) * up_e).astype(bf16)
     partial_out = jnp.dot(hidden_e, expert_down[0], preferred_element_type=f32).astype(bf16)
     summed = lax.psum_scatter(partial_out, "expert", scatter_dimension=0, tiled=True)
-    returned = dp_all_to_all(summed.reshape(n_data, share, width_model), 2).reshape(
-        n_rows, width_model
-    )
+    returned = lax.all_to_all(
+        summed.reshape(block), "dp", split_axis=0, concat_axis=0, tiled=True
+    ).reshape(n_rows, width_model)
 
     weights_n = weights_f / jnp.sum(weights_f, axis=1, keepdims=True)
     coef = jnp.sum(jnp.where(hit, weights_n[:, :, None], 0.0), axis=1)

time: 314 us -> 311 us (level)
  Pallas kernels: 167 us -> 107 us
  blocking collectives: 0 us -> 27.6 us
  waiting for transfers between devices: 80.5 us -> 101 us
  starting transfers between devices: 0.22 us -> 9.88 us
    pallas_call x3 -> x1, Pallas kernels: 86.6 us -> 24.7 us  [dp_all_to_all(): pl.pallas_call(kernel, out_shape=jax.ShapeDtypeStruct(x.shape, x.dtype),...]
    all_to_all x0 -> x1, blocking collectives: none -> 27.6 us  [shards(): lax.all_to_all(send, 'dp', split_axis=0, concat_axis=0, tiled=True)]
    all_to_all x0 -> x1, waiting for transfers between devices: none -> 14.2 us  [shards(): lax.all_to_all(summed.reshape(block), 'dp', split_axis=0, concat_axis=0,...]
    all_to_all x0 -> x1, starting transfers between devices: none -> 9.65 us  [shards(): lax.all_to_all(summed.reshape(block), 'dp', split_axis=0, concat_axis=0,...]
    reduce_scatter x1, waiting for transfers between devices: 38.7 us -> 44.3 us  [shards(): lax.psum_scatter(partial_out, 'expert', scatter_dimension=0, tiled=True)]
  transfers between devices with their start and end apart: 2 -> 3, of which waited for: 2 -> 3; matrix products, arithmetic and copies ran while one was open for 2% -> 2% of each run, Pallas kernels for 0% -> 0%
where the time goes in v7:
time: 311 us; the launch traced here: 310 us
  Pallas kernels  107 us (34%)
  waiting for transfers between devices  101 us (32%)
  matrix products  29.7 us (10%)
  blocking collectives  27.6 us (9%)
  local copies, waits for them, and re-layouts  15.9 us (5%)
  between operations  13.7 us (4%)
  starting transfers between devices  9.88 us (3%)
  other arithmetic  6.39 us (2%)
    reduce_scatter x1, waiting for transfers between devices, shards(): lax.psum_scatter(partial_out, 'expert', scatter_dimension=0, tiled=True)  44.3 us
    pallas_call x2, Pallas kernels, expert_all_gather(): pl.pallas_call(kernel, out_shape=jax.ShapeDtypeStruct((n, rows, cols), x....  44 us
    all_gather x1, waiting for transfers between devices, shards(): lax.all_gather(arrived.reshape(n_rows, width_model), 'expert', axis=0, ti...  42 us
    pallas_call x2, Pallas kernels, expert_reduce_scatter(): pl.pallas_call(kernel, out_shape=jax.ShapeDtypeStruct((rows, cols), out_d...  38.1 us
    all_to_all x1, blocking collectives, shards(): lax.all_to_all(send, 'dp', split_axis=0, concat_axis=0, tiled=True)  27.6 us
    pallas_call x1, Pallas kernels, dp_all_to_all(): pl.pallas_call(kernel, out_shape=jax.ShapeDtypeStruct(x.shape, x.dtype),...  24.7 us
    all_to_all x1, waiting for transfers between devices, shards(): lax.all_to_all(summed.reshape(block), 'dp', split_axis=0, concat_axis=0,...  14.2 us
    all_to_all x1, starting transfers between devices, shards(): lax.all_to_all(summed.reshape(block), 'dp', split_axis=0, concat_axis=0,...  9.65 us
  transfers between devices with their start and end apart: 3, of which 3 were waited for; matrix products, arithmetic and copies ran while one was open for 2% of the time, Pallas kernels for 0%

profile of v7, /device:TPU:1, one launch (start us, length us, event | category | flops | bytes accessed | tf_op | source)
XLA Modules:
  0.0 310.4 jit_solution(7707741018003426749)
XLA Ops:
  7.4 1.6 sort.17
  12.5 24.7 %shard_map.136 = bf16[32,1,4736]{2,1,0:T(2,128)(2,1)} custom-call(bf16[32,1,4736]{2,1,0:T(2,128)(2,1)} %copy.38.x_ref), custom_call_target="tpu_custom_call" | custom-call | tf_op jit(solution)/shard_map/pallas_call | solution.py:41
  39.5 23.5 %shard_map.137 = bf16[8,32,4608]{2,1,0:T(8,128)(2,1)} custom-call(bf16[32,4608]{1,0:T(8,128)(2,1)} %slice.41.x_ref), custom_call_target="tpu_custom_call" | custom-call | tf_op jit(solution)/shard_map/pallas_call | solution.py:188
  63.0 4.6 %convolution_convert_fusion.1 = bf16[256,2048]{1,0:T(8,128)(2,1)} fusion(bf16[256,2048]{1,0:T(8,128)(2,1)} %param.18, bf16[256,4608]{1,0:T(8,128)(2,1)} %bitcast.22, bf16[4608,256]{1,0:T(8,128)(2,1)S(1)} %copy-done), kind=kOutput, calls=%fused_computation.12 | convolution fusion | flops 873529344 | bytes 6815744 | tf_op jit(solution)/shard_map/dot_general | solution.py:258
  67.6 13.4 %shard_map.138 = bf16[32,2048]{1,0:T(8,128)(2,1)} custom-call(bf16[4,2,32,2048]{3,2,1,0:T(8,128)(2,1)} %bitcast.23), custom_call_target="tpu_custom_call" | custom-call | tf_op jit(solution)/shard_map/pallas_call | solution.py:107
  81.0 1.4 multiply_reduce_fusion
  83.2 20.5 %shard_map.139 = bf16[8,64,2176]{2,1,0:T(8,128)(2,1)} custom-call(bf16[64,2176]{1,0:T(8,128)(2,1)} %fusion.37.x_ref), custom_call_target="tpu_custom_call" | custom-call | tf_op jit(solution)/shard_map/pallas_call | solution.py:188
  106.3 3.1 %convolution_convert_fusion.2 = bf16[192,2048]{1,0:T(8,128)(2,1)} fusion(bf16[512,2176]{1,0:T(8,128)(2,1)} %bitcast.25, bf16[512,192]{0,1:T(8,128)(2,1)S(1)} %get-tuple-element.8), kind=kOutput, calls=%fused_computation.13 | convolution fusion | flops 403046400 | bytes 3080192 | tf_op jit(solution)/shard_map/dot_general | solution.py:212
  109.4 2.2 reshape.85
  111.6 27.6 %all_to_all.10 = bf16[32,96,128]{2,1,0:T(8,128)(2,1)} all-to-all(bf16[32,96,128]{2,1,0:T(8,128)(2,1)} %reshape.85), channel_id=1, replica_groups=mesh['dp'=32,'expert'=8] {'dp'}, dimensions={0} | all-to-all | bytes 1572864 | tf_op jit(solution)/shard_map/all_to_all | solution.py:306
  139.1 2.2 reshape.86
  141.6 42.0 %all-gather.2.cloned.1.call-done = bf16[1536,2048]{1,0:T(8,128)(2,1)} async-done(((bf16[192,2048]{1,0:T(8,128)(2,1)}), bf16[1536,2048]{1,0:T(8,128)(2,1)}) %all-gather.2.cloned.1.call-update) | async-done | bytes 6291472 | tf_op jit(solution)/shard_map/all_gather | solution.py:307
  183.7 5.6 %fusion.15 = f32[1536,352]{0,1:T(8,128)S(1)} fusion(bf16[1536,2048]{1,0:T(8,128)(2,1)} %all-gather.2.cloned.1.call-done, bf16[2048,176]{0,1:T(8,128)(2,1)} %bitcast.31, bf16[2048,176]{0,1:T(8,128)(2,1)} %bitcast.32), kind=kOutput, calls=%fused_computation.20 | convolution fusion | flops 2217476096 | bytes 9895936 | tf_op jit(solution)/shard_map/dot_general | solution.py:310
  189.3 4.5 %convolution_convert_fusion = bf16[1536,2048]{1,0:T(8,128)(2,1)} fusion(bf16[1,176,2048]{2,1,0:T(8,128)(2,1)S(1)} %copy-done.8, f32[1536,352]{0,1:T(8,128)S(1)} %fusion.15), kind=kOutput, calls=%fused_computation.2 | convolution fusion | flops 1112064000 | bytes 9175040 | tf_op jit(solution)/shard_map/dot_general | solution.py:315
  193.8 44.3 %reduce-scatter.2.cloned.1.call-done = bf16[192,2048]{1,0:T(8,128)(2,1)} async-done(((bf16[1536,2048]{1,0:T(8,128)(2,1)}), bf16[192,2048]{1,0:T(8,128)(2,1)}) %reduce-scatter.2.cloned.1.call-update) | async-done | bytes 786448 | tf_op jit(solution)/shard_map/reduce_scatter | solution.py:316
  238.1 2.2 reshape.87
  240.3 9.7 %all-to-all-start.1 = ((bf16[32,96,128]{2,1,0:T(8,128)(2,1)}), bf16[32,96,128]{2,1,0:T(8,128)(2,1)}, u32[]{:S(2)}, u32[]{:S(2)}) async-start(bf16[32,96,128]{2,1,0:T(8,128)(2,1)} %reshape.87), calls=%async_computation.2 | async-start | bytes 1572864 | tf_op jit(solution)/shard_map/all_to_all | solution.py:317
  250.7 3.1 fusion.13
  253.8 1.7 fusion.22
  255.6 14.2 %all-to-all-done.1 = bf16[32,96,128]{2,1,0:T(8,128)(2,1)} async-done(((bf16[32,96,128]{2,1,0:T(8,128)(2,1)}), bf16[32,96,128]{2,1,0:T(8,128)(2,1)}, u32[]{:S(2)}, u32[]{:S(2)}) %all-to-all-start.1) | async-done | bytes 786464 | tf_op jit(solution)/shard_map/all_to_all | solution.py:317
  269.8 2.2 reshape.88
  272.0 5.1 %fusion.7 = bf16[512,2048]{1,0:T(8,128)(2,1)} fusion(bf16[192,2048]{1,0:T(8,128)(2,1)} %reshape.88, bf16[352,2048]{1,0:T(8,128)(2,1)} %param.22, bf16[512,192]{0,1:T(8,128)(2,1)S(1)} %get-tuple-element.9, bf16[512,192]{0,1:T(8,128)(2,1)S(1)} %copy-done.4, bf16[512,352]{0,1:T(8,128)(2,1)} %fusion.22), kind=kOutput, calls=%fused_computation.11 | convolution fusion | flops 1555857408 | bytes 5079040 | tf_op jit(solution)/shard_map/dot_general | solution.py:325
  277.1 24.7 %shard_map.140 = f32[64,2048]{1,0:T(8,128)} custom-call(bf16[4,2,64,2048]{3,2,1,0:T(8,128)(2,1)} %bitcast.28), custom_call_target="tpu_custom_call" | custom-call | tf_op jit(solution)/shard_map/pallas_call | solution.py:107
  301.8 1.8 add_convert_fusion
  (60 shorter events, 10.9 us)
Async XLA Ops:
  6.5 56.4 %copy-start = (bf16[4608,256]{1,0:T(8,128)(2,1)S(1)}, bf16[4608,256]{1,0:T(8,128)(2,1)}, u32[]{:S(2)}) copy-start(bf16[4608,256]{1,0:T(8,128)(2,1)} %param.17) | copy-start | bytes 7077892
  6.5 3.8 %copy-start.1 = (bf16[32,4608]{1,0:T(8,128)(2,1)S(1)}, bf16[32,4608]{1,0:T(8,128)(2,1)}, u32[]{:S(2)}) copy-start(bf16[32,4608]{1,0:T(8,128)(2,1)} %param.15) | copy-start | bytes 884740
  6.5 177.1 %all-gather.2.cloned.1.call-start = ((), (), s32[]{:S(2)}) async-start(), calls=%async_computation.3 | async-start | bytes 7077888 | tf_op jit(solution)/shard_map/all_gather | solution.py:307
  11.1 28.1 %copy-start.9 = (s32[64,2]{0,1:T(2,128)S(1)}, s32[64,2]{0,1:T(2,128)}, u32[]{:S(2)}) copy-start(s32[64,2]{0,1:T(2,128)} %param.26) | copy-start | bytes 1540
  11.1 28.1 %copy-start.6 = (s32[64,2]{0,1:T(2,128)S(1)}, s32[64,2]{0,1:T(2,128)}, u32[]{:S(2)}) copy-start(s32[64,2]{0,1:T(2,128)} %param.27) | copy-start | bytes 1540
  63.0 18.0 %copy-start.3 = (bf16[64,2048]{1,0:T(8,128)(2,1)S(1)}, bf16[64,2048]{1,0:T(8,128)(2,1)}, u32[]{:S(2)}) copy-start(bf16[64,2048]{1,0:T(8,128)(2,1)} %param.14) | copy-start | bytes 786436
  63.0 19.4 %copy-start.5 = (f32[2048]{0:T(1024)S(1)}, f32[2048]{0:T(1024)}, u32[]{:S(2)}) copy-start(f32[2048]{0:T(1024)} %param.19) | copy-start | bytes 24580
  141.4 96.7 %reduce-scatter.2.cloned.1.call-start = ((), (), s32[]{:S(2)}) async-start(), calls=%async_computation.4 | async-start | bytes 7077888 | tf_op jit(solution)/shard_map/reduce_scatter | solution.py:316
  183.7 5.6 %copy-start.8 = (bf16[1,176,2048]{2,1,0:T(8,128)(2,1)S(1)}, bf16[1,176,2048]{2,1,0:T(8,128)(2,1)}, u32[]{:S(2)}) copy-start(bf16[1,176,2048]{2,1,0:T(8,128)(2,1)} %param.25) | copy-start | bytes 2162692
  240.3 29.5 %all-to-all-start.1 = ((bf16[32,96,128]{2,1,0:T(8,128)(2,1)}), bf16[32,96,128]{2,1,0:T(8,128)(2,1)}, u32[]{:S(2)}, u32[]{:S(2)}) async-start(bf16[32,96,128]{2,1,0:T(8,128)(2,1)} %reshape.87), calls=%async_computation.2 | async-start | bytes 1572864 | tf_op jit(solution)/shard_map/all_to_all | solution.py:317
  250.7 3.1 copy-start.2
  250.7 3.1 copy-start.7
  253.8 18.2 %copy-start.4 = (bf16[512,192]{0,1:T(8,128)(2,1)S(1)}, bf16[512,192]{0,1:T(8,128)(2,1)}, u32[]{:S(2)}) copy-start(bf16[512,192]{0,1:T(8,128)(2,1)} %get-tuple-element.10) | copy-start | bytes 589828
Sparse Core Ops, SparseCore 0:
  141.5 42.1 all-gather.1
  194.0 44.1 reduce-scatter.1

commit v8 on v7

--- a/solution.py
+++ b/solution.py
@@ -202,6 +202,85 @@
     )(x)
 
 
+def fused_projector(feats, proj_in, proj_out, collective_id):
+    rows, width_vis = feats.shape
+    n = lax.axis_size("expert")
+    width_model = proj_out.shape[1]
+    mesh_ids = pl.DeviceIdType.MESH
+    f32, bf16 = jnp.float32, jnp.bfloat16
+
+    def kernel(f_ref, wi_ref, wo_ref, o_ref, fbuf, psend, pbuf, send_f, recv_f, send_p, recv_p):
+        me = lax.axis_index("expert")
+        row = lax.axis_index("dp")
+        barrier = pltpu.get_barrier_semaphore()
+        for k in range(1, n):
+            pl.semaphore_signal(
+                barrier, inc=1, device_id=(row, lax.rem(me + k, n)), device_id_type=mesh_ids
+            )
+        pl.semaphore_wait(barrier, n - 1)
+        feat_copies = []
+        for k in range(1, n):
+            copy = pltpu.make_async_remote_copy(
+                src_ref=f_ref,
+                dst_ref=fbuf.at[me],
+                send_sem=send_f.at[k],
+                recv_sem=recv_f.at[k],
+                device_id=(row, lax.rem(me + k, n)),
+                device_id_type=mesh_ids,
+            )
+            copy.start()
+            feat_copies.append(copy)
+
+        def partial(x):
+            hidden = jnp.dot(x, wi_ref[...], preferred_element_type=f32)
+            hidden = jax.nn.gelu(hidden, approximate=True).astype(bf16)
+            return jnp.dot(hidden, wo_ref[...], preferred_element_type=f32)
+
+        acc = partial(f_ref[...])
+        part_copies = []
+        for k, copy in enumerate(feat_copies, 1):
+            copy.wait_recv()
+            source = lax.rem(me - k + n, n)
+            psend[k] = partial(fbuf[source]).astype(bf16)
+            back = pltpu.make_async_remote_copy(
+                src_ref=psend.at[k],
+                dst_ref=pbuf.at[k],
+                send_sem=send_p.at[k],
+                recv_sem=recv_p.at[k],
+                device_id=(row, source),
+                device_id_type=mesh_ids,
+            )
+            back.start()
+            part_copies.append(back)
+        for k, back in enumerate(part_copies, 1):
+            back.wait_recv()
+            acc = acc + pbuf[k].astype(f32)
+        o_ref[...] = acc.astype(o_ref.dtype)
+        for copy in feat_copies:
+            copy.wait_send()
+        for back in part_copies:
+            back.wait_send()
+
+    return pl.pallas_call(
+        kernel,
+        out_shape=jax.ShapeDtypeStruct((rows, width_model), bf16),
+        in_specs=[pl.BlockSpec(memory_space=pltpu.VMEM)] * 3,
+        out_specs=pl.BlockSpec(memory_space=pltpu.VMEM),
+        scratch_shapes=[
+            pltpu.VMEM((n, rows, width_vis), feats.dtype),
+            pltpu.VMEM((n, rows, width_model), bf16),
+            pltpu.VMEM((n, rows, width_model), bf16),
+            pltpu.SemaphoreType.DMA((n,)),
+            pltpu.SemaphoreType.DMA((n,)),
+            pltpu.SemaphoreType.DMA((n,)),
+            pltpu.SemaphoreType.DMA((n,)),
+        ],
+        compiler_params=pltpu.CompilerParams(
+            collective_id=collective_id, has_side_effects=True, vmem_limit_bytes=48 * 1024 * 1024
+        ),
+    )(feats, proj_in, proj_out)
+
+
 def normalize(rows, norm_gain):
     rows_f = rows.astype(jnp.float32)
     meansq = jnp.mean(rows_f * rows_f, axis=-1, keepdims=True) + 1e-06
@@ -251,14 +330,7 @@
     moved_feats = moved[:, :width_vis]
     moved_offs = moved[:, width_vis].astype(jnp.int32)
 
-    feats = expert_all_gather(moved_feats, 5).reshape(n_group * img_dev, width_vis)
-    vis_hidden = jax.nn.gelu(
-        jnp.dot(feats, proj_in, preferred_element_type=f32), approximate=True
-    ).astype(bf16)
-    partial_proj = jnp.dot(vis_hidden, proj_out, preferred_element_type=f32).astype(bf16)
-    projected = expert_reduce_scatter(
-        partial_proj.reshape(n_group, img_dev, width_model), 3, bf16
-    )
+    projected = fused_projector(moved_feats, proj_in, proj_out, 5)
 
     place = (
         moved_offs[None, :] == jnp.arange(tok_dev, dtype=jnp.int32)[:, None]

time: 311 us -> 307 us (0.987)
  matrix products: 29.7 us -> 22.4 us
  Pallas kernels: 107 us -> 113 us
  local copies, waits for them, and re-layouts: 15.9 us -> 12.2 us
    pallas_call x0 -> x1, Pallas kernels: none -> 42.3 us  [fused_projector(): pl.pallas_call(kernel, out_shape=jax.ShapeDtypeStruct((rows, width_model)...]
    pallas_call x2 -> x1, Pallas kernels: 44 us -> 21.6 us  [expert_all_gather(): pl.pallas_call(kernel, out_shape=jax.ShapeDtypeStruct((n, rows, cols), x....]
    pallas_call x2 -> x1, Pallas kernels: 38.1 us -> 24.7 us  [expert_reduce_scatter(): pl.pallas_call(kernel, out_shape=jax.ShapeDtypeStruct((rows, cols), out_d...]
    dot_general x1 -> x0, matrix products: 4.61 us -> none  [shards(): jnp.dot(vis_hidden, proj_out, preferred_element_type=f32).astype(bf16)]
where the time goes in v8:
time: 307 us
  Pallas kernels  113 us (37%)
  waiting for transfers between devices  101 us (33%)
  blocking collectives  27.3 us (9%)
  matrix products  22.4 us (7%)
  between operations  13.7 us (4%)
  local copies, waits for them, and re-layouts  12.2 us (4%)
  starting transfers between devices  9.76 us (3%)
  other arithmetic  7.18 us (2%)
    reduce_scatter x1, waiting for transfers between devices, shards(): lax.psum_scatter(partial_out, 'expert', scatter_dimension=0, tiled=True)  44.3 us
    pallas_call x1, Pallas kernels, fused_projector(): pl.pallas_call(kernel, out_shape=jax.ShapeDtypeStruct((rows, width_model)...  42.3 us
    all_gather x1, waiting for transfers between devices, shards(): lax.all_gather(arrived.reshape(n_rows, width_model), 'expert', axis=0, ti...  42.1 us
    all_to_all x1, blocking collectives, shards(): lax.all_to_all(send, 'dp', split_axis=0, concat_axis=0, tiled=True)  27.3 us
    pallas_call x1, Pallas kernels, dp_all_to_all(): pl.pallas_call(kernel, out_shape=jax.ShapeDtypeStruct(x.shape, x.dtype),...  24.7 us
    pallas_call x1, Pallas kernels, expert_reduce_scatter(): pl.pallas_call(kernel, out_shape=jax.ShapeDtypeStruct((rows, cols), out_d...  24.7 us
    pallas_call x1, Pallas kernels, expert_all_gather(): pl.pallas_call(kernel, out_shape=jax.ShapeDtypeStruct((n, rows, cols), x....  21.6 us
    all_to_all x1, waiting for transfers between devices, shards(): lax.all_to_all(summed.reshape(block), 'dp', split_axis=0, concat_axis=0,...  14.6 us
  transfers between devices with their start and end apart: 3, of which 3 were waited for; matrix products, arithmetic and copies ran while one was open for 2% of the time, Pallas kernels for 0%

profile of v8, /device:TPU:1, one launch (start us, length us, event | category | flops | bytes accessed | tf_op | source)
XLA Modules:
  0.0 306.8 jit_solution(3901720763412234056)
XLA Ops:
  7.3 1.6 sort.17
  9.0 1.4 gather_fusion.1
  11.2 1.3 copy.38.x_ref
  12.5 24.7 %shard_map.136 = bf16[32,1,4736]{2,1,0:T(2,128)(2,1)} custom-call(bf16[32,1,4736]{2,1,0:T(2,128)(2,1)} %copy.38.x_ref), custom_call_target="tpu_custom_call" | custom-call | tf_op jit(solution)/shard_map/pallas_call | solution.py:41
  37.2 1.1 copy.49
  38.7 1.7 copy-done.1
  40.4 42.3 %shard_map.137 = bf16[32,2048]{1,0:T(8,128)(2,1)S(1)} custom-call(bf16[32,4608]{1,0:T(8,128)(2,1)S(1)} %slice.41.f_ref, bf16[4608,256]{1,0:T(8,128)(2,1)S(1)} %copy-done.1, bf16[256,2048]{1,0:T(8,128)(2,1)S(1)} %copy-done.2), custom_call_target="tpu_custom_call" | custom-call | tf_op jit(solution)/shard_map/pallas_call | solution.py:264
  84.1 21.6 %shard_map.138 = bf16[8,64,2176]{2,1,0:T(8,128)(2,1)} custom-call(bf16[64,2176]{1,0:T(8,128)(2,1)} %fusion.37.x_ref), custom_call_target="tpu_custom_call" | custom-call | tf_op jit(solution)/shard_map/pallas_call | solution.py:188
  108.1 1.0 select_reduce_fusion
  109.0 2.2 convolution_convert_fusion.1
  111.6 27.3 %all_to_all.10 = bf16[32,96,128]{2,1,0:T(8,128)(2,1)S(1)} all-to-all(bf16[32,96,128]{2,1,0:T(8,128)(2,1)S(1)} %reshape.81), channel_id=1, replica_groups=mesh['dp'=32,'expert'=8] {'dp'}, dimensions={0} | all-to-all | bytes 1572864 | tf_op jit(solution)/shard_map/all_to_all | solution.py:378
  138.9 1.3 reshape.82
  140.4 42.1 %all-gather.2.cloned.1.call-done = bf16[1536,2048]{1,0:T(8,128)(2,1)} async-done(((bf16[192,2048]{1,0:T(8,128)(2,1)}), bf16[1536,2048]{1,0:T(8,128)(2,1)}) %all-gather.2.cloned.1.call-update) | async-done | bytes 6291472 | tf_op jit(solution)/shard_map/all_gather | solution.py:379
  182.5 5.4 %fusion.15 = f32[1536,352]{0,1:T(8,128)S(1)} fusion(bf16[1536,2048]{1,0:T(8,128)(2,1)} %all-gather.2.cloned.1.call-done, bf16[2048,176]{0,1:T(8,128)(2,1)S(1)} %bitcast.24, bf16[2048,176]{0,1:T(8,128)(2,1)} %bitcast.25), kind=kOutput, calls=%fused_computation.19 | convolution fusion | flops 2217476096 | bytes 9895936 | tf_op jit(solution)/shard_map/dot_general | solution.py:382
  187.9 4.5 %convolution_convert_fusion = bf16[1536,2048]{1,0:T(8,128)(2,1)} fusion(bf16[1,176,2048]{2,1,0:T(8,128)(2,1)S(1)} %copy-done.11, f32[1536,352]{0,1:T(8,128)S(1)} %fusion.15), kind=kOutput, calls=%fused_computation.2 | convolution fusion | flops 1112064000 | bytes 9175040 | tf_op jit(solution)/shard_map/dot_general | solution.py:387
  192.5 44.3 %reduce-scatter.2.cloned.1.call-done = bf16[192,2048]{1,0:T(8,128)(2,1)} async-done(((bf16[1536,2048]{1,0:T(8,128)(2,1)}), bf16[192,2048]{1,0:T(8,128)(2,1)}) %reduce-scatter.2.cloned.1.call-update) | async-done | bytes 786448 | tf_op jit(solution)/shard_map/reduce_scatter | solution.py:388
  236.8 2.2 reshape.83
  238.9 9.5 %all-to-all-start.1 = ((bf16[32,96,128]{2,1,0:T(8,128)(2,1)}), bf16[32,96,128]{2,1,0:T(8,128)(2,1)S(1)}, u32[]{:S(2)}, u32[]{:S(2)}) async-start(bf16[32,96,128]{2,1,0:T(8,128)(2,1)} %reshape.83), calls=%async_computation.2 | async-start | bytes 1572864 | tf_op jit(solution)/shard_map/all_to_all | solution.py:389
  249.3 2.7 fusion.13
  252.0 1.8 fusion.22
  253.7 14.6 %all-to-all-done.1 = bf16[32,96,128]{2,1,0:T(8,128)(2,1)S(1)} async-done(((bf16[32,96,128]{2,1,0:T(8,128)(2,1)}), bf16[32,96,128]{2,1,0:T(8,128)(2,1)S(1)}, u32[]{:S(2)}, u32[]{:S(2)}) %all-to-all-start.1) | async-done | bytes 786464 | tf_op jit(solution)/shard_map/all_to_all | solution.py:389
  268.6 4.9 %fusion.7 = bf16[512,2048]{1,0:T(8,128)(2,1)} fusion(bf16[192,2048]{1,0:T(8,128)(2,1)S(1)} %reshape.84, bf16[352,2048]{1,0:T(8,128)(2,1)} %param.22, bf16[512,192]{0,1:T(8,128)(2,1)} %get-tuple-element.9, bf16[512,192]{0,1:T(8,128)(2,1)} %get-tuple-element.10, bf16[512,352]{0,1:T(8,128)(2,1)} %fusion.22), kind=kOutput, calls=%fused_computation.11 | convolution fusion | flops 1555857408 | bytes 5079040 | tf_op jit(solution)/shard_map/dot_general | solution.py:397
  273.5 24.7 %shard_map.139 = f32[64,2048]{1,0:T(8,128)} custom-call(bf16[4,2,64,2048]{3,2,1,0:T(8,128)(2,1)} %bitcast.21), custom_call_target="tpu_custom_call" | custom-call | tf_op jit(solution)/shard_map/pallas_call | solution.py:107
  298.2 1.8 add_convert_fusion
  (64 shorter events, 7.4 us)
Async XLA Ops:
  6.5 242.7 %copy-start = (bf16[2048,352]{0,1:T(8,128)(2,1)S(1)}, bf16[2048,352]{0,1:T(8,128)(2,1)}, u32[]{:S(2)}) copy-start(bf16[2048,352]{0,1:T(8,128)(2,1)} %param.20) | copy-start | bytes 4325380
  6.5 3.8 %copy-start.3 = (bf16[32,4608]{1,0:T(8,128)(2,1)S(1)}, bf16[32,4608]{1,0:T(8,128)(2,1)}, u32[]{:S(2)}) copy-start(bf16[32,4608]{1,0:T(8,128)(2,1)} %param.15) | copy-start | bytes 884740
  6.5 176.0 %all-gather.2.cloned.1.call-start = ((), (), s32[]{:S(2)}) async-start(), calls=%async_computation.3 | async-start | bytes 7077888 | tf_op jit(solution)/shard_map/all_gather | solution.py:379
  11.2 27.3 %copy-start.12 = (s32[64,2]{0,1:T(2,128)S(1)}, s32[64,2]{0,1:T(2,128)}, u32[]{:S(2)}) copy-start(s32[64,2]{0,1:T(2,128)} %param.26) | copy-start | bytes 1540
  11.2 27.3 %copy-start.8 = (s32[64,2]{0,1:T(2,128)S(1)}, s32[64,2]{0,1:T(2,128)}, u32[]{:S(2)}) copy-start(s32[64,2]{0,1:T(2,128)} %param.27) | copy-start | bytes 1540
  11.2 27.6 %copy-start.2 = (bf16[256,2048]{1,0:T(8,128)(2,1)S(1)}, bf16[256,2048]{1,0:T(8,128)(2,1)}, u32[]{:S(2)}) copy-start(bf16[256,2048]{1,0:T(8,128)(2,1)} %wo_ref.1) | copy-start | bytes 3145732
  38.4 44.3 %copy-start.6 = (bf16[64,2048]{1,0:T(8,128)(2,1)S(1)}, bf16[64,2048]{1,0:T(8,128)(2,1)}, u32[]{:S(2)}) copy-start(bf16[64,2048]{1,0:T(8,128)(2,1)} %param.14) | copy-start | bytes 786436
  38.7 1.7 copy-start.1
  40.4 42.8 %copy-start.7 = (f32[2048]{0:T(1024)S(1)}, f32[2048]{0:T(1024)}, u32[]{:S(2)}) copy-start(f32[2048]{0:T(1024)} %param.19) | copy-start | bytes 24580
  138.9 43.6 %copy-start.10 = (bf16[1,2048,176]{1,2,0:T(8,128)(2,1)S(1)}, bf16[1,2048,176]{1,2,0:T(8,128)(2,1)}, u32[]{:S(2)}) copy-start(bf16[1,2048,176]{1,2,0:T(8,128)(2,1)} %param.24) | copy-start | bytes 2162692
  140.2 96.6 %reduce-scatter.2.cloned.1.call-start = ((), (), s32[]{:S(2)}) async-start(), calls=%async_computation.4 | async-start | bytes 7077888 | tf_op jit(solution)/shard_map/reduce_scatter | solution.py:388
  182.5 5.4 %copy-start.11 = (bf16[1,176,2048]{2,1,0:T(8,128)(2,1)S(1)}, bf16[1,176,2048]{2,1,0:T(8,128)(2,1)}, u32[]{:S(2)}) copy-start(bf16[1,176,2048]{2,1,0:T(8,128)(2,1)} %param.25) | copy-start | bytes 2162692
  192.5 56.0 %copy-start.5 = (f32[512,192]{0,1:T(8,128)S(1)}, f32[512,192]{0,1:T(8,128)}, u32[]{:S(2)}) copy-start(f32[512,192]{0,1:T(8,128)} %get-tuple-element.7) | copy-start | bytes 1179652
  238.9 29.3 %all-to-all-start.1 = ((bf16[32,96,128]{2,1,0:T(8,128)(2,1)}), bf16[32,96,128]{2,1,0:T(8,128)(2,1)S(1)}, u32[]{:S(2)}, u32[]{:S(2)}) async-start(bf16[32,96,128]{2,1,0:T(8,128)(2,1)} %reshape.83), calls=%async_computation.2 | async-start | bytes 1572864 | tf_op jit(solution)/shard_map/all_to_all | solution.py:389
  249.3 2.7 copy-start.4
  249.3 2.7 copy-start.9
Sparse Core Ops, SparseCore 0:
  140.3 42.1 all-gather.1
  192.6 44.1 reduce-scatter.1

commit v9 on v8

--- a/solution.py
+++ b/solution.py
@@ -52,12 +52,12 @@
     )(x)
 
 
-def expert_reduce_scatter(x, collective_id, out_dtype):
+def expert_reduce_scatter(x, collective_id, out_dtype, base):
     n, rows, cols = x.shape
     chips = n // 2
     mesh_ids = pl.DeviceIdType.MESH
 
-    def kernel(x_ref, o_ref, pair_buf, part, far_buf, send1, recv1, send2, recv2):
+    def kernel(x_ref, b_ref, o_ref, pair_buf, part, far_buf, send1, recv1, send2, recv2):
         me = lax.axis_index("expert")
         row = lax.axis_index("dp")
         chip, core = me // 2, me % 2
@@ -99,6 +99,7 @@
             copy.start()
             copies.append(copy)
         acc = x_ref[chip, core].astype(jnp.float32) + pair_buf[chip].astype(jnp.float32)
+        acc = acc + b_ref[...].astype(jnp.float32)
         for k, copy in enumerate(copies, 1):
             copy.wait()
             acc = acc + far_buf[k].astype(jnp.float32)
@@ -107,7 +108,7 @@
     return pl.pallas_call(
         kernel,
         out_shape=jax.ShapeDtypeStruct((rows, cols), out_dtype),
-        in_specs=[pl.BlockSpec(memory_space=pltpu.VMEM)],
+        in_specs=[pl.BlockSpec(memory_space=pltpu.VMEM)] * 2,
         out_specs=pl.BlockSpec(memory_space=pltpu.VMEM),
         scratch_shapes=[
             pltpu.VMEM((chips, rows, cols), x.dtype),
@@ -119,7 +120,7 @@
             pltpu.SemaphoreType.DMA((chips,)),
         ],
         compiler_params=pltpu.CompilerParams(collective_id=collective_id, has_side_effects=True),
-    )(x.reshape(chips, 2, rows, cols))
+    )(x.reshape(chips, 2, rows, cols), base)
 
 
 def expert_all_gather(x, collective_id):
@@ -399,13 +400,12 @@
         jnp.concatenate([shared_down, returned, returned], axis=0),
         preferred_element_type=f32,
     )
-    total = expert_reduce_scatter(
-        terms.astype(bf16)
-        .reshape(n_group, tok_dev, width_model),
+    return expert_reduce_scatter(
+        terms.astype(bf16).reshape(n_group, tok_dev, width_model),
         4,
-        f32,
+        bf16,
+        embed_own.astype(bf16),
     )
-    return (embed_own + total).astype(bf16)
 
 
 def solution(mesh):

time: 307 us -> 307 us (level)
  no operation moved by 1% of the time
where the time goes in v9:
time: 307 us; the launch traced here: 306 us
  Pallas kernels  113 us (37%)
  waiting for transfers between devices  101 us (33%)
  blocking collectives  27.3 us (9%)
  matrix products  22.2 us (7%)
  local copies, waits for them, and re-layouts  13.8 us (4%)
  between operations  13.7 us (4%)
  starting transfers between devices  9.76 us (3%)
  other arithmetic  5.25 us (2%)
    reduce_scatter x1, waiting for transfers between devices, shards(): lax.psum_scatter(partial_out, 'expert', scatter_dimension=0, tiled=True)  44.3 us
    pallas_call x1, Pallas kernels, fused_projector(): pl.pallas_call(kernel, out_shape=jax.ShapeDtypeStruct((rows, width_model)...  42.3 us
    all_gather x1, waiting for transfers between devices, shards(): lax.all_gather(arrived.reshape(n_rows, width_model), 'expert', axis=0, ti...  42.1 us
    all_to_all x1, blocking collectives, shards(): lax.all_to_all(send, 'dp', split_axis=0, concat_axis=0, tiled=True)  27.3 us
    pallas_call x1, Pallas kernels, dp_all_to_all(): pl.pallas_call(kernel, out_shape=jax.ShapeDtypeStruct(x.shape, x.dtype),...  24.7 us
    pallas_call x1, Pallas kernels, expert_reduce_scatter(): pl.pallas_call(kernel, out_shape=jax.ShapeDtypeStruct((rows, cols), out_d...  24.6 us
    pallas_call x1, Pallas kernels, expert_all_gather(): pl.pallas_call(kernel, out_shape=jax.ShapeDtypeStruct((n, rows, cols), x....  21.6 us
    all_to_all x1, waiting for transfers between devices, shards(): lax.all_to_all(summed.reshape(block), 'dp', split_axis=0, concat_axis=0,...  14.6 us
  transfers between devices with their start and end apart: 3, of which 3 were waited for; matrix products, arithmetic and copies ran while one was open for 2% of the time, Pallas kernels for 0%

profile of v9, /device:TPU:1, one launch (start us, length us, event | category | flops | bytes accessed | tf_op | source)
XLA Modules:
  0.0 306.3 jit_solution(4806745614990626511)
XLA Ops:
  7.3 1.6 sort.17
  9.0 1.4 gather_fusion.1
  11.2 1.3 copy.38.x_ref
  12.5 24.7 %shard_map.136 = bf16[32,1,4736]{2,1,0:T(2,128)(2,1)} custom-call(bf16[32,1,4736]{2,1,0:T(2,128)(2,1)} %copy.38.x_ref), custom_call_target="tpu_custom_call" | custom-call | tf_op jit(solution)/shard_map/pallas_call | solution.py:41
  37.2 1.1 copy.49
  38.7 1.7 copy-done.1
  40.4 42.3 %shard_map.137 = bf16[32,2048]{1,0:T(8,128)(2,1)S(1)} custom-call(bf16[32,4608]{1,0:T(8,128)(2,1)S(1)} %slice.41.f_ref, bf16[4608,256]{1,0:T(8,128)(2,1)S(1)} %copy-done.1, bf16[256,2048]{1,0:T(8,128)(2,1)S(1)} %copy-done.2), custom_call_target="tpu_custom_call" | custom-call | tf_op jit(solution)/shard_map/pallas_call | solution.py:265
  84.7 21.6 %shard_map.138 = bf16[8,64,2176]{2,1,0:T(8,128)(2,1)} custom-call(bf16[64,2176]{1,0:T(8,128)(2,1)} %fusion.37.x_ref), custom_call_target="tpu_custom_call" | custom-call | tf_op jit(solution)/shard_map/pallas_call | solution.py:189
  106.3 0.9 slice.43
  108.9 2.2 convolution_convert_fusion.1
  111.5 27.3 %all_to_all.10 = bf16[32,96,128]{2,1,0:T(8,128)(2,1)S(1)} all-to-all(bf16[32,96,128]{2,1,0:T(8,128)(2,1)S(1)} %reshape.81), channel_id=1, replica_groups=mesh['dp'=32,'expert'=8] {'dp'}, dimensions={0} | all-to-all | bytes 1572864 | tf_op jit(solution)/shard_map/all_to_all | solution.py:379
  138.7 1.3 reshape.82
  140.2 42.1 %all-gather.2.cloned.1.call-done = bf16[1536,2048]{1,0:T(8,128)(2,1)} async-done(((bf16[192,2048]{1,0:T(8,128)(2,1)}), bf16[1536,2048]{1,0:T(8,128)(2,1)}) %all-gather.2.cloned.1.call-update) | async-done | bytes 6291472 | tf_op jit(solution)/shard_map/all_gather | solution.py:380
  182.4 5.4 %fusion.15 = f32[1536,352]{0,1:T(8,128)S(1)} fusion(bf16[1536,2048]{1,0:T(8,128)(2,1)} %all-gather.2.cloned.1.call-done, bf16[2048,176]{0,1:T(8,128)(2,1)S(1)} %bitcast.24, bf16[2048,176]{0,1:T(8,128)(2,1)} %bitcast.25), kind=kOutput, calls=%fused_computation.19 | convolution fusion | flops 2217476096 | bytes 9895936 | tf_op jit(solution)/shard_map/dot_general | solution.py:383
  187.8 4.5 %convolution_convert_fusion = bf16[1536,2048]{1,0:T(8,128)(2,1)} fusion(bf16[1,176,2048]{2,1,0:T(8,128)(2,1)S(1)} %copy-done.12, f32[1536,352]{0,1:T(8,128)S(1)} %fusion.15), kind=kOutput, calls=%fused_computation.2 | convolution fusion | flops 1112064000 | bytes 9175040 | tf_op jit(solution)/shard_map/dot_general | solution.py:388
  192.3 44.3 %reduce-scatter.2.cloned.1.call-done = bf16[192,2048]{1,0:T(8,128)(2,1)} async-done(((bf16[1536,2048]{1,0:T(8,128)(2,1)}), bf16[192,2048]{1,0:T(8,128)(2,1)}) %reduce-scatter.2.cloned.1.call-update) | async-done | bytes 786448 | tf_op jit(solution)/shard_map/reduce_scatter | solution.py:389
  236.6 2.2 reshape.83
  238.8 9.5 %all-to-all-start.1 = ((bf16[32,96,128]{2,1,0:T(8,128)(2,1)}), bf16[32,96,128]{2,1,0:T(8,128)(2,1)S(1)}, u32[]{:S(2)}, u32[]{:S(2)}) async-start(bf16[32,96,128]{2,1,0:T(8,128)(2,1)} %reshape.83), calls=%async_computation.2 | async-start | bytes 1572864 | tf_op jit(solution)/shard_map/all_to_all | solution.py:390
  249.1 2.7 fusion.13
  251.8 1.8 fusion.22
  253.6 14.6 %all-to-all-done.1 = bf16[32,96,128]{2,1,0:T(8,128)(2,1)S(1)} async-done(((bf16[32,96,128]{2,1,0:T(8,128)(2,1)}), bf16[32,96,128]{2,1,0:T(8,128)(2,1)S(1)}, u32[]{:S(2)}, u32[]{:S(2)}) %all-to-all-start.1) | async-done | bytes 786464 | tf_op jit(solution)/shard_map/all_to_all | solution.py:390
  268.5 4.7 %fusion.7 = bf16[512,2048]{1,0:T(8,128)(2,1)} fusion(bf16[192,2048]{1,0:T(8,128)(2,1)S(1)} %reshape.84, bf16[352,2048]{1,0:T(8,128)(2,1)} %param.22, bf16[512,192]{0,1:T(8,128)(2,1)S(1)} %copy-done.6, bf16[512,192]{0,1:T(8,128)(2,1)S(1)} %copy-done.7, bf16[512,352]{0,1:T(8,128)(2,1)} %fusion.22), kind=kOutput, calls=%fused_computation.11 | convolution fusion | flops 1555857408 | bytes 5079040 | tf_op jit(solution)/shard_map/dot_general | solution.py:398
  273.2 24.6 %shard_map.139 = bf16[64,2048]{1,0:T(8,128)(2,1)} custom-call(bf16[4,2,64,2048]{3,2,1,0:T(8,128)(2,1)} %bitcast.21, bf16[64,2048]{1,0:T(8,128)(2,1)} %get-tuple-element.11.b_ref), custom_call_target="tpu_custom_call" | custom-call | tf_op jit(solution)/shard_map/pallas_call | solution.py:108
  297.8 1.7 copy.51
  (66 shorter events, 7.3 us)
Async XLA Ops:
  6.5 242.6 %copy-start = (bf16[2048,352]{0,1:T(8,128)(2,1)S(1)}, bf16[2048,352]{0,1:T(8,128)(2,1)}, u32[]{:S(2)}) copy-start(bf16[2048,352]{0,1:T(8,128)(2,1)} %param.20) | copy-start | bytes 4325380
  6.5 3.8 %copy-start.3 = (bf16[32,4608]{1,0:T(8,128)(2,1)S(1)}, bf16[32,4608]{1,0:T(8,128)(2,1)}, u32[]{:S(2)}) copy-start(bf16[32,4608]{1,0:T(8,128)(2,1)} %param.15) | copy-start | bytes 884740
  6.5 175.8 %all-gather.2.cloned.1.call-start = ((), (), s32[]{:S(2)}) async-start(), calls=%async_computation.3 | async-start | bytes 7077888 | tf_op jit(solution)/shard_map/all_gather | solution.py:380
  11.2 27.3 %copy-start.13 = (s32[64,2]{0,1:T(2,128)S(1)}, s32[64,2]{0,1:T(2,128)}, u32[]{:S(2)}) copy-start(s32[64,2]{0,1:T(2,128)} %param.26) | copy-start | bytes 1540
  11.2 27.3 %copy-start.9 = (s32[64,2]{0,1:T(2,128)S(1)}, s32[64,2]{0,1:T(2,128)}, u32[]{:S(2)}) copy-start(s32[64,2]{0,1:T(2,128)} %param.27) | copy-start | bytes 1540
  11.2 27.6 %copy-start.2 = (bf16[256,2048]{1,0:T(8,128)(2,1)S(1)}, bf16[256,2048]{1,0:T(8,128)(2,1)}, u32[]{:S(2)}) copy-start(bf16[256,2048]{1,0:T(8,128)(2,1)} %wo_ref.1) | copy-start | bytes 3145732
  38.4 44.3 %copy-start.5 = (bf16[64,2048]{1,0:T(8,128)(2,1)S(1)}, bf16[64,2048]{1,0:T(8,128)(2,1)}, u32[]{:S(2)}) copy-start(bf16[64,2048]{1,0:T(8,128)(2,1)} %param.14) | copy-start | bytes 786436
  38.7 1.7 copy-start.1
  40.4 42.8 %copy-start.8 = (f32[2048]{0:T(1024)S(1)}, f32[2048]{0:T(1024)}, u32[]{:S(2)}) copy-start(f32[2048]{0:T(1024)} %param.19) | copy-start | bytes 24580
  138.7 43.6 %copy-start.11 = (bf16[1,2048,176]{1,2,0:T(8,128)(2,1)S(1)}, bf16[1,2048,176]{1,2,0:T(8,128)(2,1)}, u32[]{:S(2)}) copy-start(bf16[1,2048,176]{1,2,0:T(8,128)(2,1)} %param.24) | copy-start | bytes 2162692
  140.0 96.6 %reduce-scatter.2.cloned.1.call-start = ((), (), s32[]{:S(2)}) async-start(), calls=%async_computation.4 | async-start | bytes 7077888 | tf_op jit(solution)/shard_map/reduce_scatter | solution.py:389
  182.3 5.4 %copy-start.12 = (bf16[1,176,2048]{2,1,0:T(8,128)(2,1)S(1)}, bf16[1,176,2048]{2,1,0:T(8,128)(2,1)}, u32[]{:S(2)}) copy-start(bf16[1,176,2048]{2,1,0:T(8,128)(2,1)} %param.25) | copy-start | bytes 2162692
  238.8 29.3 %all-to-all-start.1 = ((bf16[32,96,128]{2,1,0:T(8,128)(2,1)}), bf16[32,96,128]{2,1,0:T(8,128)(2,1)S(1)}, u32[]{:S(2)}, u32[]{:S(2)}) async-start(bf16[32,96,128]{2,1,0:T(8,128)(2,1)} %reshape.83), calls=%async_computation.2 | async-start | bytes 1572864 | tf_op jit(solution)/shard_map/all_to_all | solution.py:390
  249.1 2.7 copy-start.4
  249.1 2.7 copy-start.10
  251.8 16.7 %copy-start.6 = (bf16[512,192]{0,1:T(8,128)(2,1)S(1)}, bf16[512,192]{0,1:T(8,128)(2,1)}, u32[]{:S(2)}) copy-start(bf16[512,192]{0,1:T(8,128)(2,1)} %get-tuple-element.9) | copy-start | bytes 589828
  251.8 16.7 %copy-start.7 = (bf16[512,192]{0,1:T(8,128)(2,1)S(1)}, bf16[512,192]{0,1:T(8,128)(2,1)}, u32[]{:S(2)}) copy-start(bf16[512,192]{0,1:T(8,128)(2,1)} %get-tuple-element.10) | copy-start | bytes 589828
Sparse Core Ops, SparseCore 0:
  140.1 42.1 all-gather.1
  192.5 44.1 reduce-scatter.1

commit v10 on v9

--- a/solution.py
+++ b/solution.py
@@ -326,7 +326,7 @@
     packed = jnp.concatenate(
         [image_feats[order], jnp.broadcast_to(offs_sorted[:, None], (img_dev, pad))], axis=1
     ).reshape(n_data, peer, width_vis + pad)
-    moved = dp_all_to_all(packed, 0)
+    moved = lax.all_to_all(packed, "dp", split_axis=0, concat_axis=0, tiled=True)
     moved = moved.reshape(img_dev, width_vis + pad)
     moved_feats = moved[:, :width_vis]
     moved_offs = moved[:, width_vis].astype(jnp.int32)

time: 307 us -> 303 us (0.987)
  Pallas kernels: 113 us -> 90.7 us
  starting transfers between devices: 9.76 us -> 21.7 us
  waiting for transfers between devices: 101 us -> 111 us
  blocking collectives: 27.3 us -> 24.1 us
    pallas_call x1 -> x0, Pallas kernels: 24.7 us -> none  [dp_all_to_all(): pl.pallas_call(kernel, out_shape=jax.ShapeDtypeStruct(x.shape, x.dtype),...]
    all_to_all x0 -> x1, starting transfers between devices: none -> 11.9 us  [shards(): lax.all_to_all(packed, 'dp', split_axis=0, concat_axis=0, tiled=True)]
    all_to_all x0 -> x1, waiting for transfers between devices: none -> 9.67 us  [shards(): lax.all_to_all(packed, 'dp', split_axis=0, concat_axis=0, tiled=True)]
    all_to_all x1, blocking collectives: 27.3 us -> 24.1 us  [shards(): lax.all_to_all(send, 'dp', split_axis=0, concat_axis=0, tiled=True)]
  transfers between devices with their start and end apart: 3 -> 4, of which waited for: 3 -> 4; matrix products, arithmetic and copies ran while one was open for 2% -> 2% of each run, Pallas kernels for 0% -> 0%
where the time goes in v10:
time: 303 us
  waiting for transfers between devices  111 us (37%)
  Pallas kernels  90.7 us (30%)
  blocking collectives  24.1 us (8%)
  matrix products  22.2 us (7%)
  starting transfers between devices  21.7 us (7%)
  between operations  13.8 us (5%)
  local copies, waits for them, and re-layouts  13.5 us (4%)
  other arithmetic  6.12 us (2%)
    pallas_call x1, Pallas kernels, fused_projector(): pl.pallas_call(kernel, out_shape=jax.ShapeDtypeStruct((rows, width_model)...  44.4 us
    reduce_scatter x1, waiting for transfers between devices, shards(): lax.psum_scatter(partial_out, 'expert', scatter_dimension=0, tiled=True)  44.3 us
    all_gather x1, waiting for transfers between devices, shards(): lax.all_gather(arrived.reshape(n_rows, width_model), 'expert', axis=0, ti...  42.1 us
    pallas_call x1, Pallas kernels, expert_reduce_scatter(): pl.pallas_call(kernel, out_shape=jax.ShapeDtypeStruct((rows, cols), out_d...  24.6 us
    all_to_all x1, blocking collectives, shards(): lax.all_to_all(send, 'dp', split_axis=0, concat_axis=0, tiled=True)  24.1 us
    pallas_call x1, Pallas kernels, expert_all_gather(): pl.pallas_call(kernel, out_shape=jax.ShapeDtypeStruct((n, rows, cols), x....  21.6 us
    all_to_all x1, waiting for transfers between devices, shards(): lax.all_to_all(summed.reshape(block), 'dp', split_axis=0, concat_axis=0,...  14.5 us
    all_to_all x1, starting transfers between devices, shards(): lax.all_to_all(packed, 'dp', split_axis=0, concat_axis=0, tiled=True)  11.9 us
  transfers between devices with their start and end apart: 4, of which 4 were waited for; matrix products, arithmetic and copies ran while one was open for 2% of the time, Pallas kernels for 0%

profile of v10, /device:TPU:1, one launch (start us, length us, event | category | flops | bytes accessed | tf_op | source)
XLA Modules:
  0.0 302.7 jit_solution(14758045809683600628)
XLA Ops:
  7.3 1.6 sort.17
  9.0 1.4 gather_fusion.1
  12.6 1.1 reshape.105
  13.6 11.9 %all-to-all-start = ((bf16[32,2,2368]{2,1,0:T(2,128)(2,1)}), bf16[32,2,2368]{2,1,0:T(2,128)(2,1)S(1)}, u32[]{:S(2)}, u32[]{:S(2)}) async-start(bf16[32,2,2368]{2,1,0:T(2,128)(2,1)} %reshape.105), calls=%async_computation | async-start | bytes 622592 | tf_op jit(solution)/shard_map/all_to_all | solution.py:329
  25.7 9.7 %all-to-all-done = bf16[32,2,2368]{2,1,0:T(2,128)(2,1)S(1)} async-done(((bf16[32,2,2368]{2,1,0:T(2,128)(2,1)}), bf16[32,2,2368]{2,1,0:T(2,128)(2,1)S(1)}, u32[]{:S(2)}, u32[]{:S(2)}) %all-to-all-start) | async-done | bytes 303136 | tf_op jit(solution)/shard_map/all_to_all | solution.py:329
  36.2 1.7 copy-done.1
  37.9 44.4 %shard_map.136 = bf16[32,2048]{1,0:T(8,128)(2,1)S(1)} custom-call(bf16[32,4608]{1,0:T(8,128)(2,1)S(1)} %slice.41.f_ref, bf16[4608,256]{1,0:T(8,128)(2,1)S(1)} %copy-done.1, bf16[256,2048]{1,0:T(8,128)(2,1)S(1)} %copy-done.2), custom_call_target="tpu_custom_call" | custom-call | tf_op jit(solution)/shard_map/pallas_call | solution.py:265
  84.2 21.6 %shard_map.137 = bf16[8,64,2176]{2,1,0:T(8,128)(2,1)} custom-call(bf16[64,2176]{1,0:T(8,128)(2,1)} %fusion.37.x_ref), custom_call_target="tpu_custom_call" | custom-call | tf_op jit(solution)/shard_map/pallas_call | solution.py:189
  105.9 0.9 slice.43
  108.4 2.2 convolution_convert_fusion.1
  111.0 24.1 %all_to_all.15 = bf16[32,96,128]{2,1,0:T(8,128)(2,1)S(1)} all-to-all(bf16[32,96,128]{2,1,0:T(8,128)(2,1)S(1)} %reshape.81), channel_id=1, replica_groups=mesh['dp'=32,'expert'=8] {'dp'}, dimensions={0} | all-to-all | bytes 1572864 | tf_op jit(solution)/shard_map/all_to_all | solution.py:379
  135.1 1.3 reshape.82
  136.6 42.1 %all-gather.2.cloned.1.call-done = bf16[1536,2048]{1,0:T(8,128)(2,1)} async-done(((bf16[192,2048]{1,0:T(8,128)(2,1)}), bf16[1536,2048]{1,0:T(8,128)(2,1)}) %all-gather.2.cloned.1.call-update) | async-done | bytes 6291472 | tf_op jit(solution)/shard_map/all_gather | solution.py:380
  178.8 5.4 %fusion.15 = f32[1536,352]{0,1:T(8,128)S(1)} fusion(bf16[1536,2048]{1,0:T(8,128)(2,1)} %all-gather.2.cloned.1.call-done, bf16[2048,176]{0,1:T(8,128)(2,1)S(1)} %bitcast.24, bf16[2048,176]{0,1:T(8,128)(2,1)} %bitcast.25), kind=kOutput, calls=%fused_computation.19 | convolution fusion | flops 2217476096 | bytes 9895936 | tf_op jit(solution)/shard_map/dot_general | solution.py:383
  184.2 4.5 %convolution_convert_fusion = bf16[1536,2048]{1,0:T(8,128)(2,1)} fusion(bf16[1,176,2048]{2,1,0:T(8,128)(2,1)S(1)} %copy-done.12, f32[1536,352]{0,1:T(8,128)S(1)} %fusion.15), kind=kOutput, calls=%fused_computation.2 | convolution fusion | flops 1112064000 | bytes 9175040 | tf_op jit(solution)/shard_map/dot_general | solution.py:388
  188.7 44.3 %reduce-scatter.2.cloned.1.call-done = bf16[192,2048]{1,0:T(8,128)(2,1)} async-done(((bf16[1536,2048]{1,0:T(8,128)(2,1)}), bf16[192,2048]{1,0:T(8,128)(2,1)}) %reduce-scatter.2.cloned.1.call-update) | async-done | bytes 786448 | tf_op jit(solution)/shard_map/reduce_scatter | solution.py:389
  233.0 2.2 reshape.83
  235.2 9.5 %all-to-all-start.2 = ((bf16[32,96,128]{2,1,0:T(8,128)(2,1)}), bf16[32,96,128]{2,1,0:T(8,128)(2,1)S(1)}, u32[]{:S(2)}, u32[]{:S(2)}) async-start(bf16[32,96,128]{2,1,0:T(8,128)(2,1)} %reshape.83), calls=%async_computation.3 | async-start | bytes 1572864 | tf_op jit(solution)/shard_map/all_to_all | solution.py:390
  245.5 2.7 fusion.13
  248.2 1.8 fusion.22
  250.0 14.5 %all-to-all-done.2 = bf16[32,96,128]{2,1,0:T(8,128)(2,1)S(1)} async-done(((bf16[32,96,128]{2,1,0:T(8,128)(2,1)}), bf16[32,96,128]{2,1,0:T(8,128)(2,1)S(1)}, u32[]{:S(2)}, u32[]{:S(2)}) %all-to-all-start.2) | async-done | bytes 786464 | tf_op jit(solution)/shard_map/all_to_all | solution.py:390
  264.9 4.7 %fusion.7 = bf16[512,2048]{1,0:T(8,128)(2,1)} fusion(bf16[192,2048]{1,0:T(8,128)(2,1)S(1)} %reshape.84, bf16[352,2048]{1,0:T(8,128)(2,1)} %param.22, bf16[512,192]{0,1:T(8,128)(2,1)S(1)} %copy-done.6, bf16[512,192]{0,1:T(8,128)(2,1)S(1)} %copy-done.7, bf16[512,352]{0,1:T(8,128)(2,1)} %fusion.22), kind=kOutput, calls=%fused_computation.11 | convolution fusion | flops 1555857408 | bytes 5079040 | tf_op jit(solution)/shard_map/dot_general | solution.py:398
  269.6 24.6 %shard_map.138 = bf16[64,2048]{1,0:T(8,128)(2,1)} custom-call(bf16[4,2,64,2048]{3,2,1,0:T(8,128)(2,1)} %bitcast.21, bf16[64,2048]{1,0:T(8,128)(2,1)} %get-tuple-element.11.b_ref), custom_call_target="tpu_custom_call" | custom-call | tf_op jit(solution)/shard_map/pallas_call | solution.py:108
  294.2 1.7 copy.53
  (70 shorter events, 9.2 us)
Async XLA Ops:
  6.5 239.0 %copy-start = (bf16[2048,352]{0,1:T(8,128)(2,1)S(1)}, bf16[2048,352]{0,1:T(8,128)(2,1)}, u32[]{:S(2)}) copy-start(bf16[2048,352]{0,1:T(8,128)(2,1)} %param.20) | copy-start | bytes 4325380
  6.5 3.8 %copy-start.3 = (bf16[32,4608]{1,0:T(8,128)(2,1)S(1)}, bf16[32,4608]{1,0:T(8,128)(2,1)}, u32[]{:S(2)}) copy-start(bf16[32,4608]{1,0:T(8,128)(2,1)} %param.15) | copy-start | bytes 884740
  10.3 15.2 %copy-start.13 = (s32[64,2]{0,1:T(2,128)S(1)}, s32[64,2]{0,1:T(2,128)}, u32[]{:S(2)}) copy-start(s32[64,2]{0,1:T(2,128)} %param.26) | copy-start | bytes 1540
  10.4 15.2 %copy-start.9 = (s32[64,2]{0,1:T(2,128)S(1)}, s32[64,2]{0,1:T(2,128)}, u32[]{:S(2)}) copy-start(s32[64,2]{0,1:T(2,128)} %param.27) | copy-start | bytes 1540
  11.7 24.5 %copy-start.2 = (bf16[256,2048]{1,0:T(8,128)(2,1)S(1)}, bf16[256,2048]{1,0:T(8,128)(2,1)}, u32[]{:S(2)}) copy-start(bf16[256,2048]{1,0:T(8,128)(2,1)} %wo_ref.1) | copy-start | bytes 3145732
  13.6 21.8 %all-to-all-start = ((bf16[32,2,2368]{2,1,0:T(2,128)(2,1)}), bf16[32,2,2368]{2,1,0:T(2,128)(2,1)S(1)}, u32[]{:S(2)}, u32[]{:S(2)}) async-start(bf16[32,2,2368]{2,1,0:T(2,128)(2,1)} %reshape.105), calls=%async_computation | async-start | bytes 622592 | tf_op jit(solution)/shard_map/all_to_all | solution.py:329
  25.5 153.2 %all-gather.2.cloned.1.call-start = ((), (), s32[]{:S(2)}) async-start(), calls=%async_computation.4 | async-start | bytes 7077888 | tf_op jit(solution)/shard_map/all_gather | solution.py:380
  36.0 46.2 %copy-start.5 = (bf16[64,2048]{1,0:T(8,128)(2,1)S(1)}, bf16[64,2048]{1,0:T(8,128)(2,1)}, u32[]{:S(2)}) copy-start(bf16[64,2048]{1,0:T(8,128)(2,1)} %param.14) | copy-start | bytes 786436
  36.2 1.7 copy-start.1
  37.9 44.9 %copy-start.8 = (f32[2048]{0:T(1024)S(1)}, f32[2048]{0:T(1024)}, u32[]{:S(2)}) copy-start(f32[2048]{0:T(1024)} %param.19) | copy-start | bytes 24580
  135.1 43.6 %copy-start.11 = (bf16[1,2048,176]{1,2,0:T(8,128)(2,1)S(1)}, bf16[1,2048,176]{1,2,0:T(8,128)(2,1)}, u32[]{:S(2)}) copy-start(bf16[1,2048,176]{1,2,0:T(8,128)(2,1)} %param.24) | copy-start | bytes 2162692
  136.4 96.6 %reduce-scatter.2.cloned.1.call-start = ((), (), s32[]{:S(2)}) async-start(), calls=%async_computation.5 | async-start | bytes 7077888 | tf_op jit(solution)/shard_map/reduce_scatter | solution.py:389
  178.7 5.4 %copy-start.12 = (bf16[1,176,2048]{2,1,0:T(8,128)(2,1)S(1)}, bf16[1,176,2048]{2,1,0:T(8,128)(2,1)}, u32[]{:S(2)}) copy-start(bf16[1,176,2048]{2,1,0:T(8,128)(2,1)} %param.25) | copy-start | bytes 2162692
  235.2 29.3 %all-to-all-start.2 = ((bf16[32,96,128]{2,1,0:T(8,128)(2,1)}), bf16[32,96,128]{2,1,0:T(8,128)(2,1)S(1)}, u32[]{:S(2)}, u32[]{:S(2)}) async-start(bf16[32,96,128]{2,1,0:T(8,128)(2,1)} %reshape.83), calls=%async_computation.3 | async-start | bytes 1572864 | tf_op jit(solution)/shard_map/all_to_all | solution.py:390
  245.5 2.7 copy-start.4
  245.5 2.7 copy-start.10
  248.2 16.7 %copy-start.6 = (bf16[512,192]{0,1:T(8,128)(2,1)S(1)}, bf16[512,192]{0,1:T(8,128)(2,1)}, u32[]{:S(2)}) copy-start(bf16[512,192]{0,1:T(8,128)(2,1)} %get-tuple-element.9) | copy-start | bytes 589828
  248.2 16.7 %copy-start.7 = (bf16[512,192]{0,1:T(8,128)(2,1)S(1)}, bf16[512,192]{0,1:T(8,128)(2,1)}, u32[]{:S(2)}) copy-start(bf16[512,192]{0,1:T(8,128)(2,1)} %get-tuple-element.10) | copy-start | bytes 589828
Sparse Core Ops, SparseCore 0:
  136.5 42.1 all-gather.1
  188.9 44.1 reduce-scatter.1

commit v11 on v10

--- a/solution.py
+++ b/solution.py
@@ -206,60 +206,98 @@
 def fused_projector(feats, proj_in, proj_out, collective_id):
     rows, width_vis = feats.shape
     n = lax.axis_size("expert")
+    chips = n // 2
     width_model = proj_out.shape[1]
     mesh_ids = pl.DeviceIdType.MESH
     f32, bf16 = jnp.float32, jnp.bfloat16
 
-    def kernel(f_ref, wi_ref, wo_ref, o_ref, fbuf, psend, pbuf, send_f, recv_f, send_p, recv_p):
+    def kernel(
+        f_ref, wi_ref, wo_ref, o_ref, fbuf, psend, pbuf,
+        send_n, recv_n, send_f, recv_f, send_r, recv_r, send_p, recv_p,
+    ):
         me = lax.axis_index("expert")
         row = lax.axis_index("dp")
+        chip, core = me // 2, me % 2
+        sibling = chip * 2 + 1 - core
         barrier = pltpu.get_barrier_semaphore()
         for k in range(1, n):
             pl.semaphore_signal(
                 barrier, inc=1, device_id=(row, lax.rem(me + k, n)), device_id_type=mesh_ids
             )
         pl.semaphore_wait(barrier, n - 1)
-        feat_copies = []
-        for k in range(1, n):
+        near = pltpu.make_async_remote_copy(
+            src_ref=f_ref,
+            dst_ref=fbuf.at[me],
+            send_sem=send_n,
+            recv_sem=recv_n,
+            device_id=(row, sibling),
+            device_id_type=mesh_ids,
+        )
+        near.start()
+        far = []
+        for k in range(1, chips):
             copy = pltpu.make_async_remote_copy(
                 src_ref=f_ref,
                 dst_ref=fbuf.at[me],
                 send_sem=send_f.at[k],
                 recv_sem=recv_f.at[k],
-                device_id=(row, lax.rem(me + k, n)),
+                device_id=(row, lax.rem(chip + k, chips) * 2 + core),
                 device_id_type=mesh_ids,
             )
             copy.start()
-            feat_copies.append(copy)
+            far.append(copy)
 
         def partial(x):
             hidden = jnp.dot(x, wi_ref[...], preferred_element_type=f32)
             hidden = jax.nn.gelu(hidden, approximate=True).astype(bf16)
             return jnp.dot(hidden, wo_ref[...], preferred_element_type=f32)
 
+        backs = []
+
+        def answer(index, source):
+            psend[index] = partial(fbuf[source]).astype(bf16)
+            back = pltpu.make_async_remote_copy(
+                src_ref=psend.at[index],
+                dst_ref=pbuf.at[index],
+                send_sem=send_p.at[index],
+                recv_sem=recv_p.at[index],
+                device_id=(row, source),
+                device_id_type=mesh_ids,
+            )
+            back.start()
+            backs.append(back)
+
         acc = partial(f_ref[...])
-        part_copies = []
-        for k, copy in enumerate(feat_copies, 1):
+        near.wait_recv()
+        answer(0, sibling)
+        relays = []
+        for k, copy in enumerate(far, 1):
             copy.wait_recv()
-            source = lax.rem(me - k + n, n)
-            psend[k] = partial(fbuf[source]).astype(bf16)
-            back = pltpu.make_async_remote_copy(
-                src_ref=psend.at[k],
-                dst_ref=pbuf.at[k],
-                send_sem=send_p.at[k],
-                recv_sem=recv_p.at[k],
-                device_id=(row, source),
-                device_id_type=mesh_ids,
-            )
-            back.start()
-            part_copies.append(back)
-        for k, back in enumerate(part_copies, 1):
+            source = lax.rem(chip - k + chips, chips) * 2 + core
+            relay = pltpu.make_async_remote_copy(
+                src_ref=fbuf.at[source],
+                dst_ref=fbuf.at[source],
+                send_sem=send_r.at[k],
+                recv_sem=recv_r.at[k],
+                device_id=(row, sibling),
+                device_id_type=mesh_ids,
+            )
+            relay.start()
+            relays.append(relay)
+            answer(k, source)
+        for k, relay in enumerate(relays, 1):
+            relay.wait_recv()
+            answer(chips - 1 + k, lax.rem(chip - k + chips, chips) * 2 + 1 - core)
+        for index, back in enumerate(backs):
             back.wait_recv()
-            acc = acc + pbuf[k].astype(f32)
+            acc = acc + pbuf[index].astype(f32)
         o_ref[...] = acc.astype(o_ref.dtype)
-        for copy in feat_copies:
+        near.wait_send()
+        for copy in far:
             copy.wait_send()
-        for back in part_copies:
+        for relay in relays:
+            relay.wait_send()
+        for back in backs:
             back.wait_send()
 
     return pl.pallas_call(
@@ -271,8 +309,12 @@
             pltpu.VMEM((n, rows, width_vis), feats.dtype),
             pltpu.VMEM((n, rows, width_model), bf16),
             pltpu.VMEM((n, rows, width_model), bf16),
-            pltpu.SemaphoreType.DMA((n,)),
-            pltpu.SemaphoreType.DMA((n,)),
+            pltpu.SemaphoreType.DMA,
+            pltpu.SemaphoreType.DMA,
+            pltpu.SemaphoreType.DMA((chips,)),
+            pltpu.SemaphoreType.DMA((chips,)),
+            pltpu.SemaphoreType.DMA((chips,)),
+            pltpu.SemaphoreType.DMA((chips,)),
             pltpu.SemaphoreType.DMA((n,)),
             pltpu.SemaphoreType.DMA((n,)),
         ],

time: 303 us -> 294 us (0.970)
  Pallas kernels: 90.7 us -> 82.3 us
    pallas_call x1, Pallas kernels: 44.4 us -> 37.2 us  [fused_projector(): pl.pallas_call(kernel, out_shape=jax.ShapeDtypeStruct((rows, width_model)...]
where the time goes in v11:
time: 294 us
  waiting for transfers between devices  110 us (37%)
  Pallas kernels  82.3 us (28%)
  blocking collectives  24.1 us (8%)
  matrix products  22.2 us (8%)
  starting transfers between devices  21.7 us (7%)
  between operations  13.8 us (5%)
  local copies, waits for them, and re-layouts  13.5 us (5%)
  other arithmetic  6.12 us (2%)
    reduce_scatter x1, waiting for transfers between devices, shards(): lax.psum_scatter(partial_out, 'expert', scatter_dimension=0, tiled=True)  44.3 us
    all_gather x1, waiting for transfers between devices, shards(): lax.all_gather(arrived.reshape(n_rows, width_model), 'expert', axis=0, ti...  41.6 us
    pallas_call x1, Pallas kernels, fused_projector(): pl.pallas_call(kernel, out_shape=jax.ShapeDtypeStruct((rows, width_model)...  37.2 us
    pallas_call x1, Pallas kernels, expert_reduce_scatter(): pl.pallas_call(kernel, out_shape=jax.ShapeDtypeStruct((rows, cols), out_d...  24.6 us
    all_to_all x1, blocking collectives, shards(): lax.all_to_all(send, 'dp', split_axis=0, concat_axis=0, tiled=True)  24.1 us
    pallas_call x1, Pallas kernels, expert_all_gather(): pl.pallas_call(kernel, out_shape=jax.ShapeDtypeStruct((n, rows, cols), x....  20.5 us
    all_to_all x1, waiting for transfers between devices, shards(): lax.all_to_all(summed.reshape(block), 'dp', split_axis=0, concat_axis=0,...  14.5 us
    all_to_all x1, starting transfers between devices, shards(): lax.all_to_all(packed, 'dp', split_axis=0, concat_axis=0, tiled=True)  11.9 us
  transfers between devices with their start and end apart: 4, of which 4 were waited for; matrix products, arithmetic and copies ran while one was open for 2% of the time, Pallas kernels for 0%

profile of v11, /device:TPU:1, one launch (start us, length us, event | category | flops | bytes accessed | tf_op | source)
XLA Modules:
  0.0 293.9 jit_solution(7277057266683224339)
XLA Ops:
  7.3 1.6 sort.17
  9.0 1.4 gather_fusion.1
  12.6 1.1 reshape.105
  13.6 11.9 %all-to-all-start = ((bf16[32,2,2368]{2,1,0:T(2,128)(2,1)}), bf16[32,2,2368]{2,1,0:T(2,128)(2,1)S(1)}, u32[]{:S(2)}, u32[]{:S(2)}) async-start(bf16[32,2,2368]{2,1,0:T(2,128)(2,1)} %reshape.105), calls=%async_computation | async-start | bytes 622592 | tf_op jit(solution)/shard_map/all_to_all | solution.py:371
  25.7 9.7 %all-to-all-done = bf16[32,2,2368]{2,1,0:T(2,128)(2,1)S(1)} async-done(((bf16[32,2,2368]{2,1,0:T(2,128)(2,1)}), bf16[32,2,2368]{2,1,0:T(2,128)(2,1)S(1)}, u32[]{:S(2)}, u32[]{:S(2)}) %all-to-all-start) | async-done | bytes 303136 | tf_op jit(solution)/shard_map/all_to_all | solution.py:371
  36.2 1.7 copy-done.1
  37.9 37.2 %shard_map.136 = bf16[32,2048]{1,0:T(8,128)(2,1)S(1)} custom-call(bf16[32,4608]{1,0:T(8,128)(2,1)S(1)} %slice.41.f_ref, bf16[4608,256]{1,0:T(8,128)(2,1)S(1)} %copy-done.1, bf16[256,2048]{1,0:T(8,128)(2,1)S(1)} %copy-done.2), custom_call_target="tpu_custom_call" | custom-call | tf_op jit(solution)/shard_map/pallas_call | solution.py:303
  77.0 20.5 %shard_map.137 = bf16[8,64,2176]{2,1,0:T(8,128)(2,1)} custom-call(bf16[64,2176]{1,0:T(8,128)(2,1)} %fusion.37.x_ref), custom_call_target="tpu_custom_call" | custom-call | tf_op jit(solution)/shard_map/pallas_call | solution.py:189
  97.5 0.9 slice.43
  100.1 2.2 convolution_convert_fusion.1
  102.7 24.1 %all_to_all.15 = bf16[32,96,128]{2,1,0:T(8,128)(2,1)S(1)} all-to-all(bf16[32,96,128]{2,1,0:T(8,128)(2,1)S(1)} %reshape.81), channel_id=1, replica_groups=mesh['dp'=32,'expert'=8] {'dp'}, dimensions={0} | all-to-all | bytes 1572864 | tf_op jit(solution)/shard_map/all_to_all | solution.py:421
  126.8 1.3 reshape.82
  128.3 41.6 %all-gather.2.cloned.1.call-done = bf16[1536,2048]{1,0:T(8,128)(2,1)} async-done(((bf16[192,2048]{1,0:T(8,128)(2,1)}), bf16[1536,2048]{1,0:T(8,128)(2,1)}) %all-gather.2.cloned.1.call-update) | async-done | bytes 6291472 | tf_op jit(solution)/shard_map/all_gather | solution.py:422
  169.9 5.4 %fusion.15 = f32[1536,352]{0,1:T(8,128)S(1)} fusion(bf16[1536,2048]{1,0:T(8,128)(2,1)} %all-gather.2.cloned.1.call-done, bf16[2048,176]{0,1:T(8,128)(2,1)S(1)} %bitcast.24, bf16[2048,176]{0,1:T(8,128)(2,1)} %bitcast.25), kind=kOutput, calls=%fused_computation.19 | convolution fusion | flops 2217476096 | bytes 9895936 | tf_op jit(solution)/shard_map/dot_general | solution.py:425
  175.4 4.5 %convolution_convert_fusion = bf16[1536,2048]{1,0:T(8,128)(2,1)} fusion(bf16[1,176,2048]{2,1,0:T(8,128)(2,1)S(1)} %copy-done.12, f32[1536,352]{0,1:T(8,128)S(1)} %fusion.15), kind=kOutput, calls=%fused_computation.2 | convolution fusion | flops 1112064000 | bytes 9175040 | tf_op jit(solution)/shard_map/dot_general | solution.py:430
  179.9 44.3 %reduce-scatter.2.cloned.1.call-done = bf16[192,2048]{1,0:T(8,128)(2,1)} async-done(((bf16[1536,2048]{1,0:T(8,128)(2,1)}), bf16[192,2048]{1,0:T(8,128)(2,1)}) %reduce-scatter.2.cloned.1.call-update) | async-done | bytes 786448 | tf_op jit(solution)/shard_map/reduce_scatter | solution.py:431
  224.2 2.2 reshape.83
  226.4 9.5 %all-to-all-start.2 = ((bf16[32,96,128]{2,1,0:T(8,128)(2,1)}), bf16[32,96,128]{2,1,0:T(8,128)(2,1)S(1)}, u32[]{:S(2)}, u32[]{:S(2)}) async-start(bf16[32,96,128]{2,1,0:T(8,128)(2,1)} %reshape.83), calls=%async_computation.3 | async-start | bytes 1572864 | tf_op jit(solution)/shard_map/all_to_all | solution.py:432
  236.7 2.7 fusion.13
  239.4 1.8 fusion.22
  241.2 14.5 %all-to-all-done.2 = bf16[32,96,128]{2,1,0:T(8,128)(2,1)S(1)} async-done(((bf16[32,96,128]{2,1,0:T(8,128)(2,1)}), bf16[32,96,128]{2,1,0:T(8,128)(2,1)S(1)}, u32[]{:S(2)}, u32[]{:S(2)}) %all-to-all-start.2) | async-done | bytes 786464 | tf_op jit(solution)/shard_map/all_to_all | solution.py:432
  256.1 4.7 %fusion.7 = bf16[512,2048]{1,0:T(8,128)(2,1)} fusion(bf16[192,2048]{1,0:T(8,128)(2,1)S(1)} %reshape.84, bf16[352,2048]{1,0:T(8,128)(2,1)} %param.22, bf16[512,192]{0,1:T(8,128)(2,1)S(1)} %copy-done.6, bf16[512,192]{0,1:T(8,128)(2,1)S(1)} %copy-done.7, bf16[512,352]{0,1:T(8,128)(2,1)} %fusion.22), kind=kOutput, calls=%fused_computation.11 | convolution fusion | flops 1555857408 | bytes 5079040 | tf_op jit(solution)/shard_map/dot_general | solution.py:440
  260.7 24.6 %shard_map.138 = bf16[64,2048]{1,0:T(8,128)(2,1)} custom-call(bf16[4,2,64,2048]{3,2,1,0:T(8,128)(2,1)} %bitcast.21, bf16[64,2048]{1,0:T(8,128)(2,1)} %get-tuple-element.11.b_ref), custom_call_target="tpu_custom_call" | custom-call | tf_op jit(solution)/shard_map/pallas_call | solution.py:108
  285.4 1.7 copy.53
  (70 shorter events, 9.2 us)
Async XLA Ops:
  6.5 230.2 %copy-start = (bf16[2048,352]{0,1:T(8,128)(2,1)S(1)}, bf16[2048,352]{0,1:T(8,128)(2,1)}, u32[]{:S(2)}) copy-start(bf16[2048,352]{0,1:T(8,128)(2,1)} %param.20) | copy-start | bytes 4325380
  6.5 3.8 %copy-start.3 = (bf16[32,4608]{1,0:T(8,128)(2,1)S(1)}, bf16[32,4608]{1,0:T(8,128)(2,1)}, u32[]{:S(2)}) copy-start(bf16[32,4608]{1,0:T(8,128)(2,1)} %param.15) | copy-start | bytes 884740
  10.3 15.2 %copy-start.13 = (s32[64,2]{0,1:T(2,128)S(1)}, s32[64,2]{0,1:T(2,128)}, u32[]{:S(2)}) copy-start(s32[64,2]{0,1:T(2,128)} %param.26) | copy-start | bytes 1540
  10.4 15.2 %copy-start.9 = (s32[64,2]{0,1:T(2,128)S(1)}, s32[64,2]{0,1:T(2,128)}, u32[]{:S(2)}) copy-start(s32[64,2]{0,1:T(2,128)} %param.27) | copy-start | bytes 1540
  11.7 24.5 %copy-start.2 = (bf16[256,2048]{1,0:T(8,128)(2,1)S(1)}, bf16[256,2048]{1,0:T(8,128)(2,1)}, u32[]{:S(2)}) copy-start(bf16[256,2048]{1,0:T(8,128)(2,1)} %wo_ref.1) | copy-start | bytes 3145732
  13.6 21.8 %all-to-all-start = ((bf16[32,2,2368]{2,1,0:T(2,128)(2,1)}), bf16[32,2,2368]{2,1,0:T(2,128)(2,1)S(1)}, u32[]{:S(2)}, u32[]{:S(2)}) async-start(bf16[32,2,2368]{2,1,0:T(2,128)(2,1)} %reshape.105), calls=%async_computation | async-start | bytes 622592 | tf_op jit(solution)/shard_map/all_to_all | solution.py:371
  25.5 144.4 %all-gather.2.cloned.1.call-start = ((), (), s32[]{:S(2)}) async-start(), calls=%async_computation.4 | async-start | bytes 7077888 | tf_op jit(solution)/shard_map/all_gather | solution.py:422
  36.0 39.0 %copy-start.5 = (bf16[64,2048]{1,0:T(8,128)(2,1)S(1)}, bf16[64,2048]{1,0:T(8,128)(2,1)}, u32[]{:S(2)}) copy-start(bf16[64,2048]{1,0:T(8,128)(2,1)} %param.14) | copy-start | bytes 786436
  36.2 1.7 copy-start.1
  37.9 37.7 %copy-start.8 = (f32[2048]{0:T(1024)S(1)}, f32[2048]{0:T(1024)}, u32[]{:S(2)}) copy-start(f32[2048]{0:T(1024)} %param.19) | copy-start | bytes 24580
  126.8 43.2 %copy-start.11 = (bf16[1,2048,176]{1,2,0:T(8,128)(2,1)S(1)}, bf16[1,2048,176]{1,2,0:T(8,128)(2,1)}, u32[]{:S(2)}) copy-start(bf16[1,2048,176]{1,2,0:T(8,128)(2,1)} %param.24) | copy-start | bytes 2162692
  128.1 96.1 %reduce-scatter.2.cloned.1.call-start = ((), (), s32[]{:S(2)}) async-start(), calls=%async_computation.5 | async-start | bytes 7077888 | tf_op jit(solution)/shard_map/reduce_scatter | solution.py:431
  169.9 5.4 %copy-start.12 = (bf16[1,176,2048]{2,1,0:T(8,128)(2,1)S(1)}, bf16[1,176,2048]{2,1,0:T(8,128)(2,1)}, u32[]{:S(2)}) copy-start(bf16[1,176,2048]{2,1,0:T(8,128)(2,1)} %param.25) | copy-start | bytes 2162692
  226.4 29.3 %all-to-all-start.2 = ((bf16[32,96,128]{2,1,0:T(8,128)(2,1)}), bf16[32,96,128]{2,1,0:T(8,128)(2,1)S(1)}, u32[]{:S(2)}, u32[]{:S(2)}) async-start(bf16[32,96,128]{2,1,0:T(8,128)(2,1)} %reshape.83), calls=%async_computation.3 | async-start | bytes 1572864 | tf_op jit(solution)/shard_map/all_to_all | solution.py:432
  236.7 2.7 copy-start.4
  236.7 2.7 copy-start.10
  239.4 16.7 %copy-start.6 = (bf16[512,192]{0,1:T(8,128)(2,1)S(1)}, bf16[512,192]{0,1:T(8,128)(2,1)}, u32[]{:S(2)}) copy-start(bf16[512,192]{0,1:T(8,128)(2,1)} %get-tuple-element.9) | copy-start | bytes 589828
  239.4 16.7 %copy-start.7 = (bf16[512,192]{0,1:T(8,128)(2,1)S(1)}, bf16[512,192]{0,1:T(8,128)(2,1)}, u32[]{:S(2)}) copy-start(bf16[512,192]{0,1:T(8,128)(2,1)} %get-tuple-element.10) | copy-start | bytes 589828
Sparse Core Ops, SparseCore 0:
  128.2 41.6 all-gather.1
  180.0 44.1 reduce-scatter.1

commit v12 on v11

--- a/solution.py
+++ b/solution.py
@@ -381,13 +381,33 @@
     placed = select_dot(place, projected)
     has_image = jnp.sum(place.astype(f32), axis=1, keepdims=True) > 0
     embed_own = jnp.where(has_image, placed, text_embed.astype(f32))
-    normed_own = normalize(embed_own, norm_gain)
-
-    gathered = expert_all_gather(
-        jnp.concatenate([normed_own, route_cols.astype(bf16)], axis=1), 6
-    ).reshape(n_group * tok_dev, width_model + route_cols.shape[1])
-    normed = gathered[:, :width_model]
-    routes = gathered[:, width_model:].astype(f32)
+
+    text_gathered = lax.all_gather(
+        jnp.concatenate([normalize(text_embed, norm_gain), route_cols.astype(bf16)], axis=1),
+        "expert",
+        axis=0,
+        tiled=True,
+    )
+    image_block = jnp.concatenate(
+        [
+            normalize(projected, norm_gain),
+            jnp.broadcast_to(moved_offs.astype(bf16)[:, None], (img_dev, pad)),
+        ],
+        axis=1,
+    )
+    image_rows = expert_all_gather(image_block, 6)
+    group_offs = image_rows[:, :, width_model].astype(jnp.int32)
+    spot = (
+        group_offs[:, None, :] == jnp.arange(tok_dev, dtype=jnp.int32)[None, :, None]
+    ).astype(bf16)
+    image_placed = jnp.einsum(
+        "gri,gid->grd", spot, image_rows[:, :, :width_model], preferred_element_type=f32
+    ).reshape(n_group * tok_dev, width_model)
+    image_here = (jnp.sum(spot.astype(f32), axis=2) > 0).reshape(n_group * tok_dev, 1)
+    normed = jnp.where(
+        image_here, image_placed, text_gathered[:, :width_model].astype(f32)
+    ).astype(bf16)
+    routes = text_gathered[:, width_model:].astype(f32)
     top_count = route_ids.shape[1]
     ids = routes[:, :top_count].astype(jnp.int32)
     weights_f = routes[:, top_count : 2 * top_count] * 256.0 + routes[:, 2 * top_count : 3 * top_count]

time: 294 us -> 299 us (1.017)
  other arithmetic: 6.12 us -> 16.3 us
  Pallas kernels: 82.3 us -> 75.5 us
    pallas_call x1, Pallas kernels: 20.5 us -> 13.7 us  [expert_all_gather(): pl.pallas_call(kernel, out_shape=jax.ShapeDtypeStruct((n, rows, cols), x....]
    convert_element_type x2 -> x6, other arithmetic: 0.77 us -> 6.05 us  [the longest x1 2.77 us: shards(): normed = jnp.where(image_here, image_placed, text_gathered[:, :width_mode...]
    dot_general x0 -> x1, matrix products: none -> 3.35 us  [shards(): jnp.einsum('gri,gid->grd', spot, image_rows[:, :, :width_model], preferre...]
    unnamed x33 -> x32, local copies, waits for them, and re-layouts: 5.05 us -> 6.38 us
  transfers between devices with their start and end apart: 4 -> 5, of which waited for: 4 -> 4; matrix products, arithmetic and copies ran while one was open for 2% -> 7% of each run, Pallas kernels for 0% -> 17%
where the time goes in v12:
time: 299 us; the launch traced here: 298 us
  waiting for transfers between devices  109 us (36%)
  Pallas kernels  75.5 us (25%)
  matrix products  24.5 us (8%)
  blocking collectives  24.3 us (8%)
  starting transfers between devices  21.5 us (7%)
  other arithmetic  16.3 us (5%)
  local copies, waits for them, and re-layouts  14.1 us (5%)
  between operations  13.5 us (5%)
    reduce_scatter x1, waiting for transfers between devices, shards(): lax.psum_scatter(partial_out, 'expert', scatter_dimension=0, tiled=True)  43.4 us
    all_gather x1, waiting for transfers between devices, shards(): lax.all_gather(arrived.reshape(n_rows, width_model), 'expert', axis=0, ti...  42 us
    pallas_call x1, Pallas kernels, fused_projector(): pl.pallas_call(kernel, out_shape=jax.ShapeDtypeStruct((rows, width_model)...  37.1 us
    pallas_call x1, Pallas kernels, expert_reduce_scatter(): pl.pallas_call(kernel, out_shape=jax.ShapeDtypeStruct((rows, cols), out_d...  24.6 us
    all_to_all x1, blocking collectives, shards(): lax.all_to_all(send, 'dp', split_axis=0, concat_axis=0, tiled=True)  24.3 us
    pallas_call x1, Pallas kernels, expert_all_gather(): pl.pallas_call(kernel, out_shape=jax.ShapeDtypeStruct((n, rows, cols), x....  13.7 us
    all_to_all x1, waiting for transfers between devices, shards(): lax.all_to_all(summed.reshape(block), 'dp', split_axis=0, concat_axis=0,...  13.4 us
    all_to_all x1, starting transfers between devices, shards(): lax.all_to_all(packed, 'dp', split_axis=0, concat_axis=0, tiled=True)  11.9 us
  transfers between devices with their start and end apart: 5, of which 4 were waited for; matrix products, arithmetic and copies ran while one was open for 7% of the time, Pallas kernels for 17%

profile of v12, /device:TPU:1, one launch (start us, length us, event | category | flops | bytes accessed | tf_op | source)
XLA Modules:
  0.0 298.4 jit_solution(16679875629740027214)
XLA Ops:
  11.8 1.6 sort.17
  13.5 1.4 gather_fusion.1
  18.1 11.9 %all-to-all-start = ((bf16[32,2,2368]{2,1,0:T(2,128)(2,1)}), bf16[32,2,2368]{2,1,0:T(2,128)(2,1)S(1)}, u32[]{:S(2)}, u32[]{:S(2)}) async-start(bf16[32,2,2368]{2,1,0:T(2,128)(2,1)} %reshape.131), calls=%async_computation | async-start | bytes 622592 | tf_op jit(solution)/shard_map/all_to_all | solution.py:371
  30.0 9.9 %all-to-all-done = bf16[32,2,2368]{2,1,0:T(2,128)(2,1)S(1)} async-done(((bf16[32,2,2368]{2,1,0:T(2,128)(2,1)}), bf16[32,2,2368]{2,1,0:T(2,128)(2,1)S(1)}, u32[]{:S(2)}, u32[]{:S(2)}) %all-to-all-start) | async-done | bytes 303136 | tf_op jit(solution)/shard_map/all_to_all | solution.py:371
  40.5 1.8 copy-done.1
  42.2 37.1 %shard_map.136 = bf16[32,2048]{1,0:T(8,128)(2,1)S(1)} custom-call(bf16[32,4608]{1,0:T(8,128)(2,1)S(1)} %slice.48.f_ref, bf16[4608,256]{1,0:T(8,128)(2,1)S(1)} %copy-done.1, bf16[256,2048]{1,0:T(8,128)(2,1)S(1)} %copy-done.2), custom_call_target="tpu_custom_call" | custom-call | tf_op jit(solution)/shard_map/pallas_call | solution.py:303
  80.5 13.7 %shard_map.137 = bf16[8,32,2176]{2,1,0:T(8,128)(2,1)} custom-call(bf16[32,2176]{1,0:T(8,128)(2,1)} %pad_maximum_fusion.x_ref), custom_call_target="tpu_custom_call" | custom-call | tf_op jit(solution)/shard_map/pallas_call | solution.py:189
  95.5 3.3 %fusion.20 = bf16[8,64,2048]{2,1,0:T(8,128)(2,1)} fusion(bf16[8,32,2176]{2,1,0:T(8,128)(2,1)} %shard_map.137, s32[8,32]{1,0:T(8,128)S(1)} %convert_reduce_fusion.1), kind=kOutput, calls=%fused_computation.27 | convolution fusion | flops 67125248 | bytes 3146752 | tf_op jit(solution)/shard_map/gri,gid->grd/dot_general | solution.py:403
  102.0 2.8 fusion
  104.8 1.3 copy-done.4
  107.1 24.3 %all_to_all.15 = bf16[32,96,128]{2,1,0:T(8,128)(2,1)S(1)} all-to-all(bf16[32,96,128]{2,1,0:T(8,128)(2,1)S(1)} %reshape.104), channel_id=1, replica_groups=mesh['dp'=32,'expert'=8] {'dp'}, dimensions={0} | all-to-all | bytes 1572864 | tf_op jit(solution)/shard_map/all_to_all | solution.py:441
  131.4 1.3 reshape.105
  132.7 42.0 %all-gather.5.cloned.1.call-done = bf16[1536,2048]{1,0:T(8,128)(2,1)} async-done(((bf16[192,2048]{1,0:T(8,128)(2,1)}), bf16[1536,2048]{1,0:T(8,128)(2,1)}) %all-gather.5.cloned.1.call-update) | async-done | bytes 6291472 | tf_op jit(solution)/shard_map/all_gather | solution.py:442
  174.7 5.4 %fusion.12 = f32[1536,352]{0,1:T(8,128)S(1)} fusion(bf16[1536,2048]{1,0:T(8,128)(2,1)} %all-gather.5.cloned.1.call-done, bf16[2048,176]{0,1:T(8,128)(2,1)S(1)} %bitcast.27, bf16[2048,176]{0,1:T(8,128)(2,1)} %bitcast.28), kind=kOutput, calls=%fused_computation.17 | convolution fusion | flops 2217476096 | bytes 9895936 | tf_op jit(solution)/shard_map/dot_general | solution.py:445
  180.2 4.5 %convolution_convert_fusion = bf16[1536,2048]{1,0:T(8,128)(2,1)} fusion(bf16[1,176,2048]{2,1,0:T(8,128)(2,1)S(1)} %copy-done.13, f32[1536,352]{0,1:T(8,128)S(1)} %fusion.12), kind=kOutput, calls=%fused_computation.2 | convolution fusion | flops 1112064000 | bytes 9175040 | tf_op jit(solution)/shard_map/dot_general | solution.py:450
  185.6 43.4 %reduce-scatter.2.cloned.1.call-done = bf16[192,2048]{1,0:T(8,128)(2,1)} async-done(((bf16[1536,2048]{1,0:T(8,128)(2,1)}), bf16[192,2048]{1,0:T(8,128)(2,1)}) %reduce-scatter.2.cloned.1.call-update) | async-done | bytes 786448 | tf_op jit(solution)/shard_map/reduce_scatter | solution.py:451
  229.0 2.2 reshape.106
  231.2 9.5 %all-to-all-start.2 = ((bf16[32,96,128]{2,1,0:T(8,128)(2,1)}), bf16[32,96,128]{2,1,0:T(8,128)(2,1)S(1)}, u32[]{:S(2)}, u32[]{:S(2)}) async-start(bf16[32,96,128]{2,1,0:T(8,128)(2,1)} %reshape.106), calls=%async_computation.3 | async-start | bytes 1572864 | tf_op jit(solution)/shard_map/all_to_all | solution.py:452
  242.6 2.7 fusion.56
  245.4 1.7 fusion.16
  247.1 13.4 %all-to-all-done.2 = bf16[32,96,128]{2,1,0:T(8,128)(2,1)S(1)} async-done(((bf16[32,96,128]{2,1,0:T(8,128)(2,1)}), bf16[32,96,128]{2,1,0:T(8,128)(2,1)S(1)}, u32[]{:S(2)}, u32[]{:S(2)}) %all-to-all-start.2) | async-done | bytes 786464 | tf_op jit(solution)/shard_map/all_to_all | solution.py:452
  260.8 4.7 %fusion.8 = bf16[512,2048]{1,0:T(8,128)(2,1)} fusion(bf16[192,2048]{1,0:T(8,128)(2,1)S(1)} %reshape.107, bf16[352,2048]{1,0:T(8,128)(2,1)} %param.22, bf16[512,192]{0,1:T(8,128)(2,1)S(1)} %copy-done.8, bf16[512,192]{0,1:T(8,128)(2,1)S(1)} %copy-done.9, bf16[512,352]{0,1:T(8,128)(2,1)} %fusion.16), kind=kOutput, calls=%fused_computation.13 | convolution fusion | flops 1555857408 | bytes 5079040 | tf_op jit(solution)/shard_map/dot_general | solution.py:460
  265.5 24.6 %shard_map.138 = bf16[64,2048]{1,0:T(8,128)(2,1)} custom-call(bf16[4,2,64,2048]{3,2,1,0:T(8,128)(2,1)} %bitcast.23, bf16[64,2048]{1,0:T(8,128)(2,1)} %fusion.11.b_ref), custom_call_target="tpu_custom_call" | custom-call | tf_op jit(solution)/shard_map/pallas_call | solution.py:108
  290.2 1.7 copy.49
  (84 shorter events, 18.7 us)
Async XLA Ops:
  6.5 236.1 %copy-start = (bf16[2048,352]{0,1:T(8,128)(2,1)S(1)}, bf16[2048,352]{0,1:T(8,128)(2,1)}, u32[]{:S(2)}) copy-start(bf16[2048,352]{0,1:T(8,128)(2,1)} %param.20) | copy-start | bytes 4325380
  6.5 8.3 %copy-start.3 = (bf16[32,4608]{1,0:T(8,128)(2,1)S(1)}, bf16[32,4608]{1,0:T(8,128)(2,1)}, u32[]{:S(2)}) copy-start(bf16[32,4608]{1,0:T(8,128)(2,1)} %param.15) | copy-start | bytes 884740
  6.5 92.3 %all-gather.3.cloned.1.call-start = ((), (), s32[]{:S(2)}) async-start(), calls=%async_computation.4 | async-start | bytes 2506752 | tf_op jit(solution)/shard_map/all_gather | solution.py:385
  16.2 24.3 %copy-start.2 = (bf16[256,2048]{1,0:T(8,128)(2,1)S(1)}, bf16[256,2048]{1,0:T(8,128)(2,1)}, u32[]{:S(2)}) copy-start(bf16[256,2048]{1,0:T(8,128)(2,1)} %wo_ref.1) | copy-start | bytes 3145732
  18.1 21.8 %all-to-all-start = ((bf16[32,2,2368]{2,1,0:T(2,128)(2,1)}), bf16[32,2,2368]{2,1,0:T(2,128)(2,1)S(1)}, u32[]{:S(2)}, u32[]{:S(2)}) async-start(bf16[32,2,2368]{2,1,0:T(2,128)(2,1)} %reshape.131), calls=%async_computation | async-start | bytes 622592 | tf_op jit(solution)/shard_map/all_to_all | solution.py:371
  30.0 144.7 %all-gather.5.cloned.1.call-start = ((), (), s32[]{:S(2)}) async-start(), calls=%async_computation.5 | async-start | bytes 7077888 | tf_op jit(solution)/shard_map/all_gather | solution.py:442
  40.4 39.0 %copy-start.7 = (bf16[32,1,4736]{2,0,1:T(8,128)(2,1)}, bf16[32,1,4736]{2,0,1:T(8,128)(2,1)S(1)}, u32[]{:S(2)}) copy-start(bf16[32,1,4736]{2,0,1:T(8,128)(2,1)S(1)} %copy.46) | copy-start | bytes 909316
  40.5 1.8 copy-start.1
  42.2 37.4 %copy-start.10 = (f32[2048]{0:T(1024)S(1)}, f32[2048]{0:T(1024)}, u32[]{:S(2)}) copy-start(f32[2048]{0:T(1024)} %param.19) | copy-start | bytes 24580
  104.8 1.3 copy-start.4
  131.4 43.4 %copy-start.12 = (bf16[1,2048,176]{1,2,0:T(8,128)(2,1)S(1)}, bf16[1,2048,176]{1,2,0:T(8,128)(2,1)}, u32[]{:S(2)}) copy-start(bf16[1,2048,176]{1,2,0:T(8,128)(2,1)} %param.24) | copy-start | bytes 2162692
  132.7 96.3 %reduce-scatter.2.cloned.1.call-start = ((), (), s32[]{:S(2)}) async-start(), calls=%async_computation.6 | async-start | bytes 7077888 | tf_op jit(solution)/shard_map/reduce_scatter | solution.py:451
  174.7 5.4 %copy-start.13 = (bf16[1,176,2048]{2,1,0:T(8,128)(2,1)S(1)}, bf16[1,176,2048]{2,1,0:T(8,128)(2,1)}, u32[]{:S(2)}) copy-start(bf16[1,176,2048]{2,1,0:T(8,128)(2,1)} %param.25) | copy-start | bytes 2162692
  184.7 56.1 %copy-start.6 = (bf16[64,2048]{1,0:T(8,128)(2,1)S(1)}, bf16[64,2048]{1,0:T(8,128)(2,1)}, u32[]{:S(2)}) copy-start(bf16[64,2048]{1,0:T(8,128)(2,1)} %param.14) | copy-start | bytes 786436
  231.2 29.3 %all-to-all-start.2 = ((bf16[32,96,128]{2,1,0:T(8,128)(2,1)}), bf16[32,96,128]{2,1,0:T(8,128)(2,1)S(1)}, u32[]{:S(2)}, u32[]{:S(2)}) async-start(bf16[32,96,128]{2,1,0:T(8,128)(2,1)} %reshape.106), calls=%async_computation.3 | async-start | bytes 1572864 | tf_op jit(solution)/shard_map/all_to_all | solution.py:452
  242.6 2.7 copy-start.5
  242.6 2.7 copy-start.11
  245.3 15.5 %copy-start.8 = (bf16[512,192]{0,1:T(8,128)(2,1)S(1)}, bf16[512,192]{0,1:T(8,128)(2,1)}, u32[]{:S(2)}) copy-start(bf16[512,192]{0,1:T(8,128)(2,1)} %get-tuple-element.9) | copy-start | bytes 589828
  245.4 15.5 %copy-start.9 = (bf16[512,192]{0,1:T(8,128)(2,1)S(1)}, bf16[512,192]{0,1:T(8,128)(2,1)}, u32[]{:S(2)}) copy-start(bf16[512,192]{0,1:T(8,128)(2,1)} %get-tuple-element.10) | copy-start | bytes 589828
Sparse Core Ops, SparseCore 0:
  11.3 32.1 all-gather.2
  132.8 41.8 all-gather.4
  184.8 44.1 reduce-scatter.1

commit v13 on v11

--- a/solution.py
+++ b/solution.py
@@ -418,7 +418,7 @@
     lanes = 128
     block = (n_data, share * width_model // lanes, lanes)
     send = select_dot(pick.T, normed).astype(bf16).reshape(block)
-    arrived = lax.all_to_all(send, "dp", split_axis=0, concat_axis=0, tiled=True)
+    arrived = dp_all_to_all(send, 1)
     slots = lax.all_gather(arrived.reshape(n_rows, width_model), "expert", axis=0, tiled=True)
 
     width_e = expert_gate.shape[2]

time: 294 us -> 295 us (level)
  Pallas kernels: 82.3 us -> 107 us
  blocking collectives: 24.1 us -> 0 us
    pallas_call x0 -> x1, Pallas kernels: none -> 24.7 us  [dp_all_to_all(): pl.pallas_call(kernel, out_shape=jax.ShapeDtypeStruct(x.shape, x.dtype),...]
    all_to_all x1 -> x0, blocking collectives: 24.1 us -> none  [shards(): lax.all_to_all(send, 'dp', split_axis=0, concat_axis=0, tiled=True)]
where the time goes in v13:
time: 295 us; the launch traced here: 294 us
  waiting for transfers between devices  108 us (37%)
  Pallas kernels  107 us (36%)
  matrix products  22.1 us (7%)
  starting transfers between devices  21.7 us (7%)
  local copies, waits for them, and re-layouts  15.4 us (5%)
  between operations  13.8 us (5%)
  other arithmetic  6.12 us (2%)
    reduce_scatter x1, waiting for transfers between devices, shards(): lax.psum_scatter(partial_out, 'expert', scatter_dimension=0, tiled=True)  44.3 us
    all_gather x1, waiting for transfers between devices, shards(): lax.all_gather(arrived.reshape(n_rows, width_model), 'expert', axis=0, ti...  39.4 us
    pallas_call x1, Pallas kernels, fused_projector(): pl.pallas_call(kernel, out_shape=jax.ShapeDtypeStruct((rows, width_model)...  37.2 us
    pallas_call x1, Pallas kernels, dp_all_to_all(): pl.pallas_call(kernel, out_shape=jax.ShapeDtypeStruct(x.shape, x.dtype),...  24.7 us
    pallas_call x1, Pallas kernels, expert_reduce_scatter(): pl.pallas_call(kernel, out_shape=jax.ShapeDtypeStruct((rows, cols), out_d...  24.6 us
    pallas_call x1, Pallas kernels, expert_all_gather(): pl.pallas_call(kernel, out_shape=jax.ShapeDtypeStruct((n, rows, cols), x....  20.5 us
    all_to_all x1, waiting for transfers between devices, shards(): lax.all_to_all(summed.reshape(block), 'dp', split_axis=0, concat_axis=0,...  14.5 us
    all_to_all x1, starting transfers between devices, shards(): lax.all_to_all(packed, 'dp', split_axis=0, concat_axis=0, tiled=True)  11.9 us
  transfers between devices with their start and end apart: 4, of which 4 were waited for; matrix products, arithmetic and copies ran while one was open for 2% of the time, Pallas kernels for 0%

profile of v13, /device:TPU:1, one launch (start us, length us, event | category | flops | bytes accessed | tf_op | source)
XLA Modules:
  0.0 294.0 jit_solution(10094887730869256849)
XLA Ops:
  7.3 1.6 sort.17
  9.0 1.4 gather_fusion.1
  12.6 1.1 reshape.105
  13.6 11.9 %all-to-all-start = ((bf16[32,2,2368]{2,1,0:T(2,128)(2,1)}), bf16[32,2,2368]{2,1,0:T(2,128)(2,1)S(1)}, u32[]{:S(2)}, u32[]{:S(2)}) async-start(bf16[32,2,2368]{2,1,0:T(2,128)(2,1)} %reshape.105), calls=%async_computation | async-start | bytes 622592 | tf_op jit(solution)/shard_map/all_to_all | solution.py:371
  25.7 9.7 %all-to-all-done = bf16[32,2,2368]{2,1,0:T(2,128)(2,1)S(1)} async-done(((bf16[32,2,2368]{2,1,0:T(2,128)(2,1)}), bf16[32,2,2368]{2,1,0:T(2,128)(2,1)S(1)}, u32[]{:S(2)}, u32[]{:S(2)}) %all-to-all-start) | async-done | bytes 303136 | tf_op jit(solution)/shard_map/all_to_all | solution.py:371
  36.2 1.7 copy-done.1
  37.9 37.2 %shard_map.136 = bf16[32,2048]{1,0:T(8,128)(2,1)S(1)} custom-call(bf16[32,4608]{1,0:T(8,128)(2,1)S(1)} %slice.41.f_ref, bf16[4608,256]{1,0:T(8,128)(2,1)S(1)} %copy-done.1, bf16[256,2048]{1,0:T(8,128)(2,1)S(1)} %copy-done.2), custom_call_target="tpu_custom_call" | custom-call | tf_op jit(solution)/shard_map/pallas_call | solution.py:303
  77.0 20.5 %shard_map.137 = bf16[8,64,2176]{2,1,0:T(8,128)(2,1)} custom-call(bf16[64,2176]{1,0:T(8,128)(2,1)} %fusion.37.x_ref), custom_call_target="tpu_custom_call" | custom-call | tf_op jit(solution)/shard_map/pallas_call | solution.py:189
  100.1 2.2 convolution_convert_fusion.1
  102.3 1.3 reshape.81.x_ref
  103.6 24.7 %shard_map.138 = bf16[32,96,128]{2,1,0:T(8,128)(2,1)} custom-call(bf16[32,96,128]{2,1,0:T(8,128)(2,1)} %reshape.81.x_ref), custom_call_target="tpu_custom_call" | custom-call | tf_op jit(solution)/shard_map/pallas_call | solution.py:41
  128.2 2.2 reshape.82
  130.7 39.4 %all-gather.2.cloned.1.call-done = bf16[1536,2048]{1,0:T(8,128)(2,1)} async-done(((bf16[192,2048]{1,0:T(8,128)(2,1)}), bf16[1536,2048]{1,0:T(8,128)(2,1)}) %all-gather.2.cloned.1.call-update) | async-done | bytes 6291472 | tf_op jit(solution)/shard_map/all_gather | solution.py:422
  170.2 5.3 %fusion.15 = f32[1536,352]{0,1:T(8,128)S(1)} fusion(bf16[1536,2048]{1,0:T(8,128)(2,1)} %all-gather.2.cloned.1.call-done, bf16[2048,176]{0,1:T(8,128)(2,1)S(1)} %bitcast.24, bf16[2048,176]{0,1:T(8,128)(2,1)S(1)} %bitcast.25), kind=kOutput, calls=%fused_computation.19 | convolution fusion | flops 2217476096 | bytes 9895936 | tf_op jit(solution)/shard_map/dot_general | solution.py:425
  175.5 4.5 %convolution_convert_fusion = bf16[1536,2048]{1,0:T(8,128)(2,1)} fusion(bf16[1,176,2048]{2,1,0:T(8,128)(2,1)S(1)} %copy-done.13, f32[1536,352]{0,1:T(8,128)S(1)} %fusion.15), kind=kOutput, calls=%fused_computation.2 | convolution fusion | flops 1112064000 | bytes 9175040 | tf_op jit(solution)/shard_map/dot_general | solution.py:430
  180.0 44.3 %reduce-scatter.2.cloned.1.call-done = bf16[192,2048]{1,0:T(8,128)(2,1)} async-done(((bf16[1536,2048]{1,0:T(8,128)(2,1)}), bf16[192,2048]{1,0:T(8,128)(2,1)}) %reduce-scatter.2.cloned.1.call-update) | async-done | bytes 786448 | tf_op jit(solution)/shard_map/reduce_scatter | solution.py:431
  224.3 2.2 reshape.83
  226.5 9.5 %all-to-all-start.1 = ((bf16[32,96,128]{2,1,0:T(8,128)(2,1)}), bf16[32,96,128]{2,1,0:T(8,128)(2,1)S(1)}, u32[]{:S(2)}, u32[]{:S(2)}) async-start(bf16[32,96,128]{2,1,0:T(8,128)(2,1)} %reshape.83), calls=%async_computation.2 | async-start | bytes 1572864 | tf_op jit(solution)/shard_map/all_to_all | solution.py:432
  236.8 2.7 fusion.13
  239.5 1.8 fusion.22
  241.3 14.5 %all-to-all-done.1 = bf16[32,96,128]{2,1,0:T(8,128)(2,1)S(1)} async-done(((bf16[32,96,128]{2,1,0:T(8,128)(2,1)}), bf16[32,96,128]{2,1,0:T(8,128)(2,1)S(1)}, u32[]{:S(2)}, u32[]{:S(2)}) %all-to-all-start.1) | async-done | bytes 786464 | tf_op jit(solution)/shard_map/all_to_all | solution.py:432
  256.2 4.7 %fusion.7 = bf16[512,2048]{1,0:T(8,128)(2,1)} fusion(bf16[192,2048]{1,0:T(8,128)(2,1)S(1)} %reshape.84, bf16[352,2048]{1,0:T(8,128)(2,1)} %param.22, bf16[512,192]{0,1:T(8,128)(2,1)S(1)} %copy-done.6, bf16[512,192]{0,1:T(8,128)(2,1)S(1)} %copy-done.7, bf16[512,352]{0,1:T(8,128)(2,1)} %fusion.22), kind=kOutput, calls=%fused_computation.11 | convolution fusion | flops 1555857408 | bytes 5079040 | tf_op jit(solution)/shard_map/dot_general | solution.py:440
  260.8 24.6 %shard_map.139 = bf16[64,2048]{1,0:T(8,128)(2,1)} custom-call(bf16[4,2,64,2048]{3,2,1,0:T(8,128)(2,1)} %bitcast.21, bf16[64,2048]{1,0:T(8,128)(2,1)} %get-tuple-element.11.b_ref), custom_call_target="tpu_custom_call" | custom-call | tf_op jit(solution)/shard_map/pallas_call | solution.py:108
  285.5 1.7 copy.53
  (72 shorter events, 9.8 us)
Async XLA Ops:
  6.5 230.2 %copy-start = (bf16[2048,352]{0,1:T(8,128)(2,1)S(1)}, bf16[2048,352]{0,1:T(8,128)(2,1)}, u32[]{:S(2)}) copy-start(bf16[2048,352]{0,1:T(8,128)(2,1)} %param.20) | copy-start | bytes 4325380
  6.5 3.8 %copy-start.3 = (bf16[32,4608]{1,0:T(8,128)(2,1)S(1)}, bf16[32,4608]{1,0:T(8,128)(2,1)}, u32[]{:S(2)}) copy-start(bf16[32,4608]{1,0:T(8,128)(2,1)} %param.15) | copy-start | bytes 884740
  10.3 15.2 %copy-start.14 = (s32[64,2]{0,1:T(2,128)S(1)}, s32[64,2]{0,1:T(2,128)}, u32[]{:S(2)}) copy-start(s32[64,2]{0,1:T(2,128)} %param.26) | copy-start | bytes 1540
  10.4 15.2 %copy-start.9 = (s32[64,2]{0,1:T(2,128)S(1)}, s32[64,2]{0,1:T(2,128)}, u32[]{:S(2)}) copy-start(s32[64,2]{0,1:T(2,128)} %param.27) | copy-start | bytes 1540
  11.7 24.5 %copy-start.2 = (bf16[256,2048]{1,0:T(8,128)(2,1)S(1)}, bf16[256,2048]{1,0:T(8,128)(2,1)}, u32[]{:S(2)}) copy-start(bf16[256,2048]{1,0:T(8,128)(2,1)} %wo_ref.1) | copy-start | bytes 3145732
  13.6 21.8 %all-to-all-start = ((bf16[32,2,2368]{2,1,0:T(2,128)(2,1)}), bf16[32,2,2368]{2,1,0:T(2,128)(2,1)S(1)}, u32[]{:S(2)}, u32[]{:S(2)}) async-start(bf16[32,2,2368]{2,1,0:T(2,128)(2,1)} %reshape.105), calls=%async_computation | async-start | bytes 622592 | tf_op jit(solution)/shard_map/all_to_all | solution.py:371
  25.5 144.6 %all-gather.2.cloned.1.call-start = ((), (), s32[]{:S(2)}) async-start(), calls=%async_computation.3 | async-start | bytes 7077888 | tf_op jit(solution)/shard_map/all_gather | solution.py:422
  36.0 39.0 %copy-start.5 = (bf16[64,2048]{1,0:T(8,128)(2,1)S(1)}, bf16[64,2048]{1,0:T(8,128)(2,1)}, u32[]{:S(2)}) copy-start(bf16[64,2048]{1,0:T(8,128)(2,1)} %param.14) | copy-start | bytes 786436
  36.2 1.7 copy-start.1
  37.9 37.7 %copy-start.8 = (f32[2048]{0:T(1024)S(1)}, f32[2048]{0:T(1024)}, u32[]{:S(2)}) copy-start(f32[2048]{0:T(1024)} %param.19) | copy-start | bytes 24580
  103.6 66.6 %copy-start.11 = (bf16[1,2048,176]{1,2,0:T(8,128)(2,1)S(1)}, bf16[1,2048,176]{1,2,0:T(8,128)(2,1)}, u32[]{:S(2)}) copy-start(bf16[1,2048,176]{1,2,0:T(8,128)(2,1)} %param.24) | copy-start | bytes 2162692
  103.6 66.6 %copy-start.12 = (bf16[1,2048,176]{1,2,0:T(8,128)(2,1)S(1)}, bf16[1,2048,176]{1,2,0:T(8,128)(2,1)}, u32[]{:S(2)}) copy-start(bf16[1,2048,176]{1,2,0:T(8,128)(2,1)} %param.23) | copy-start | bytes 2162692
  130.5 93.8 %reduce-scatter.2.cloned.1.call-start = ((), (), s32[]{:S(2)}) async-start(), calls=%async_computation.4 | async-start | bytes 7077888 | tf_op jit(solution)/shard_map/reduce_scatter | solution.py:431
  170.2 5.3 %copy-start.13 = (bf16[1,176,2048]{2,1,0:T(8,128)(2,1)S(1)}, bf16[1,176,2048]{2,1,0:T(8,128)(2,1)}, u32[]{:S(2)}) copy-start(bf16[1,176,2048]{2,1,0:T(8,128)(2,1)} %param.25) | copy-start | bytes 2162692
  226.5 29.3 %all-to-all-start.1 = ((bf16[32,96,128]{2,1,0:T(8,128)(2,1)}), bf16[32,96,128]{2,1,0:T(8,128)(2,1)S(1)}, u32[]{:S(2)}, u32[]{:S(2)}) async-start(bf16[32,96,128]{2,1,0:T(8,128)(2,1)} %reshape.83), calls=%async_computation.2 | async-start | bytes 1572864 | tf_op jit(solution)/shard_map/all_to_all | solution.py:432
  236.8 2.7 copy-start.4
  236.8 2.7 copy-start.10
  239.5 16.7 %copy-start.6 = (bf16[512,192]{0,1:T(8,128)(2,1)S(1)}, bf16[512,192]{0,1:T(8,128)(2,1)}, u32[]{:S(2)}) copy-start(bf16[512,192]{0,1:T(8,128)(2,1)} %get-tuple-element.9) | copy-start | bytes 589828
  239.5 16.7 %copy-start.7 = (bf16[512,192]{0,1:T(8,128)(2,1)S(1)}, bf16[512,192]{0,1:T(8,128)(2,1)}, u32[]{:S(2)}) copy-start(bf16[512,192]{0,1:T(8,128)(2,1)} %get-tuple-element.10) | copy-start | bytes 589828
Sparse Core Ops, SparseCore 0:
  130.6 39.4 all-gather.1
  180.1 44.1 reduce-scatter.1

commit v14 on v11

--- a/solution.py
+++ b/solution.py
@@ -362,12 +362,16 @@
     route_cols = jnp.pad(route_cols, ((0, 0), (0, 128 - route_cols.shape[1])))
 
     dest_index = tile_pos // tok_dev // n_group
-    order = jnp.argsort(dest_index, stable=True)
-    offs_sorted = (tile_pos[order] % tok_dev).astype(bf16)
+    img_iota = jnp.arange(img_dev, dtype=jnp.int32)
+    same_before = (dest_index[None, :] == dest_index[:, None]) & (img_iota[None, :] < img_iota[:, None])
+    send_slot = dest_index * peer + jnp.sum(same_before.astype(jnp.int32), axis=1)
+    reorder = (send_slot[None, :] == img_iota[:, None]).astype(bf16)
     pad = 128
-    packed = jnp.concatenate(
-        [image_feats[order], jnp.broadcast_to(offs_sorted[:, None], (img_dev, pad))], axis=1
-    ).reshape(n_data, peer, width_vis + pad)
+    unordered = jnp.concatenate(
+        [image_feats, jnp.broadcast_to((tile_pos % tok_dev).astype(bf16)[:, None], (img_dev, pad))],
+        axis=1,
+    )
+    packed = select_dot(reorder, unordered).astype(bf16).reshape(n_data, peer, width_vis + pad)
     moved = lax.all_to_all(packed, "dp", split_axis=0, concat_axis=0, tiled=True)
     moved = moved.reshape(img_dev, width_vis + pad)
     moved_feats = moved[:, :width_vis]

time: 294 us -> 292 us (level)
  no operation moved by 1% of the time
where the time goes in v14:
time: 292 us; the launch traced here: 291 us
  waiting for transfers between devices  110 us (38%)
  Pallas kernels  82.3 us (28%)
  blocking collectives  24.1 us (8%)
  matrix products  23.4 us (8%)
  starting transfers between devices  21.7 us (7%)
  between operations  13.7 us (5%)
  local copies, waits for them, and re-layouts  11.4 us (4%)
  other arithmetic  4.65 us (2%)
    reduce_scatter x1, waiting for transfers between devices, shards(): lax.psum_scatter(partial_out, 'expert', scatter_dimension=0, tiled=True)  44.3 us
    all_gather x1, waiting for transfers between devices, shards(): lax.all_gather(arrived.reshape(n_rows, width_model), 'expert', axis=0, ti...  41.6 us
    pallas_call x1, Pallas kernels, fused_projector(): pl.pallas_call(kernel, out_shape=jax.ShapeDtypeStruct((rows, width_model)...  37.2 us
    pallas_call x1, Pallas kernels, expert_reduce_scatter(): pl.pallas_call(kernel, out_shape=jax.ShapeDtypeStruct((rows, cols), out_d...  24.7 us
    all_to_all x1, blocking collectives, shards(): lax.all_to_all(send, 'dp', split_axis=0, concat_axis=0, tiled=True)  24.1 us
    pallas_call x1, Pallas kernels, expert_all_gather(): pl.pallas_call(kernel, out_shape=jax.ShapeDtypeStruct((n, rows, cols), x....  20.5 us
    all_to_all x1, waiting for transfers between devices, shards(): lax.all_to_all(summed.reshape(block), 'dp', split_axis=0, concat_axis=0,...  14.5 us
    all_to_all x1, starting transfers between devices, shards(): lax.all_to_all(packed, 'dp', split_axis=0, concat_axis=0, tiled=True)  11.9 us
  transfers between devices with their start and end apart: 4, of which 4 were waited for; matrix products, arithmetic and copies ran while one was open for 2% of the time, Pallas kernels for 0%

profile of v14, /device:TPU:1, one launch (start us, length us, event | category | flops | bytes accessed | tf_op | source)
XLA Modules:
  0.0 291.5 jit_solution(7689628992284480848)
XLA Ops:
  7.6 1.2 fusion
  9.3 0.9 reduce.2
  10.2 1.1 reshape.77
  11.2 11.9 %all-to-all-start = ((bf16[32,2,2368]{2,1,0:T(2,128)(2,1)}), bf16[32,2,2368]{2,1,0:T(2,128)(2,1)S(1)}, u32[]{:S(2)}, u32[]{:S(2)}) async-start(bf16[32,2,2368]{2,1,0:T(2,128)(2,1)} %reshape.77), calls=%async_computation | async-start | bytes 622592 | tf_op jit(solution)/shard_map/all_to_all | solution.py:375
  23.3 9.7 %all-to-all-done = bf16[32,2,2368]{2,1,0:T(2,128)(2,1)S(1)} async-done(((bf16[32,2,2368]{2,1,0:T(2,128)(2,1)}), bf16[32,2,2368]{2,1,0:T(2,128)(2,1)S(1)}, u32[]{:S(2)}, u32[]{:S(2)}) %all-to-all-start) | async-done | bytes 303136 | tf_op jit(solution)/shard_map/all_to_all | solution.py:375
  33.8 1.7 copy-done.1
  35.4 37.2 %shard_map.136 = bf16[32,2048]{1,0:T(8,128)(2,1)S(1)} custom-call(bf16[32,4608]{1,0:T(8,128)(2,1)S(1)} %slice.37.f_ref, bf16[4608,256]{1,0:T(8,128)(2,1)S(1)} %copy-done.1, bf16[256,2048]{1,0:T(8,128)(2,1)S(1)} %copy-done.2), custom_call_target="tpu_custom_call" | custom-call | tf_op jit(solution)/shard_map/pallas_call | solution.py:303
  74.6 20.5 %shard_map.137 = bf16[8,64,2176]{2,1,0:T(8,128)(2,1)} custom-call(bf16[64,2176]{1,0:T(8,128)(2,1)} %fusion.41.x_ref), custom_call_target="tpu_custom_call" | custom-call | tf_op jit(solution)/shard_map/pallas_call | solution.py:189
  95.1 0.9 slice.39
  97.6 2.2 convolution_convert_fusion.2
  100.2 24.1 %all_to_all.15 = bf16[32,96,128]{2,1,0:T(8,128)(2,1)S(1)} all-to-all(bf16[32,96,128]{2,1,0:T(8,128)(2,1)S(1)} %reshape.71), channel_id=1, replica_groups=mesh['dp'=32,'expert'=8] {'dp'}, dimensions={0} | all-to-all | bytes 1572864 | tf_op jit(solution)/shard_map/all_to_all | solution.py:425
  124.3 1.3 reshape.72
  125.9 41.6 %all-gather.2.cloned.1.call-done = bf16[1536,2048]{1,0:T(8,128)(2,1)} async-done(((bf16[192,2048]{1,0:T(8,128)(2,1)}), bf16[1536,2048]{1,0:T(8,128)(2,1)}) %all-gather.2.cloned.1.call-update) | async-done | bytes 6291472 | tf_op jit(solution)/shard_map/all_gather | solution.py:426
  167.5 5.4 %fusion.16 = f32[1536,352]{0,1:T(8,128)S(1)} fusion(bf16[1536,2048]{1,0:T(8,128)(2,1)} %all-gather.2.cloned.1.call-done, bf16[2048,176]{0,1:T(8,128)(2,1)S(1)} %bitcast.24, bf16[2048,176]{0,1:T(8,128)(2,1)} %bitcast.25), kind=kOutput, calls=%fused_computation.19 | convolution fusion | flops 2217476096 | bytes 9895936 | tf_op jit(solution)/shard_map/dot_general | solution.py:429
  172.9 4.5 %convolution_convert_fusion = bf16[1536,2048]{1,0:T(8,128)(2,1)} fusion(bf16[1,176,2048]{2,1,0:T(8,128)(2,1)S(1)} %copy-done.11, f32[1536,352]{0,1:T(8,128)S(1)} %fusion.16), kind=kOutput, calls=%fused_computation | convolution fusion | flops 1112064000 | bytes 9175040 | tf_op jit(solution)/shard_map/dot_general | solution.py:434
  177.5 44.3 %reduce-scatter.2.cloned.1.call-done = bf16[192,2048]{1,0:T(8,128)(2,1)} async-done(((bf16[1536,2048]{1,0:T(8,128)(2,1)}), bf16[192,2048]{1,0:T(8,128)(2,1)}) %reduce-scatter.2.cloned.1.call-update) | async-done | bytes 786448 | tf_op jit(solution)/shard_map/reduce_scatter | solution.py:435
  221.8 2.2 reshape.73
  223.9 9.5 %all-to-all-start.2 = ((bf16[32,96,128]{2,1,0:T(8,128)(2,1)}), bf16[32,96,128]{2,1,0:T(8,128)(2,1)S(1)}, u32[]{:S(2)}, u32[]{:S(2)}) async-start(bf16[32,96,128]{2,1,0:T(8,128)(2,1)} %reshape.73), calls=%async_computation.3 | async-start | bytes 1572864 | tf_op jit(solution)/shard_map/all_to_all | solution.py:436
  234.3 2.7 fusion.14
  237.0 1.7 fusion.23
  238.7 14.5 %all-to-all-done.2 = bf16[32,96,128]{2,1,0:T(8,128)(2,1)S(1)} async-done(((bf16[32,96,128]{2,1,0:T(8,128)(2,1)}), bf16[32,96,128]{2,1,0:T(8,128)(2,1)S(1)}, u32[]{:S(2)}, u32[]{:S(2)}) %all-to-all-start.2) | async-done | bytes 786464 | tf_op jit(solution)/shard_map/all_to_all | solution.py:436
  253.6 4.7 %fusion.8 = bf16[512,2048]{1,0:T(8,128)(2,1)} fusion(bf16[192,2048]{1,0:T(8,128)(2,1)S(1)} %reshape.74, bf16[352,2048]{1,0:T(8,128)(2,1)} %param.22, bf16[512,192]{0,1:T(8,128)(2,1)S(1)} %copy-done.5, bf16[512,192]{0,1:T(8,128)(2,1)S(1)} %copy-done.6, bf16[512,352]{0,1:T(8,128)(2,1)} %fusion.23), kind=kOutput, calls=%fused_computation.11 | convolution fusion | flops 1555857408 | bytes 5079040 | tf_op jit(solution)/shard_map/dot_general | solution.py:444
  258.3 24.7 %shard_map.138 = bf16[64,2048]{1,0:T(8,128)(2,1)} custom-call(bf16[4,2,64,2048]{3,2,1,0:T(8,128)(2,1)} %bitcast.21, bf16[64,2048]{1,0:T(8,128)(2,1)} %get-tuple-element.9.b_ref), custom_call_target="tpu_custom_call" | custom-call | tf_op jit(solution)/shard_map/pallas_call | solution.py:108
  282.9 1.7 copy.53
  (63 shorter events, 7.8 us)
Async XLA Ops:
  6.5 227.7 %copy-start = (bf16[2048,352]{0,1:T(8,128)(2,1)S(1)}, bf16[2048,352]{0,1:T(8,128)(2,1)}, u32[]{:S(2)}) copy-start(bf16[2048,352]{0,1:T(8,128)(2,1)} %param.20) | copy-start | bytes 4325380
  6.5 16.6 %copy-start.12 = (s32[64,2]{0,1:T(2,128)S(1)}, s32[64,2]{0,1:T(2,128)}, u32[]{:S(2)}) copy-start(s32[64,2]{0,1:T(2,128)} %param.26) | copy-start | bytes 1540
  6.5 16.6 %copy-start.8 = (s32[64,2]{0,1:T(2,128)S(1)}, s32[64,2]{0,1:T(2,128)}, u32[]{:S(2)}) copy-start(s32[64,2]{0,1:T(2,128)} %param.27) | copy-start | bytes 1540
  9.3 24.5 %copy-start.2 = (bf16[256,2048]{1,0:T(8,128)(2,1)S(1)}, bf16[256,2048]{1,0:T(8,128)(2,1)}, u32[]{:S(2)}) copy-start(bf16[256,2048]{1,0:T(8,128)(2,1)} %wo_ref.1) | copy-start | bytes 3145732
  11.2 21.8 %all-to-all-start = ((bf16[32,2,2368]{2,1,0:T(2,128)(2,1)}), bf16[32,2,2368]{2,1,0:T(2,128)(2,1)S(1)}, u32[]{:S(2)}, u32[]{:S(2)}) async-start(bf16[32,2,2368]{2,1,0:T(2,128)(2,1)} %reshape.77), calls=%async_computation | async-start | bytes 622592 | tf_op jit(solution)/shard_map/all_to_all | solution.py:375
  23.1 144.4 %all-gather.2.cloned.1.call-start = ((), (), s32[]{:S(2)}) async-start(), calls=%async_computation.4 | async-start | bytes 7077888 | tf_op jit(solution)/shard_map/all_gather | solution.py:426
  33.6 39.0 %copy-start.4 = (bf16[64,2048]{1,0:T(8,128)(2,1)S(1)}, bf16[64,2048]{1,0:T(8,128)(2,1)}, u32[]{:S(2)}) copy-start(bf16[64,2048]{1,0:T(8,128)(2,1)} %param.14) | copy-start | bytes 786436
  33.8 1.7 copy-start.1
  35.4 37.7 %copy-start.7 = (f32[2048]{0:T(1024)S(1)}, f32[2048]{0:T(1024)}, u32[]{:S(2)}) copy-start(f32[2048]{0:T(1024)} %param.19) | copy-start | bytes 24580
  124.3 43.2 %copy-start.10 = (bf16[1,2048,176]{1,2,0:T(8,128)(2,1)S(1)}, bf16[1,2048,176]{1,2,0:T(8,128)(2,1)}, u32[]{:S(2)}) copy-start(bf16[1,2048,176]{1,2,0:T(8,128)(2,1)} %param.24) | copy-start | bytes 2162692
  125.6 96.1 %reduce-scatter.2.cloned.1.call-start = ((), (), s32[]{:S(2)}) async-start(), calls=%async_computation.5 | async-start | bytes 7077888 | tf_op jit(solution)/shard_map/reduce_scatter | solution.py:435
  167.5 5.4 %copy-start.11 = (bf16[1,176,2048]{2,1,0:T(8,128)(2,1)S(1)}, bf16[1,176,2048]{2,1,0:T(8,128)(2,1)}, u32[]{:S(2)}) copy-start(bf16[1,176,2048]{2,1,0:T(8,128)(2,1)} %param.25) | copy-start | bytes 2162692
  223.9 29.3 %all-to-all-start.2 = ((bf16[32,96,128]{2,1,0:T(8,128)(2,1)}), bf16[32,96,128]{2,1,0:T(8,128)(2,1)S(1)}, u32[]{:S(2)}, u32[]{:S(2)}) async-start(bf16[32,96,128]{2,1,0:T(8,128)(2,1)} %reshape.73), calls=%async_computation.3 | async-start | bytes 1572864 | tf_op jit(solution)/shard_map/all_to_all | solution.py:436
  234.3 2.7 copy-start.3
  234.3 2.7 copy-start.9
  237.0 16.6 %copy-start.5 = (bf16[512,192]{0,1:T(8,128)(2,1)S(1)}, bf16[512,192]{0,1:T(8,128)(2,1)}, u32[]{:S(2)}) copy-start(bf16[512,192]{0,1:T(8,128)(2,1)} %get-tuple-element.7) | copy-start | bytes 589828
  237.0 16.6 %copy-start.6 = (bf16[512,192]{0,1:T(8,128)(2,1)S(1)}, bf16[512,192]{0,1:T(8,128)(2,1)}, u32[]{:S(2)}) copy-start(bf16[512,192]{0,1:T(8,128)(2,1)} %get-tuple-element.8) | copy-start | bytes 589828
Sparse Core Ops, SparseCore 0:
  125.8 41.6 all-gather.1
  177.6 44.1 reduce-scatter.1

commit v15 on v14

--- a/solution.py
+++ b/solution.py
@@ -396,9 +396,6 @@
     ids = routes[:, :top_count].astype(jnp.int32)
     weights_f = routes[:, top_count : 2 * top_count] * 256.0 + routes[:, 2 * top_count : 3 * top_count]
 
-    gate_s = jnp.dot(normed, shared_gate, preferred_element_type=f32)
-    up_s = jnp.dot(normed, shared_up, preferred_element_type=f32)
-    shared_hidden = (jax.nn.silu(gate_s) * up_s).astype(bf16)
 
     group_rows = normed.shape[0]
     n_pairs = group_rows * top_count
@@ -433,6 +430,10 @@
     hidden_e = (jax.nn.silu(gate_e) * up_e).astype(bf16)
     partial_out = jnp.dot(hidden_e, expert_down[0], preferred_element_type=f32).astype(bf16)
     summed = lax.psum_scatter(partial_out, "expert", scatter_dimension=0, tiled=True)
+    summed, normed_late = lax.optimization_barrier((summed, normed))
+    gate_s = jnp.dot(normed_late, shared_gate, preferred_element_type=f32)
+    up_s = jnp.dot(normed_late, shared_up, preferred_element_type=f32)
+    shared_hidden = (jax.nn.silu(gate_s) * up_s).astype(bf16)
     returned = lax.all_to_all(
         summed.reshape(block), "dp", split_axis=0, concat_axis=0, tiled=True
     ).reshape(n_rows, width_model)

time: 292 us -> 292 us (level)
  local copies, waits for them, and re-layouts: 11.4 us -> 14.7 us
  waiting for transfers between devices: 110 us -> 107 us
    reduce_scatter x1, waiting for transfers between devices: 44.3 us -> 41.1 us  [shards(): lax.psum_scatter(partial_out, 'expert', scatter_dimension=0, tiled=True)]
    slice x0 -> x1, local copies, waits for them, and re-layouts: none -> 3.21 us  [shards(): normed = gathered[:, :width_model]]
  transfers between devices with their start and end apart: 4 -> 4, of which waited for: 4 -> 4; matrix products, arithmetic and copies ran while one was open for 2% -> 3% of each run, Pallas kernels for 0% -> 0%
where the time goes in v15:
time: 292 us; the launch traced here: 291 us
  waiting for transfers between devices  107 us (37%)
  Pallas kernels  82.3 us (28%)
  blocking collectives  24.1 us (8%)
  matrix products  23.4 us (8%)
  starting transfers between devices  21.7 us (7%)
  local copies, waits for them, and re-layouts  14.7 us (5%)
  between operations  13.7 us (5%)
  other arithmetic  4.65 us (2%)
    all_gather x1, waiting for transfers between devices, shards(): lax.all_gather(arrived.reshape(n_rows, width_model), 'expert', axis=0, ti...  41.6 us
    reduce_scatter x1, waiting for transfers between devices, shards(): lax.psum_scatter(partial_out, 'expert', scatter_dimension=0, tiled=True)  41.1 us
    pallas_call x1, Pallas kernels, fused_projector(): pl.pallas_call(kernel, out_shape=jax.ShapeDtypeStruct((rows, width_model)...  37.2 us
    pallas_call x1, Pallas kernels, expert_reduce_scatter(): pl.pallas_call(kernel, out_shape=jax.ShapeDtypeStruct((rows, cols), out_d...  24.7 us
    all_to_all x1, blocking collectives, shards(): lax.all_to_all(send, 'dp', split_axis=0, concat_axis=0, tiled=True)  24.1 us
    pallas_call x1, Pallas kernels, expert_all_gather(): pl.pallas_call(kernel, out_shape=jax.ShapeDtypeStruct((n, rows, cols), x....  20.5 us
    all_to_all x1, waiting for transfers between devices, shards(): lax.all_to_all(summed.reshape(block), 'dp', split_axis=0, concat_axis=0,...  14.5 us
    all_to_all x1, starting transfers between devices, shards(): lax.all_to_all(packed, 'dp', split_axis=0, concat_axis=0, tiled=True)  11.9 us
  transfers between devices with their start and end apart: 4, of which 4 were waited for; matrix products, arithmetic and copies ran while one was open for 3% of the time, Pallas kernels for 0%

profile of v15, /device:TPU:1, one launch (start us, length us, event | category | flops | bytes accessed | tf_op | source)
XLA Modules:
  0.0 291.4 jit_solution(3520877772760017010)
XLA Ops:
  7.6 1.2 fusion
  10.2 1.1 reshape.77
  11.2 11.9 %all-to-all-start = ((bf16[32,2,2368]{2,1,0:T(2,128)(2,1)}), bf16[32,2,2368]{2,1,0:T(2,128)(2,1)S(1)}, u32[]{:S(2)}, u32[]{:S(2)}) async-start(bf16[32,2,2368]{2,1,0:T(2,128)(2,1)} %reshape.77), calls=%async_computation | async-start | bytes 622592 | tf_op jit(solution)/shard_map/all_to_all | solution.py:375
  23.3 9.7 %all-to-all-done = bf16[32,2,2368]{2,1,0:T(2,128)(2,1)S(1)} async-done(((bf16[32,2,2368]{2,1,0:T(2,128)(2,1)}), bf16[32,2,2368]{2,1,0:T(2,128)(2,1)S(1)}, u32[]{:S(2)}, u32[]{:S(2)}) %all-to-all-start) | async-done | bytes 303136 | tf_op jit(solution)/shard_map/all_to_all | solution.py:375
  33.8 1.7 copy-done.1
  35.4 37.2 %shard_map.136 = bf16[32,2048]{1,0:T(8,128)(2,1)S(1)} custom-call(bf16[32,4608]{1,0:T(8,128)(2,1)S(1)} %slice.37.f_ref, bf16[4608,256]{1,0:T(8,128)(2,1)S(1)} %copy-done.1, bf16[256,2048]{1,0:T(8,128)(2,1)S(1)} %copy-done.2), custom_call_target="tpu_custom_call" | custom-call | tf_op jit(solution)/shard_map/pallas_call | solution.py:303
  74.6 20.5 %shard_map.137 = bf16[8,64,2176]{2,1,0:T(8,128)(2,1)} custom-call(bf16[64,2176]{1,0:T(8,128)(2,1)} %fusion.31.x_ref), custom_call_target="tpu_custom_call" | custom-call | tf_op jit(solution)/shard_map/pallas_call | solution.py:189
  95.1 0.9 slice.38
  97.6 2.2 convolution_convert_fusion.2
  100.2 24.1 %all_to_all.15 = bf16[32,96,128]{2,1,0:T(8,128)(2,1)S(1)} all-to-all(bf16[32,96,128]{2,1,0:T(8,128)(2,1)S(1)} %reshape.71), channel_id=1, replica_groups=mesh['dp'=32,'expert'=8] {'dp'}, dimensions={0} | all-to-all | bytes 1572864 | tf_op jit(solution)/shard_map/all_to_all | solution.py:422
  124.3 1.3 reshape.72
  125.8 41.6 %all-gather.2.cloned.1.call-done = bf16[1536,2048]{1,0:T(8,128)(2,1)} async-done(((bf16[192,2048]{1,0:T(8,128)(2,1)}), bf16[1536,2048]{1,0:T(8,128)(2,1)}) %all-gather.2.cloned.1.call-update) | async-done | bytes 6291472 | tf_op jit(solution)/shard_map/all_gather | solution.py:423
  167.5 5.4 %fusion.11 = f32[1536,352]{0,1:T(8,128)S(1)} fusion(bf16[1536,2048]{1,0:T(8,128)(2,1)} %all-gather.2.cloned.1.call-done, bf16[2048,176]{0,1:T(8,128)(2,1)S(1)} %bitcast.25, bf16[2048,176]{0,1:T(8,128)(2,1)} %bitcast.26), kind=kOutput, calls=%fused_computation.14 | convolution fusion | flops 2217476096 | bytes 9895936 | tf_op jit(solution)/shard_map/dot_general | solution.py:426
  172.9 4.5 %convolution_convert_fusion = bf16[1536,2048]{1,0:T(8,128)(2,1)} fusion(bf16[1,176,2048]{2,1,0:T(8,128)(2,1)S(1)} %copy-done.11, f32[1536,352]{0,1:T(8,128)S(1)} %fusion.11), kind=kOutput, calls=%fused_computation | convolution fusion | flops 1112064000 | bytes 9175040 | tf_op jit(solution)/shard_map/dot_general | solution.py:431
  177.5 3.2 %slice.40 = bf16[512,2048]{1,0:T(8,128)(2,1)} slice(bf16[512,2176]{1,0:T(8,128)(2,1)} %bitcast.21), slice={[0:512], [0:2048]} | slice | bytes 4194304 | tf_op jit(solution)/shard_map/slice | solution.py:393
  180.7 41.1 %reduce-scatter.2.cloned.1.call-done = bf16[192,2048]{1,0:T(8,128)(2,1)} async-done(((bf16[1536,2048]{1,0:T(8,128)(2,1)}), bf16[192,2048]{1,0:T(8,128)(2,1)}) %reduce-scatter.2.cloned.1.call-update) | async-done | bytes 786448 | tf_op jit(solution)/shard_map/reduce_scatter | solution.py:432
  221.8 2.2 reshape.73
  223.9 9.5 %all-to-all-start.2 = ((bf16[32,96,128]{2,1,0:T(8,128)(2,1)}), bf16[32,96,128]{2,1,0:T(8,128)(2,1)S(1)}, u32[]{:S(2)}, u32[]{:S(2)}) async-start(bf16[32,96,128]{2,1,0:T(8,128)(2,1)} %reshape.73), calls=%async_computation.3 | async-start | bytes 1572864 | tf_op jit(solution)/shard_map/all_to_all | solution.py:437
  234.3 2.7 fusion.49
  237.0 1.7 fusion.15
  238.7 14.5 %all-to-all-done.2 = bf16[32,96,128]{2,1,0:T(8,128)(2,1)S(1)} async-done(((bf16[32,96,128]{2,1,0:T(8,128)(2,1)}), bf16[32,96,128]{2,1,0:T(8,128)(2,1)S(1)}, u32[]{:S(2)}, u32[]{:S(2)}) %all-to-all-start.2) | async-done | bytes 786464 | tf_op jit(solution)/shard_map/all_to_all | solution.py:437
  253.6 4.7 %fusion.8 = bf16[512,2048]{1,0:T(8,128)(2,1)} fusion(bf16[192,2048]{1,0:T(8,128)(2,1)S(1)} %reshape.74, bf16[352,2048]{1,0:T(8,128)(2,1)} %param.22, bf16[512,192]{0,1:T(8,128)(2,1)S(1)} %copy-done.5, bf16[512,192]{0,1:T(8,128)(2,1)S(1)} %copy-done.6, bf16[512,352]{0,1:T(8,128)(2,1)} %fusion.15), kind=kOutput, calls=%fused_computation.11 | convolution fusion | flops 1555857408 | bytes 5079040 | tf_op jit(solution)/shard_map/dot_general | solution.py:445
  258.3 24.7 %shard_map.138 = bf16[64,2048]{1,0:T(8,128)(2,1)} custom-call(bf16[4,2,64,2048]{3,2,1,0:T(8,128)(2,1)} %bitcast.22, bf16[64,2048]{1,0:T(8,128)(2,1)} %get-tuple-element.13.b_ref), custom_call_target="tpu_custom_call" | custom-call | tf_op jit(solution)/shard_map/pallas_call | solution.py:108
  282.9 1.7 copy.53
  (64 shorter events, 8.6 us)
Async XLA Ops:
  6.5 227.7 %copy-start = (bf16[2048,352]{0,1:T(8,128)(2,1)S(1)}, bf16[2048,352]{0,1:T(8,128)(2,1)}, u32[]{:S(2)}) copy-start(bf16[2048,352]{0,1:T(8,128)(2,1)} %param.20) | copy-start | bytes 4325380
  6.5 16.6 %copy-start.12 = (s32[64,2]{0,1:T(2,128)S(1)}, s32[64,2]{0,1:T(2,128)}, u32[]{:S(2)}) copy-start(s32[64,2]{0,1:T(2,128)} %param.26) | copy-start | bytes 1540
  6.5 16.6 %copy-start.8 = (s32[64,2]{0,1:T(2,128)S(1)}, s32[64,2]{0,1:T(2,128)}, u32[]{:S(2)}) copy-start(s32[64,2]{0,1:T(2,128)} %param.27) | copy-start | bytes 1540
  9.3 24.5 %copy-start.2 = (bf16[256,2048]{1,0:T(8,128)(2,1)S(1)}, bf16[256,2048]{1,0:T(8,128)(2,1)}, u32[]{:S(2)}) copy-start(bf16[256,2048]{1,0:T(8,128)(2,1)} %wo_ref.1) | copy-start | bytes 3145732
  11.2 21.8 %all-to-all-start = ((bf16[32,2,2368]{2,1,0:T(2,128)(2,1)}), bf16[32,2,2368]{2,1,0:T(2,128)(2,1)S(1)}, u32[]{:S(2)}, u32[]{:S(2)}) async-start(bf16[32,2,2368]{2,1,0:T(2,128)(2,1)} %reshape.77), calls=%async_computation | async-start | bytes 622592 | tf_op jit(solution)/shard_map/all_to_all | solution.py:375
  23.1 144.4 %all-gather.2.cloned.1.call-start = ((), (), s32[]{:S(2)}) async-start(), calls=%async_computation.4 | async-start | bytes 7077888 | tf_op jit(solution)/shard_map/all_gather | solution.py:423
  33.6 39.0 %copy-start.4 = (bf16[64,2048]{1,0:T(8,128)(2,1)S(1)}, bf16[64,2048]{1,0:T(8,128)(2,1)}, u32[]{:S(2)}) copy-start(bf16[64,2048]{1,0:T(8,128)(2,1)} %param.14) | copy-start | bytes 786436
  33.8 1.7 copy-start.1
  35.4 37.6 %copy-start.7 = (f32[2048]{0:T(1024)S(1)}, f32[2048]{0:T(1024)}, u32[]{:S(2)}) copy-start(f32[2048]{0:T(1024)} %param.19) | copy-start | bytes 24580
  124.3 43.2 %copy-start.10 = (bf16[1,2048,176]{1,2,0:T(8,128)(2,1)S(1)}, bf16[1,2048,176]{1,2,0:T(8,128)(2,1)}, u32[]{:S(2)}) copy-start(bf16[1,2048,176]{1,2,0:T(8,128)(2,1)} %param.24) | copy-start | bytes 2162692
  125.6 96.1 %reduce-scatter.2.cloned.1.call-start = ((), (), s32[]{:S(2)}) async-start(), calls=%async_computation.5 | async-start | bytes 7077888 | tf_op jit(solution)/shard_map/reduce_scatter | solution.py:432
  167.5 5.4 %copy-start.11 = (bf16[1,176,2048]{2,1,0:T(8,128)(2,1)S(1)}, bf16[1,176,2048]{2,1,0:T(8,128)(2,1)}, u32[]{:S(2)}) copy-start(bf16[1,176,2048]{2,1,0:T(8,128)(2,1)} %param.25) | copy-start | bytes 2162692
  223.9 29.3 %all-to-all-start.2 = ((bf16[32,96,128]{2,1,0:T(8,128)(2,1)}), bf16[32,96,128]{2,1,0:T(8,128)(2,1)S(1)}, u32[]{:S(2)}, u32[]{:S(2)}) async-start(bf16[32,96,128]{2,1,0:T(8,128)(2,1)} %reshape.73), calls=%async_computation.3 | async-start | bytes 1572864 | tf_op jit(solution)/shard_map/all_to_all | solution.py:437
  234.3 2.7 copy-start.3
  234.3 2.7 copy-start.9
  237.0 16.6 %copy-start.5 = (bf16[512,192]{0,1:T(8,128)(2,1)S(1)}, bf16[512,192]{0,1:T(8,128)(2,1)}, u32[]{:S(2)}) copy-start(bf16[512,192]{0,1:T(8,128)(2,1)} %get-tuple-element.11) | copy-start | bytes 589828
  237.0 16.6 %copy-start.6 = (bf16[512,192]{0,1:T(8,128)(2,1)S(1)}, bf16[512,192]{0,1:T(8,128)(2,1)}, u32[]{:S(2)}) copy-start(bf16[512,192]{0,1:T(8,128)(2,1)} %get-tuple-element.12) | copy-start | bytes 589828
Sparse Core Ops, SparseCore 0:
  125.7 41.6 all-gather.1
  177.6 44.1 reduce-scatter.1

commit v16 on v15

--- a/solution.py
+++ b/solution.py
@@ -442,9 +442,9 @@
     coef = jnp.sum(jnp.where(hit, weights_n[:, :, None], 0.0), axis=1)
     coef_hi = coef.astype(bf16)
     coef_lo = (coef - coef_hi.astype(f32)).astype(bf16)
-    terms = jnp.dot(
-        jnp.concatenate([shared_hidden, coef_hi, coef_lo], axis=1),
-        jnp.concatenate([shared_down, returned, returned], axis=0),
+    terms = jnp.dot(shared_hidden, shared_down, preferred_element_type=f32) + jnp.dot(
+        jnp.concatenate([coef_hi, coef_lo], axis=1),
+        jnp.concatenate([returned, returned], axis=0),
         preferred_element_type=f32,
     )
     return expert_reduce_scatter(

time: 292 us -> 292 us (level)
  waiting for transfers between devices: 107 us -> 102 us
  matrix products: 23.4 us -> 28.2 us
    all_to_all x1, waiting for transfers between devices: 14.5 us -> 9.87 us  [shards(): lax.all_to_all(summed.reshape(block), 'dp', split_axis=0, concat_axis=0,...]
    dot_general x2, matrix products: 6.41 us -> 11 us  [the longest x1 6.17 us: shards(): jnp.dot(shared_hidden, shared_down, preferred_element_type=f32)]
  transfers between devices with their start and end apart: 4 -> 4, of which waited for: 4 -> 4; matrix products, arithmetic and copies ran while one was open for 3% -> 5% of each run, Pallas kernels for 0% -> 0%
where the time goes in v16:
time: 292 us
  waiting for transfers between devices  102 us (35%)
  Pallas kernels  82.3 us (28%)
  matrix products  28.2 us (10%)
  blocking collectives  24.1 us (8%)
  starting transfers between devices  21.7 us (7%)
  local copies, waits for them, and re-layouts  14.6 us (5%)
  between operations  13.7 us (5%)
  other arithmetic  4.65 us (2%)
    all_gather x1, waiting for transfers between devices, shards(): lax.all_gather(arrived.reshape(n_rows, width_model), 'expert', axis=0, ti...  41.6 us
    reduce_scatter x1, waiting for transfers between devices, shards(): lax.psum_scatter(partial_out, 'expert', scatter_dimension=0, tiled=True)  41.1 us
    pallas_call x1, Pallas kernels, fused_projector(): pl.pallas_call(kernel, out_shape=jax.ShapeDtypeStruct((rows, width_model)...  37.2 us
    pallas_call x1, Pallas kernels, expert_reduce_scatter(): pl.pallas_call(kernel, out_shape=jax.ShapeDtypeStruct((rows, cols), out_d...  24.6 us
    all_to_all x1, blocking collectives, shards(): lax.all_to_all(send, 'dp', split_axis=0, concat_axis=0, tiled=True)  24.1 us
    pallas_call x1, Pallas kernels, expert_all_gather(): pl.pallas_call(kernel, out_shape=jax.ShapeDtypeStruct((n, rows, cols), x....  20.5 us
    all_to_all x1, starting transfers between devices, shards(): lax.all_to_all(packed, 'dp', split_axis=0, concat_axis=0, tiled=True)  11.9 us
    all_to_all x1, waiting for transfers between devices, shards(): lax.all_to_all(summed.reshape(block), 'dp', split_axis=0, concat_axis=0,...  9.87 us
  transfers between devices with their start and end apart: 4, of which 4 were waited for; matrix products, arithmetic and copies ran while one was open for 5% of the time, Pallas kernels for 0%

profile of v16, /device:TPU:1, one launch (start us, length us, event | category | flops | bytes accessed | tf_op | source)
XLA Modules:
  0.0 291.5 jit_solution(6284230706142762781)
XLA Ops:
  7.6 1.2 fusion
  10.2 1.1 reshape.77
  11.2 11.9 %all-to-all-start = ((bf16[32,2,2368]{2,1,0:T(2,128)(2,1)}), bf16[32,2,2368]{2,1,0:T(2,128)(2,1)S(1)}, u32[]{:S(2)}, u32[]{:S(2)}) async-start(bf16[32,2,2368]{2,1,0:T(2,128)(2,1)} %reshape.77), calls=%async_computation | async-start | bytes 622592 | tf_op jit(solution)/shard_map/all_to_all | solution.py:375
  23.3 9.7 %all-to-all-done = bf16[32,2,2368]{2,1,0:T(2,128)(2,1)S(1)} async-done(((bf16[32,2,2368]{2,1,0:T(2,128)(2,1)}), bf16[32,2,2368]{2,1,0:T(2,128)(2,1)S(1)}, u32[]{:S(2)}, u32[]{:S(2)}) %all-to-all-start) | async-done | bytes 303136 | tf_op jit(solution)/shard_map/all_to_all | solution.py:375
  33.8 1.7 copy-done.1
  35.4 37.2 %shard_map.136 = bf16[32,2048]{1,0:T(8,128)(2,1)S(1)} custom-call(bf16[32,4608]{1,0:T(8,128)(2,1)S(1)} %slice.37.f_ref, bf16[4608,256]{1,0:T(8,128)(2,1)S(1)} %copy-done.1, bf16[256,2048]{1,0:T(8,128)(2,1)S(1)} %copy-done.2), custom_call_target="tpu_custom_call" | custom-call | tf_op jit(solution)/shard_map/pallas_call | solution.py:303
  74.6 20.5 %shard_map.137 = bf16[8,64,2176]{2,1,0:T(8,128)(2,1)} custom-call(bf16[64,2176]{1,0:T(8,128)(2,1)} %fusion.30.x_ref), custom_call_target="tpu_custom_call" | custom-call | tf_op jit(solution)/shard_map/pallas_call | solution.py:189
  95.1 0.9 slice.38
  97.6 2.2 convolution_convert_fusion.2
  100.2 24.1 %all_to_all.15 = bf16[32,96,128]{2,1,0:T(8,128)(2,1)S(1)} all-to-all(bf16[32,96,128]{2,1,0:T(8,128)(2,1)S(1)} %reshape.71), channel_id=1, replica_groups=mesh['dp'=32,'expert'=8] {'dp'}, dimensions={0} | all-to-all | bytes 1572864 | tf_op jit(solution)/shard_map/all_to_all | solution.py:422
  124.3 1.3 reshape.72
  125.8 41.6 %all-gather.2.cloned.1.call-done = bf16[1536,2048]{1,0:T(8,128)(2,1)} async-done(((bf16[192,2048]{1,0:T(8,128)(2,1)}), bf16[1536,2048]{1,0:T(8,128)(2,1)}) %all-gather.2.cloned.1.call-update) | async-done | bytes 6291472 | tf_op jit(solution)/shard_map/all_gather | solution.py:423
  167.5 5.4 %fusion.5 = f32[1536,352]{0,1:T(8,128)S(1)} fusion(bf16[1536,2048]{1,0:T(8,128)(2,1)} %all-gather.2.cloned.1.call-done, bf16[2048,176]{0,1:T(8,128)(2,1)S(1)} %bitcast.26, bf16[2048,176]{0,1:T(8,128)(2,1)} %bitcast.27), kind=kOutput, calls=%fused_computation.11 | convolution fusion | flops 2217476096 | bytes 9895936 | tf_op jit(solution)/shard_map/dot_general | solution.py:426
  172.9 4.5 %convolution_convert_fusion = bf16[1536,2048]{1,0:T(8,128)(2,1)} fusion(bf16[1,176,2048]{2,1,0:T(8,128)(2,1)S(1)} %copy-done.9, f32[1536,352]{0,1:T(8,128)S(1)} %fusion.5), kind=kOutput, calls=%fused_computation | convolution fusion | flops 1112064000 | bytes 9175040 | tf_op jit(solution)/shard_map/dot_general | solution.py:431
  177.5 3.2 %slice.40 = bf16[512,2048]{1,0:T(8,128)(2,1)} slice(bf16[512,2176]{1,0:T(8,128)(2,1)} %bitcast.23), slice={[0:512], [0:2048]} | slice | bytes 4194304 | tf_op jit(solution)/shard_map/slice | solution.py:393
  180.7 41.1 %reduce-scatter.2.cloned.1.call-done = bf16[192,2048]{1,0:T(8,128)(2,1)} async-done(((bf16[1536,2048]{1,0:T(8,128)(2,1)}), bf16[192,2048]{1,0:T(8,128)(2,1)}) %reduce-scatter.2.cloned.1.call-update) | async-done | bytes 786448 | tf_op jit(solution)/shard_map/reduce_scatter | solution.py:432
  221.7 2.2 reshape.73
  223.9 9.5 %all-to-all-start.2 = ((bf16[32,96,128]{2,1,0:T(8,128)(2,1)}), bf16[32,96,128]{2,1,0:T(8,128)(2,1)S(1)}, u32[]{:S(2)}, u32[]{:S(2)}) async-start(bf16[32,96,128]{2,1,0:T(8,128)(2,1)} %reshape.73), calls=%async_computation.3 | async-start | bytes 1572864 | tf_op jit(solution)/shard_map/all_to_all | solution.py:437
  234.2 2.9 %fusion.49 = f32[512,352]{0,1:T(8,128)S(1)} fusion(bf16[512,2048]{1,0:T(8,128)(2,1)} %slice.40, bf16[2048,352]{0,1:T(8,128)(2,1)} %param.20), kind=kOutput, calls=%fused_computation.96 | convolution fusion | flops 738197504 | bytes 4259840 | tf_op jit(solution)/shard_map/dot_general | solution.py:434
  237.2 6.2 %fusion.10 = f32[512,2048]{1,0:T(8,128)} fusion(bf16[352,2048]{1,0:T(8,128)(2,1)S(1)} %copy-done, bf16[512,2048]{1,0:T(8,128)(2,1)} %slice.40, bf16[2048,352]{0,1:T(8,128)(2,1)} %param.21, f32[512,352]{0,1:T(8,128)S(1)} %fusion.49), kind=kOutput, calls=%fused_computation.17 | convolution fusion | flops 1477476352 | bytes 9895936 | tf_op jit(solution)/shard_map/dot_general | solution.py:445
  243.4 9.9 %all-to-all-done.2 = bf16[32,96,128]{2,1,0:T(8,128)(2,1)S(1)} async-done(((bf16[32,96,128]{2,1,0:T(8,128)(2,1)}), bf16[32,96,128]{2,1,0:T(8,128)(2,1)S(1)}, u32[]{:S(2)}, u32[]{:S(2)}) %all-to-all-start.2) | async-done | bytes 786464 | tf_op jit(solution)/shard_map/all_to_all | solution.py:437
  253.6 4.8 %add_convert_fusion = bf16[512,2048]{1,0:T(8,128)(2,1)} fusion(f32[512,2048]{1,0:T(8,128)} %fusion.10, bf16[192,2048]{1,0:T(8,128)(2,1)S(1)} %reshape.74, bf16[512,192]{0,1:T(8,128)(2,1)S(1)} %copy-done.3, bf16[512,192]{0,1:T(8,128)(2,1)S(1)} %copy-done.4), kind=kOutput, calls=%fused_computation.3 | convolution fusion | flops 811335680 | bytes 7471104 | tf_op jit(solution)/shard_map/dot_general | solution.py:445
  258.4 24.6 %shard_map.138 = bf16[64,2048]{1,0:T(8,128)(2,1)} custom-call(bf16[4,2,64,2048]{3,2,1,0:T(8,128)(2,1)} %bitcast.20, bf16[64,2048]{1,0:T(8,128)(2,1)} %get-tuple-element.13.b_ref), custom_call_target="tpu_custom_call" | custom-call | tf_op jit(solution)/shard_map/pallas_call | solution.py:108
  283.0 1.7 copy.53
  (60 shorter events, 8.6 us)
Async XLA Ops:
  6.5 230.7 %copy-start = (bf16[352,2048]{1,0:T(8,128)(2,1)S(1)}, bf16[352,2048]{1,0:T(8,128)(2,1)}, u32[]{:S(2)}) copy-start(bf16[352,2048]{1,0:T(8,128)(2,1)} %param.22) | copy-start | bytes 4325380
  6.5 16.6 %copy-start.10 = (s32[64,2]{0,1:T(2,128)S(1)}, s32[64,2]{0,1:T(2,128)}, u32[]{:S(2)}) copy-start(s32[64,2]{0,1:T(2,128)} %param.26) | copy-start | bytes 1540
  6.5 16.6 %copy-start.7 = (s32[64,2]{0,1:T(2,128)S(1)}, s32[64,2]{0,1:T(2,128)}, u32[]{:S(2)}) copy-start(s32[64,2]{0,1:T(2,128)} %param.27) | copy-start | bytes 1540
  9.3 24.5 %copy-start.2 = (bf16[256,2048]{1,0:T(8,128)(2,1)S(1)}, bf16[256,2048]{1,0:T(8,128)(2,1)}, u32[]{:S(2)}) copy-start(bf16[256,2048]{1,0:T(8,128)(2,1)} %wo_ref.1) | copy-start | bytes 3145732
  11.2 21.8 %all-to-all-start = ((bf16[32,2,2368]{2,1,0:T(2,128)(2,1)}), bf16[32,2,2368]{2,1,0:T(2,128)(2,1)S(1)}, u32[]{:S(2)}, u32[]{:S(2)}) async-start(bf16[32,2,2368]{2,1,0:T(2,128)(2,1)} %reshape.77), calls=%async_computation | async-start | bytes 622592 | tf_op jit(solution)/shard_map/all_to_all | solution.py:375
  23.1 144.4 %all-gather.2.cloned.1.call-start = ((), (), s32[]{:S(2)}) async-start(), calls=%async_computation.4 | async-start | bytes 7077888 | tf_op jit(solution)/shard_map/all_gather | solution.py:423
  33.6 39.0 %copy-start.5 = (bf16[64,2048]{1,0:T(8,128)(2,1)S(1)}, bf16[64,2048]{1,0:T(8,128)(2,1)}, u32[]{:S(2)}) copy-start(bf16[64,2048]{1,0:T(8,128)(2,1)} %param.14) | copy-start | bytes 786436
  33.8 1.7 copy-start.1
  35.4 37.7 %copy-start.6 = (f32[2048]{0:T(1024)S(1)}, f32[2048]{0:T(1024)}, u32[]{:S(2)}) copy-start(f32[2048]{0:T(1024)} %param.19) | copy-start | bytes 24580
  124.3 43.2 %copy-start.8 = (bf16[1,2048,176]{1,2,0:T(8,128)(2,1)S(1)}, bf16[1,2048,176]{1,2,0:T(8,128)(2,1)}, u32[]{:S(2)}) copy-start(bf16[1,2048,176]{1,2,0:T(8,128)(2,1)} %param.24) | copy-start | bytes 2162692
  125.6 96.1 %reduce-scatter.2.cloned.1.call-start = ((), (), s32[]{:S(2)}) async-start(), calls=%async_computation.5 | async-start | bytes 7077888 | tf_op jit(solution)/shard_map/reduce_scatter | solution.py:432
  167.5 5.4 %copy-start.9 = (bf16[1,176,2048]{2,1,0:T(8,128)(2,1)S(1)}, bf16[1,176,2048]{2,1,0:T(8,128)(2,1)}, u32[]{:S(2)}) copy-start(bf16[1,176,2048]{2,1,0:T(8,128)(2,1)} %param.25) | copy-start | bytes 2162692
  223.9 29.3 %all-to-all-start.2 = ((bf16[32,96,128]{2,1,0:T(8,128)(2,1)}), bf16[32,96,128]{2,1,0:T(8,128)(2,1)S(1)}, u32[]{:S(2)}, u32[]{:S(2)}) async-start(bf16[32,96,128]{2,1,0:T(8,128)(2,1)} %reshape.73), calls=%async_computation.3 | async-start | bytes 1572864 | tf_op jit(solution)/shard_map/all_to_all | solution.py:437
  237.2 16.4 %copy-start.3 = (bf16[512,192]{0,1:T(8,128)(2,1)S(1)}, bf16[512,192]{0,1:T(8,128)(2,1)}, u32[]{:S(2)}) copy-start(bf16[512,192]{0,1:T(8,128)(2,1)} %get-tuple-element.11) | copy-start | bytes 589828
  237.2 16.4 %copy-start.4 = (bf16[512,192]{0,1:T(8,128)(2,1)S(1)}, bf16[512,192]{0,1:T(8,128)(2,1)}, u32[]{:S(2)}) copy-start(bf16[512,192]{0,1:T(8,128)(2,1)} %get-tuple-element.12) | copy-start | bytes 589828
Sparse Core Ops, SparseCore 0:
  125.7 41.6 all-gather.1
  177.6 44.1 reduce-scatter.1
